TPU v7x, 512 devices: a whole 4x8x8 slice. The times are simulated.
512 devices in a mesh: grp: 16 (over y, core), dev: 32 (over x, z).
Axes of the slice: x: 4, y: 8, z: 8, core: 2. Of those that a mesh axis runs over, the one named last changes fastest.
Arguments:
- wave: bfloat16 [16384, 384], P(('grp', 'dev')), may hold values from -6 to 6
- lengths: int32 [16384], P('grp'), may hold values from 288 to 384, as said below
- order: int32 [512, 32], P('grp'), may hold values from 0 to 31, each once within a row
- w_first: bfloat16 [10, 512], replicated, may hold values from -2 to 2
- norm_gain: float32 [512], replicated, may hold values from 0.1 to 1.9
- norm_bias: float32 [512], replicated, may hold values from -3 to 3
- w_second: bfloat16 [3, 512, 512], replicated, may hold values from -0.15625 to 0.15625
- cot: bfloat16 [16384, 37, 512], P(('grp', 'dev')), may hold values from -0.0234375 to 0.0234375
Outputs:
- features: bfloat16 [16384, 37, 512], P(('grp', 'dev'))
- grad_second: float32 [3, 512, 512], P(None, None, 'dev')
- grad_first: float32 [10, 512], P(None, 'dev')
- grad_gain: float32 [512], P('dev')
- grad_bias: float32 [512], P('dev')
Inputs may be any that keep to these rules, and one draw needn't show every extreme that they name: `lengths`: every aligned block of 32 rows (the rows of one device) holds a row of exactly 384 valid samples. Each row of order is a permutation of 0 .. 31.
All inputs are finite; a program needn't handle non-finite values.
Results may differ from a plain program's by a relative error of at most 0.0054.
Values may be sent and summed in bfloat16 or wider, within the bound.
A program may use at most 64 MiB of HBM per device.

v0:
```python
import jax
import jax.numpy as jnp
from jax import lax
from jax.sharding import PartitionSpec as P


def gelu_slope(value):
    return (
        0.5 * (1.0 + lax.erf(value * 0.7071067811865476))
        + value * jnp.exp(-0.5 * value * value) * 0.3989422804014327
    )


def local_pass(wave, lens, w_first, norm_gain, norm_bias, w_second, cot):
    rows, samp = wave.shape
    ker_first = w_first.shape[0]
    stride_first = ker_first // 2
    chans = w_first.shape[1]
    taps_second = w_second.shape[0]
    frames0 = (samp - ker_first) // stride_first + 1
    frames1 = (frames0 - taps_second) // 2 + 1
    blocks = wave[:, : stride_first * (frames0 + 1)].reshape(rows, frames0 + 1, stride_first)
    patches = jnp.concatenate([blocks[:, :-1], blocks[:, 1:]], axis=2).reshape(
        rows * frames0, ker_first
    )
    pre0 = jnp.dot(patches, w_first, preferred_element_type=jnp.float32).reshape(
        rows, frames0, chans
    )
    valid0 = (lens - ker_first) // stride_first + 1
    mask0 = (jnp.arange(frames0, dtype=jnp.int32)[None, :] < valid0[:, None]).astype(jnp.float32)[
        :, :, None
    ]
    count0 = valid0.astype(jnp.float32)[:, None, None]
    mean0 = jnp.sum(pre0 * mask0, axis=1, keepdims=True) / count0
    centred = (pre0 - mean0) * mask0
    var0 = jnp.sum(centred * centred, axis=1, keepdims=True) / count0
    inv_std = lax.rsqrt(var0 + 1e-05)
    normed = centred * inv_std
    lifted = normed * norm_gain + norm_bias
    act0 = (jax.nn.gelu(lifted, approximate=False) * mask0).astype(jnp.bfloat16)
    span = 2 * frames1
    taps = jnp.concatenate(
        [act0[:, 0:span:2], act0[:, 1:span:2], act0[:, 2 : span + 1 : 2]], axis=2
    )
    taps = taps.reshape(rows * frames1, taps_second * chans)
    kernel = w_second.reshape(taps_second * chans, chans)
    pre1 = jnp.dot(taps, kernel, preferred_element_type=jnp.float32).reshape(rows, frames1, chans)
    valid1 = (valid0 - taps_second) // 2 + 1
    mask1 = (jnp.arange(frames1, dtype=jnp.int32)[None, :] < valid1[:, None]).astype(jnp.float32)[
        :, :, None
    ]
    features = (jax.nn.gelu(pre1, approximate=False) * mask1).astype(jnp.bfloat16)
    grad1 = (
        (cot.astype(jnp.float32) * gelu_slope(pre1) * mask1)
        .astype(jnp.bfloat16)
        .reshape(rows * frames1, chans)
    )
    grad_kernel = lax.dot_general(
        taps, grad1, (((0,), (0,)), ((), ())), preferred_element_type=jnp.float32
    )
    back = lax.dot_general(
        grad1, kernel, (((1,), (1,)), ((), ())), preferred_element_type=jnp.float32
    )
    back = back.reshape(rows, frames1, taps_second, chans)
    zero_row = jnp.zeros((rows, 1, chans), jnp.float32)
    even = back[:, :, 0] + jnp.concatenate([zero_row, back[:, :-1, 2]], axis=1)
    odd = back[:, :, 1]
    pieces = [jnp.stack([even, odd], axis=2).reshape(rows, span, chans), back[:, -1:, 2]]
    dact0 = jnp.concatenate(pieces, axis=1)
    dlift = dact0 * gelu_slope(lifted) * mask0
    grad_gain = jnp.sum(dlift * normed, axis=(0, 1))
    grad_bias = jnp.sum(dlift, axis=(0, 1))
    dnorm = dlift * norm_gain
    first_mean = jnp.sum(dnorm, axis=1, keepdims=True) / count0
    second_mean = jnp.sum(dnorm * normed, axis=1, keepdims=True) / count0
    dpre0 = inv_std * (dnorm - first_mean - normed * second_mean) * mask0
    grad_filter = lax.dot_general(
        patches.astype(jnp.float32),
        dpre0.reshape(rows * frames0, chans),
        (((0,), (0,)), ((), ())),
        precision=lax.Precision.HIGHEST,
        preferred_element_type=jnp.float32,
    )
    grads = jnp.concatenate(
        [grad_kernel, grad_filter, grad_gain[None, :], grad_bias[None, :]], axis=0
    )
    return (features, grads)


def shards(wave, lengths, order, w_first, norm_gain, norm_bias, w_second, cot):
    members = lax.axis_size("dev")
    member = lax.axis_index("dev")
    rows = wave.shape[0]
    share = rows // members
    own_order = lax.dynamic_index_in_dim(order, member, 0, keepdims=False)
    dealt = own_order.reshape(share, members).T.reshape(rows)
    outgoing = jnp.take(wave, dealt, axis=0)
    arrived = lax.all_to_all(outgoing, "dev", split_axis=0, concat_axis=0, tiled=True)
    group_lens = jnp.take_along_axis(lengths.reshape(members, rows), order, axis=1)
    group_lens = group_lens.reshape(members, share, members)
    lens = lax.dynamic_index_in_dim(group_lens, member, 2, keepdims=False).reshape(rows)
    features, grads = local_pass(arrived, lens, w_first, norm_gain, norm_bias, w_second, cot)
    chans = grads.shape[1]
    width = chans // members
    totals = lax.psum(grads, ("grp", "dev"))
    owned = lax.dynamic_slice_in_dim(totals, member * width, width, 1)
    taps_second = w_second.shape[0]
    ker_first = w_first.shape[0]
    in_chans = w_second.shape[1]
    grad_second = owned[: taps_second * in_chans].reshape(taps_second, in_chans, width)
    grad_first = owned[taps_second * in_chans : taps_second * in_chans + ker_first]
    grad_gain = owned[taps_second * in_chans + ker_first]
    grad_bias = owned[taps_second * in_chans + ker_first + 1]
    return (features, grad_second, grad_first, grad_gain, grad_bias)


def solution(mesh):
    placed = (
        P(("grp", "dev"), None),
        P("grp"),
        P("grp", None),
        P(),
        P(),
        P(),
        P(),
        P(("grp", "dev"), None, None),
    )
    return jax.shard_map(
        shards,
        mesh=mesh,
        in_specs=placed,
        out_specs=(
            P(("grp", "dev"), None, None),
            P(None, None, "dev"),
            P(None, "dev"),
            P("dev"),
            P("dev"),
        ),
        check_vma=False,
    )
```

profile of v0, /device:TPU:1, one launch (start us, length us, event | category | flops | bytes accessed | tf_op | source)
XLA Modules:
  0.0 425.1 jit_solution(17557020040088557377)
XLA Ops:
  7.2 0.0 copy-start
  7.2 0.9 copy.57
  8.1 0.8 reshape.259
  8.9 0.1 copy.60
  9.0 0.1 reshape.272
  9.0 7.1 %gather_fusion.1 = s32[1024]{0:T(1024)S(1)} fusion(s32[32,32]{1,0:T(8,128)S(1)} %reshape.259, s32[1024]{0:T(1024)S(1)} %reshape.272), kind=kCustom, calls=%fused_computation.1 | custom fusion | bytes 16384 | tf_op jit(solution)/shard_map/jit(take_along_axis)/gather | solution.py:99
  16.1 0.1 reshape.275
  16.2 0.7 compare_and_fusion.1
  16.9 0.1 constant_dynamic-slice_fusion.2
  16.9 0.1 copy.75
  17.1 0.7 fusion.63
  17.8 0.6 gather_fusion
  18.4 0.1 bitcast_select_fusion
  18.5 0.5 broadcast.271
  19.0 0.7 reduce
  19.7 0.7 reshape.289
  20.4 13.7 %all-to-all-start = ((bf16[32,2,192]{2,1,0:T(2,128)(2,1)}), bf16[32,2,192]{2,1,0:T(2,128)(2,1)S(1)}, u32[]{:S(2)}, u32[]{:S(2)}) async-start(bf16[32,2,192]{2,1,0:T(2,128)(2,1)} %reshape.289), calls=%async_computation | async-start | bytes 65536 | tf_op jit(solution)/shard_map/all_to_all | solution.py:98
  34.1 0.0 all-reduce.3.cloned.1.call-start
  34.2 0.1 fusion.61
  34.2 0.1 fusion.60
  34.3 8.6 %all-to-all-done = bf16[32,2,192]{2,1,0:T(2,128)(2,1)S(1)} async-done(((bf16[32,2,192]{2,1,0:T(2,128)(2,1)}), bf16[32,2,192]{2,1,0:T(2,128)(2,1)S(1)}, u32[]{:S(2)}, u32[]{:S(2)}) %all-to-all-start) | async-done | bytes 24608 | tf_op jit(solution)/shard_map/all_to_all | solution.py:98
  42.9 0.1 reshape.290
  43.0 0.1 copy.54
  43.1 0.1 reshape.258
  43.2 0.2 copy.72
  43.4 0.2 copy.71
  43.6 0.0 copy-done.6
  43.6 0.0 copy-start.7
  43.6 0.0 copy-start.8
  43.6 0.9 multiply_reduce_fusion.3
  44.6 0.0 copy-start.1
  44.6 0.1 broadcast_divide_fusion.2
  44.6 1.1 multiply_reduce_fusion.2
  45.8 0.1 add_rsqrt_fusion
  45.9 1.0 copy-done.1
  46.9 0.0 copy-done.7
  46.9 14.2 %fusion.3 = bf16[32,75,512]{2,1,0:T(8,128)(2,1)} fusion(f32[512]{0:T(512)S(1)} %copy-done.7, f32[512]{0:T(512)S(1)} %copy-done.8, f32[32,75]{1,0:T(8,128)S(1)} %fusion.60, f32[32,512]{1,0:T(8,128)S(1)} %add_rsqrt_fusion, f32[32,75,512]{2,1,0:T(8,128)S(1)} %get-tuple-element.42, f32[32,512]{1,0:T(8,128)S(1)} %broadcast_divide_fusion.2), kind=kLoop, calls=%fused_computation.7 | loop fusion | flops 87244800 | bytes 7517568 | tf_op jit(solution)/shard_map/convert_element_type | solution.py:40
  61.0 9.9 %slice.47 = bf16[32,37,512]{2,1,0:T(8,128)(2,1)} slice(bf16[32,75,512]{2,1,0:T(8,128)(2,1)} %fusion.3), slice={[0:32:1], [2:75:2], [0:512:1]} | slice | bytes 2424832 | tf_op jit(solution)/shard_map/slice | solution.py:43
  70.9 9.8 %slice.46 = bf16[32,37,512]{2,1,0:T(8,128)(2,1)} slice(bf16[32,75,512]{2,1,0:T(8,128)(2,1)} %fusion.3), slice={[0:32:1], [1:74:2], [0:512:1]} | slice | bytes 2424832 | tf_op jit(solution)/shard_map/slice | solution.py:43
  80.7 9.7 %slice.45 = bf16[32,37,512]{2,1,0:T(8,128)(2,1)} slice(bf16[32,75,512]{2,1,0:T(8,128)(2,1)} %fusion.3), slice={[0:32:1], [0:74:2], [0:512:1]} | slice | bytes 2424832 | tf_op jit(solution)/shard_map/slice | solution.py:43
  90.4 0.0 copy-done
  90.4 11.5 %fusion.35 = (bf16[32,37,512]{2,1,0:T(8,128)(2,1)S(1)}, bf16[32,37,512]{2,1,0:T(8,128)(2,1)S(1)}) fusion(bf16[32,37,512]{2,0,1:T(8,128)(2,1)} %param.15, f32[32,37]{1,0:T(8,128)S(1)} %fusion.61, bf16[1536,512,1]{1,0,2:T(8,128)(2,1)S(1)} %bitcast.78, bf16[32,37,512]{2,1,0:T(8,128)(2,1)} %slice.47, bf16[32,37,512]{2,1,0:T(8,128)(2,1)} %slice.46, ...), kind=kOutput, calls=%fused_computation.59 | convolution fusion | flops 1920466944 | bytes 8852096 | tf_op jit(solution)/shard_map/dot_general | solution.py:47
  102.0 3.9 convolution_bitcast_fusion
  105.9 2.2 fusion.51
  108.1 0.1 slice_bitcast_fusion.2
  108.2 0.2 slice.65
  108.4 0.2 slice_bitcast_fusion
  108.7 0.6 fusion.37
  109.3 0.6 pad_maximum_fusion
  110.0 2.8 copy.65
  112.8 0.0 slice-start
  112.8 0.0 slice-start.1
  112.8 2.8 copy.66
  115.7 5.9 %multiply_reduce_fusion = (f32[512]{0:T(512)S(1)}, f32[32,512]{1,0:T(8,128)S(1)}, f32[32,512]{1,0:T(8,128)S(1)}, f32[512]{0:T(512)S(1)}, f32[32,75,512]{2,1,0:T(8,128)S(1)}) fusion(f32[32,512]{1,0:T(8,128)S(1)} %add_rsqrt_fusion, f32[32,75]{1,0:T(8,128)S(1)} %fusion.60, f32[32,75,512]{2,1,0:T(8,128)S(1)} %bitcast.80, ...), kind=kLoop, calls=%fused_computation.15 | loop fusion | flops 28228608 | bytes 15025536 | tf_op jit(solution)/shard_map/reduce_sum | solution.py:71
  121.6 0.1 broadcast_divide_fusion.1
  121.6 3.5 fusion.55
  125.1 9.9 %concatenate.19 = f32[1548,512]{1,0:T(8,128)} concatenate(f32[1536,512]{1,0:T(8,128)} %convolution_bitcast_fusion, f32[10,512]{1,0:T(8,128)S(1)} %fusion.55, f32[1,512]{1,0:T(1,128)S(1)} %bitcast.84, f32[1,512]{1,0:T(1,128)S(1)} %bitcast.85), dimensions={0} | concatenate | bytes 6340608 | tf_op jit(solution)/shard_map/concatenate | solution.py:84
  135.0 0.0 all-reduce.3.cloned.1.call-update
  135.0 1.4 copy.67
  136.4 276.8 %all-reduce.3.cloned.1.call-done = f32[1548,512]{1,0:T(8,128)} async-done(((f32[1548,512]{1,0:T(8,128)}), f32[1548,512]{1,0:T(8,128)}) %all-reduce.3.cloned.1.call-update) | async-done | bytes 3170320 | tf_op jit(solution)/shard_map/psum | solution.py:105
  413.2 1.4 constant_dynamic-slice_fusion
  414.6 0.9 copy.68
  415.5 1.4 dynamic-slice.7
  416.9 1.3 dynamic-slice_bitcast_fusion
  (20 shorter events, 0.1 us)
Async XLA Ops:
  7.2 83.2 %copy-start = (bf16[3,512,512]{2,1,0:T(8,128)(2,1)S(1)}, bf16[3,512,512]{2,1,0:T(8,128)(2,1)}, u32[]{:S(2)}) copy-start(bf16[3,512,512]{2,1,0:T(8,128)(2,1)} %param.14) | copy-start | bytes 4718596
  9.0 8.8 %copy-start.2 = (bf16[32,384]{1,0:T(8,128)(2,1)S(1)}, bf16[32,384]{1,0:T(8,128)(2,1)}, u32[]{:S(2)}) copy-start(bf16[32,384]{1,0:T(8,128)(2,1)} %param.8) | copy-start | bytes 73732
  9.0 34.6 %copy-start.6 = (bf16[10,512]{1,0:T(8,128)(2,1)S(1)}, bf16[10,512]{1,0:T(8,128)(2,1)}, u32[]{:S(2)}) copy-start(bf16[10,512]{1,0:T(8,128)(2,1)} %param.11) | copy-start | bytes 30724
  20.4 22.5 %all-to-all-start = ((bf16[32,2,192]{2,1,0:T(2,128)(2,1)}), bf16[32,2,192]{2,1,0:T(2,128)(2,1)S(1)}, u32[]{:S(2)}, u32[]{:S(2)}) async-start(bf16[32,2,192]{2,1,0:T(2,128)(2,1)} %reshape.289), calls=%async_computation | async-start | bytes 65536 | tf_op jit(solution)/shard_map/all_to_all | solution.py:98
  34.1 379.1 %all-reduce.3.cloned.1.call-start = ((), (), s32[]{:S(2)}) async-start(), calls=%async_computation.1 | async-start | bytes 6356992 | tf_op jit(solution)/shard_map/psum | solution.py:105
  43.6 3.3 copy-start.7
  43.6 3.2 copy-start.8
  44.6 2.3 copy-start.1
  90.4 11.5 %copy-start.3 = (bf16[32,37,512]{2,1,0:T(8,128)(2,1)S(1)}, bf16[32,37,512]{2,1,0:T(8,128)(2,1)}, u32[]{:S(2)}) copy-start(bf16[32,37,512]{2,1,0:T(8,128)(2,1)} %slice.47) | copy-start | bytes 3637252
  90.4 11.5 %copy-start.4 = (bf16[32,37,512]{2,1,0:T(8,128)(2,1)S(1)}, bf16[32,37,512]{2,1,0:T(8,128)(2,1)}, u32[]{:S(2)}) copy-start(bf16[32,37,512]{2,1,0:T(8,128)(2,1)} %slice.46) | copy-start | bytes 3637252
  90.4 11.5 %copy-start.5 = (bf16[32,37,512]{2,1,0:T(8,128)(2,1)S(1)}, bf16[32,37,512]{2,1,0:T(8,128)(2,1)}, u32[]{:S(2)}) copy-start(bf16[32,37,512]{2,1,0:T(8,128)(2,1)} %slice.45) | copy-start | bytes 3637252
  112.8 2.9 slice-start
  112.8 2.9 slice-start.1
Sparse Core Ops, SparseCore 0:
  135.1 278.0 all-reduce.2
where the time goes:
time: 428 us; the launch traced here: 425 us
  waiting for transfers between devices  285 us (67%)
  local copies, waits for them, and re-layouts  64.4 us (15%)
  other arithmetic  25.1 us (6%)
  matrix products  22.1 us (5%)
  between operations  14.4 us (3%)
  starting transfers between devices  13.8 us (3%)
    psum x1, waiting for transfers between devices, shards(): totals = lax.psum(grads, ('grp', 'dev'))  277 us
    convert_element_type x1, other arithmetic, local_pass(): act0 = (jax.nn.gelu(lifted, approximate=False) * mask0).astype(jnp.bfloat16)  14.2 us
    all_to_all x1, starting transfers between devices, shards(): lax.all_to_all(outgoing, 'dev', split_axis=0, concat_axis=0, tiled=True)  13.7 us
    dot_general x1, matrix products, local_pass(): jnp.dot(taps, kernel, preferred_element_type=jnp.float32)  11.5 us
    concatenate x1, local copies, waits for them, and re-layouts, local_pass(): jnp.concatenate([grad_kernel, grad_filter, grad_gain[None, :], grad_bias[...  9.86 us
    slice x1, local copies, waits for them, and re-layouts, local_pass(): act0[:, 2:span + 1:2]  9.85 us
    slice x1, local copies, waits for them, and re-layouts, local_pass(): act0[:, 1:span:2]  9.77 us
    slice x1, local copies, waits for them, and re-layouts, local_pass(): act0[:, 0:span:2]  9.74 us
  transfers between devices with their start and end apart: 2, of which 2 were waited for; matrix products, arithmetic and copies ran while one was open for 0% of the time, Pallas kernels for 0%

commit v1 on v0

--- a/solution.py
+++ b/solution.py
@@ -56,7 +56,7 @@
         .reshape(rows * frames1, chans)
     )
     grad_kernel = lax.dot_general(
-        taps, grad1, (((0,), (0,)), ((), ())), preferred_element_type=jnp.float32
+        grad1, taps, (((0,), (0,)), ((), ())), preferred_element_type=jnp.float32
     )
     back = lax.dot_general(
         grad1, kernel, (((1,), (1,)), ((), ())), preferred_element_type=jnp.float32
@@ -75,15 +75,14 @@
     second_mean = jnp.sum(dnorm * normed, axis=1, keepdims=True) / count0
     dpre0 = inv_std * (dnorm - first_mean - normed * second_mean) * mask0
     grad_filter = lax.dot_general(
+        dpre0.reshape(rows * frames0, chans),
         patches.astype(jnp.float32),
-        dpre0.reshape(rows * frames0, chans),
         (((0,), (0,)), ((), ())),
         precision=lax.Precision.HIGHEST,
         preferred_element_type=jnp.float32,
     )
-    grads = jnp.concatenate(
-        [grad_kernel, grad_filter, grad_gain[None, :], grad_bias[None, :]], axis=0
-    )
+    small = jnp.concatenate([grad_filter, grad_gain[:, None], grad_bias[:, None]], axis=1)
+    grads = (grad_kernel, small)
     return (features, grads)
 
 
@@ -99,18 +98,21 @@
     group_lens = jnp.take_along_axis(lengths.reshape(members, rows), order, axis=1)
     group_lens = group_lens.reshape(members, share, members)
     lens = lax.dynamic_index_in_dim(group_lens, member, 2, keepdims=False).reshape(rows)
-    features, grads = local_pass(arrived, lens, w_first, norm_gain, norm_bias, w_second, cot)
-    chans = grads.shape[1]
-    width = chans // members
-    totals = lax.psum(grads, ("grp", "dev"))
-    owned = lax.dynamic_slice_in_dim(totals, member * width, width, 1)
+    features, (grad_kernel, small) = local_pass(
+        arrived, lens, w_first, norm_gain, norm_bias, w_second, cot
+    )
     taps_second = w_second.shape[0]
+    in_chans = w_second.shape[1]
+    part_kernel = lax.psum_scatter(grad_kernel, "dev", scatter_dimension=0, tiled=True)
+    part_small = lax.psum_scatter(small, "dev", scatter_dimension=0, tiled=True)
+    owned_kernel = lax.psum(part_kernel, "grp")
+    owned_small = lax.psum(part_small, "grp")
+    width = owned_kernel.shape[0]
+    grad_second = owned_kernel.reshape(width, taps_second, in_chans).transpose(1, 2, 0)
     ker_first = w_first.shape[0]
-    in_chans = w_second.shape[1]
-    grad_second = owned[: taps_second * in_chans].reshape(taps_second, in_chans, width)
-    grad_first = owned[taps_second * in_chans : taps_second * in_chans + ker_first]
-    grad_gain = owned[taps_second * in_chans + ker_first]
-    grad_bias = owned[taps_second * in_chans + ker_first + 1]
+    grad_first = owned_small[:, :ker_first].T
+    grad_gain = owned_small[:, ker_first]
+    grad_bias = owned_small[:, ker_first + 1]
     return (features, grad_second, grad_first, grad_gain, grad_bias)
 
 

time: 428 us -> 688 us (1.61)
  waiting for transfers between devices: 285 us -> 524 us
  blocking collectives: 0 us -> 29.2 us
  local copies, waits for them, and re-layouts: 64.4 us -> 55.6 us
    unnamed x1 -> x4, waiting for transfers between devices: 0.02 us -> 203 us
    reduce_scatter x0 -> x1, waiting for transfers between devices: none -> 197 us  [shards(): lax.psum_scatter(grad_kernel, 'dev', scatter_dimension=0, tiled=True)]
    psum x1, waiting for transfers between devices: 277 us -> 116 us  [shards(): owned_kernel = lax.psum(part_kernel, 'grp')]
    psum x0 -> x1, blocking collectives: none -> 29.2 us  [shards(): owned_small = lax.psum(part_small, 'grp')]
    concatenate x1 -> x0, local copies, waits for them, and re-layouts: 9.86 us -> none  [local_pass(): jnp.concatenate([grad_kernel, grad_filter, grad_gain[None, :], grad_bias[...]
  transfers between devices with their start and end apart: 2 -> 4, of which waited for: 2 -> 4; matrix products, arithmetic and copies ran while one was open for 0% -> 1% of each run, Pallas kernels for 0% -> 0%
where the time goes in v1:
time: 688 us; the launch traced here: 687 us
  waiting for transfers between devices  524 us (76%)
  local copies, waits for them, and re-layouts  55.6 us (8%)
  blocking collectives  29.2 us (4%)
  other arithmetic  25.1 us (4%)
  matrix products  24.6 us (4%)
  between operations  14.1 us (2%)
  starting transfers between devices  13.8 us (2%)
    unnamed x4, waiting for transfers between devices  203 us
    reduce_scatter x1, waiting for transfers between devices, shards(): lax.psum_scatter(grad_kernel, 'dev', scatter_dimension=0, tiled=True)  197 us
    psum x1, waiting for transfers between devices, shards(): owned_kernel = lax.psum(part_kernel, 'grp')  116 us
    psum x1, blocking collectives, shards(): owned_small = lax.psum(part_small, 'grp')  29.2 us
    convert_element_type x1, other arithmetic, local_pass(): act0 = (jax.nn.gelu(lifted, approximate=False) * mask0).astype(jnp.bfloat16)  14.2 us
  transfers between devices with their start and end apart: 4, of which 4 were waited for; matrix products, arithmetic and copies ran while one was open for 1% of the time, Pallas kernels for 0%

profile of v1, /device:TPU:1, one launch (start us, length us, event | category | flops | bytes accessed | tf_op | source)
XLA Modules:
  0.0 686.9 jit_solution(4473526065860579296)
XLA Ops:
  7.2 0.0 copy-start
  7.2 0.9 copy.57
  8.1 0.7 compare_and_fusion.1
  8.8 0.1 copy.60
  8.9 0.1 reshape.272
  9.0 0.8 reshape.259
  9.7 7.1 %gather_fusion.1 = s32[1024]{0:T(1024)S(1)} fusion(s32[32,32]{1,0:T(8,128)S(1)} %reshape.259, s32[1024]{0:T(1024)S(1)} %reshape.272), kind=kCustom, calls=%fused_computation.1 | custom fusion | bytes 16384 | tf_op jit(solution)/shard_map/jit(take_along_axis)/gather | solution.py:98
  16.8 0.1 reshape.275
  16.9 0.1 constant_dynamic-slice_fusion.1
  17.0 0.1 copy.77
  17.1 0.7 fusion.63
  17.8 0.6 gather_fusion
  18.4 0.1 bitcast_select_fusion
  18.5 0.5 broadcast.271
  19.0 0.7 reduce
  19.7 0.7 reshape.291
  20.4 13.7 %all-to-all-start = ((bf16[32,2,192]{2,1,0:T(2,128)(2,1)}), bf16[32,2,192]{2,1,0:T(2,128)(2,1)S(1)}, u32[]{:S(2)}, u32[]{:S(2)}) async-start(bf16[32,2,192]{2,1,0:T(2,128)(2,1)} %reshape.291), calls=%async_computation | async-start | bytes 65536 | tf_op jit(solution)/shard_map/all_to_all | solution.py:97
  34.1 0.0 reduce-scatter.7.cloned.1.call-start
  34.2 0.1 fusion.61
  34.2 0.1 fusion.60
  34.3 8.6 %all-to-all-done = bf16[32,2,192]{2,1,0:T(2,128)(2,1)S(1)} async-done(((bf16[32,2,192]{2,1,0:T(2,128)(2,1)}), bf16[32,2,192]{2,1,0:T(2,128)(2,1)S(1)}, u32[]{:S(2)}, u32[]{:S(2)}) %all-to-all-start) | async-done | bytes 24608 | tf_op jit(solution)/shard_map/all_to_all | solution.py:97
  42.9 0.1 reshape.292
  43.0 0.1 copy.54
  43.1 0.1 reshape.258
  43.2 0.2 copy.73
  43.4 0.2 copy.74
  43.6 0.9 multiply_reduce_fusion.3
  44.6 0.1 broadcast_divide_fusion.2
  44.7 1.1 multiply_reduce_fusion.2
  45.8 0.1 add_rsqrt_fusion
  45.9 1.0 copy-done.1
  46.9 14.2 %fusion.3 = bf16[32,75,512]{2,1,0:T(8,128)(2,1)} fusion(f32[512]{0:T(512)S(1)} %copy-done.4, f32[512]{0:T(512)S(1)} %copy-done.5, f32[32,75]{1,0:T(8,128)S(1)} %fusion.60, f32[32,512]{1,0:T(8,128)S(1)} %add_rsqrt_fusion, f32[32,75,512]{2,1,0:T(8,128)S(1)} %get-tuple-element.42, f32[32,512]{1,0:T(8,128)S(1)} %broadcast_divide_fusion.2), kind=kLoop, calls=%fused_computation.7 | loop fusion | flops 87244800 | bytes 7517568 | tf_op jit(solution)/shard_map/convert_element_type | solution.py:40
  61.1 9.9 %slice.44 = bf16[32,37,512]{2,1,0:T(8,128)(2,1)} slice(bf16[32,75,512]{2,1,0:T(8,128)(2,1)} %fusion.3), slice={[0:32:1], [2:75:2], [0:512:1]} | slice | bytes 2424832 | tf_op jit(solution)/shard_map/slice | solution.py:43
  70.9 9.8 %slice.43 = bf16[32,37,512]{2,1,0:T(8,128)(2,1)} slice(bf16[32,75,512]{2,1,0:T(8,128)(2,1)} %fusion.3), slice={[0:32:1], [1:74:2], [0:512:1]} | slice | bytes 2424832 | tf_op jit(solution)/shard_map/slice | solution.py:43
  80.7 9.8 %slice.42 = bf16[32,37,512]{2,1,0:T(8,128)(2,1)} slice(bf16[32,75,512]{2,1,0:T(8,128)(2,1)} %fusion.3), slice={[0:32:1], [0:74:2], [0:512:1]} | slice | bytes 2424832 | tf_op jit(solution)/shard_map/slice | solution.py:43
  90.5 11.3 %fusion.35 = (bf16[32,37,512]{2,1,0:T(8,128)(2,1)S(1)}, bf16[32,37,512]{2,1,0:T(8,128)(2,1)S(1)}) fusion(bf16[32,37,512]{2,0,1:T(8,128)(2,1)} %param.15, f32[32,37]{1,0:T(8,128)S(1)} %fusion.61, bf16[1536,512,1]{1,0,2:T(8,128)(2,1)S(1)} %bitcast.81, bf16[32,37,512]{2,1,0:T(8,128)(2,1)} %slice.44, bf16[32,37,512]{2,1,0:T(8,128)(2,1)} %slice.43, ...), kind=kOutput, calls=%fused_computation.59 | convolution fusion | flops 1920466944 | bytes 8852096 | tf_op jit(solution)/shard_map/dot_general | solution.py:47
  101.8 2.2 fusion.51
  104.1 0.1 slice_bitcast_fusion.2
  104.2 0.2 slice.61
  104.4 0.2 slice_bitcast_fusion
  104.7 0.6 fusion.37
  105.3 0.6 pad_maximum_fusion
  106.0 2.8 copy.65
  108.8 2.8 copy.66
  111.7 5.9 multiply_reduce_fusion.1
  117.5 0.1 broadcast_divide_fusion.1
  117.6 3.7 fusion.55
  121.4 0.9 copy.70
  122.2 0.0 reduce-scatter.7.cloned.1.call-update
  122.3 0.0 reduce-scatter.5.cloned.1.call-start
  122.3 6.4 convolution_bitcast_fusion
  128.7 0.0 reduce-scatter.5.cloned.1.call-update
  128.7 0.0 all-reduce.3.cloned.1.call-start
  128.8 1.4 copy.67
  130.2 203.1 %reduce-scatter.7.cloned.1.call-done = f32[16,12]{1,0:T(8,128)} async-done(((f32[512,12]{1,0:T(8,128)}), f32[16,12]{1,0:T(8,128)}) %reduce-scatter.7.cloned.1.call-update) | async-done | bytes 784
  333.3 0.8 copy.71
  334.1 29.2 %psum.15 = f32[16,12]{0,1:T(8,128)S(1)} all-reduce(f32[16,12]{0,1:T(8,128)S(1)} %copy.71), channel_id=1, replica_groups=mesh['grp'=16,'dev'=32] {'grp'}, use_global_device_ids=true, to_apply=%region_9.10 | all-reduce | flops 192 | bytes 1536 | tf_op jit(solution)/shard_map/psum | solution.py:109
  363.3 0.6 slice_bitcast_fusion.3
  363.9 196.8 %reduce-scatter.5.cloned.1.call-done = f32[16,1536]{1,0:T(8,128)} async-done(((f32[512,1536]{1,0:T(8,128)}), f32[16,1536]{1,0:T(8,128)}) %reduce-scatter.5.cloned.1.call-update) | async-done | bytes 98320 | tf_op jit(solution)/shard_map/reduce_scatter | solution.py:106
  560.7 1.6 reshape.262
  562.3 0.0 all-reduce.3.cloned.1.call-update
  562.3 0.5 slice_bitcast_fusion.4
  562.8 116.0 %all-reduce.3.cloned.1.call-done = f32[3,512,16]{1,0,2:T(4,128)} async-done(((f32[3,512,16]{1,0,2:T(4,128)}), f32[3,512,16]{1,0,2:T(4,128)}) %all-reduce.3.cloned.1.call-update) | async-done | bytes 98320 | tf_op jit(solution)/shard_map/psum | solution.py:108
  678.8 1.6 copy.68
  (25 shorter events, 0.2 us)
Async XLA Ops:
  7.2 83.3 %copy-start = (bf16[3,512,512]{2,1,0:T(8,128)(2,1)S(1)}, bf16[3,512,512]{2,1,0:T(8,128)(2,1)}, u32[]{:S(2)}) copy-start(bf16[3,512,512]{2,1,0:T(8,128)(2,1)} %param.14) | copy-start | bytes 4718596
  9.7 8.1 %copy-start.2 = (bf16[32,384]{1,0:T(8,128)(2,1)S(1)}, bf16[32,384]{1,0:T(8,128)(2,1)}, u32[]{:S(2)}) copy-start(bf16[32,384]{1,0:T(8,128)(2,1)} %param.8) | copy-start | bytes 73732
  9.7 33.9 %copy-start.3 = (bf16[10,512]{1,0:T(8,128)(2,1)S(1)}, bf16[10,512]{1,0:T(8,128)(2,1)}, u32[]{:S(2)}) copy-start(bf16[10,512]{1,0:T(8,128)(2,1)} %param.11) | copy-start | bytes 30724
  20.4 22.5 %all-to-all-start = ((bf16[32,2,192]{2,1,0:T(2,128)(2,1)}), bf16[32,2,192]{2,1,0:T(2,128)(2,1)S(1)}, u32[]{:S(2)}, u32[]{:S(2)}) async-start(bf16[32,2,192]{2,1,0:T(2,128)(2,1)} %reshape.291), calls=%async_computation | async-start | bytes 65536 | tf_op jit(solution)/shard_map/all_to_all | solution.py:97
  34.1 299.2 %reduce-scatter.7.cloned.1.call-start = ((), (), s32[]{:S(2)}) async-start(), calls=%async_computation.5 | async-start | bytes 270336
  43.6 3.3 copy-start.4
  43.6 3.3 copy-start.5
  44.6 2.3 copy-start.1
  101.8 2.3 copy-start.6
  108.8 2.9 slice-start
  108.8 2.9 slice-start.1
  122.3 438.4 %reduce-scatter.5.cloned.1.call-start = ((), (), s32[]{:S(2)}) async-start(), calls=%async_computation.3 | async-start | bytes 3244032 | tf_op jit(solution)/shard_map/reduce_scatter | solution.py:106
  128.7 550.0 %all-reduce.3.cloned.1.call-start = ((), (), s32[]{:S(2)}) async-start(), calls=%async_computation.4 | async-start | bytes 262144 | tf_op jit(solution)/shard_map/psum | solution.py:108
Sparse Core Ops, SparseCore 0:
  122.4 210.8 reduce-scatter.6
  338.4 222.2 reduce-scatter.4
  563.0 115.7 all-reduce.2

commit v2 on v1

--- a/solution.py
+++ b/solution.py
@@ -103,16 +103,30 @@
     )
     taps_second = w_second.shape[0]
     in_chans = w_second.shape[1]
-    part_kernel = lax.psum_scatter(grad_kernel, "dev", scatter_dimension=0, tiled=True)
-    part_small = lax.psum_scatter(small, "dev", scatter_dimension=0, tiled=True)
-    owned_kernel = lax.psum(part_kernel, "grp")
-    owned_small = lax.psum(part_small, "grp")
-    width = owned_kernel.shape[0]
-    grad_second = owned_kernel.reshape(width, taps_second, in_chans).transpose(1, 2, 0)
     ker_first = w_first.shape[0]
-    grad_first = owned_small[:, :ker_first].T
-    grad_gain = owned_small[:, ker_first]
-    grad_bias = owned_small[:, ker_first + 1]
+    members = lax.axis_size("dev")
+    groups = lax.axis_size("grp")
+    full = jnp.concatenate([grad_kernel, small], axis=1)
+    chans, span = full.shape
+    width = chans // members
+    pieces = lax.all_to_all(
+        full.reshape(members, width, span), "dev", split_axis=0, concat_axis=0, tiled=True
+    )
+    part = jnp.sum(pieces, axis=0)
+    sub = width // groups
+    mine = lax.all_to_all(
+        part.reshape(groups, sub, span), "grp", split_axis=0, concat_axis=0, tiled=True
+    )
+    mine = jnp.sum(mine, axis=0)
+    spread = jnp.broadcast_to(mine[None], (groups, sub, span))
+    owned = lax.all_to_all(spread, "grp", split_axis=0, concat_axis=0, tiled=True)
+    owned = owned.reshape(width, span)
+    grad_second = (
+        owned[:, : taps_second * in_chans].reshape(width, taps_second, in_chans).transpose(1, 2, 0)
+    )
+    grad_first = owned[:, taps_second * in_chans : taps_second * in_chans + ker_first].T
+    grad_gain = owned[:, taps_second * in_chans + ker_first]
+    grad_bias = owned[:, taps_second * in_chans + ker_first + 1]
     return (features, grad_second, grad_first, grad_gain, grad_bias)
 
 

time: 688 us -> 256 us (0.37)
  waiting for transfers between devices: 524 us -> 15.6 us
  blocking collectives: 29.2 us -> 101 us
  between operations: 14.1 us -> 1.05 us
  matrix products: 24.6 us -> 31.7 us
    unnamed x4 -> x0, waiting for transfers between devices: 203 us -> none
    reduce_scatter x1 -> x0, waiting for transfers between devices: 197 us -> none  [shards(): lax.psum_scatter(grad_kernel, 'dev', scatter_dimension=0, tiled=True)]
    psum x1 -> x0, waiting for transfers between devices: 116 us -> none  [shards(): owned_kernel = lax.psum(part_kernel, 'grp')]
    all_to_all x0 -> x2, blocking collectives: none -> 101 us  [the longest x1 80.9 us: shards(): lax.all_to_all(full.reshape(members, width, span), 'dev', split_axis=0, c...]
    psum x1 -> x0, blocking collectives: 29.2 us -> none  [shards(): owned_small = lax.psum(part_small, 'grp')]
    dot_general x1, matrix products: 3.74 us -> 13 us  [local_pass(): lax.dot_general(dpre0.reshape(rows * frames0, chans), patches.astype(jnp....]
    all_to_all x0 -> x1, waiting for transfers between devices: none -> 7.01 us  [shards(): lax.all_to_all(spread, 'grp', split_axis=0, concat_axis=0, tiled=True)]
  transfers between devices with their start and end apart: 4 -> 2, of which waited for: 4 -> 2; matrix products, arithmetic and copies ran while one was open for 1% -> 1% of each run, Pallas kernels for 0% -> 0%
where the time goes in v2:
time: 256 us; the launch traced here: 254 us
  blocking collectives  101 us (39%)
  local copies, waits for them, and re-layouts  58 us (23%)
  matrix products  31.7 us (12%)
  other arithmetic  29.7 us (12%)
  starting transfers between devices  17.1 us (7%)
  waiting for transfers between devices  15.6 us (6%)
    all_to_all x1, blocking collectives, shards(): lax.all_to_all(full.reshape(members, width, span), 'dev', split_axis=0, c...  80.9 us
    all_to_all x1, blocking collectives, shards(): lax.all_to_all(part.reshape(groups, sub, span), 'grp', split_axis=0, conc...  20.3 us
    convert_element_type x1, other arithmetic, local_pass(): act0 = (jax.nn.gelu(lifted, approximate=False) * mask0).astype(jnp.bfloat16)  14.2 us
    all_to_all x1, starting transfers between devices, shards(): lax.all_to_all(outgoing, 'dev', split_axis=0, concat_axis=0, tiled=True)  13.7 us
    dot_general x1, matrix products, local_pass(): lax.dot_general(dpre0.reshape(rows * frames0, chans), patches.astype(jnp....  13 us
    dot_general x1, matrix products, local_pass(): jnp.dot(taps, kernel, preferred_element_type=jnp.float32)  11.5 us
    slice x1, local copies, waits for them, and re-layouts, local_pass(): act0[:, 2:span + 1:2]  9.86 us
    slice x1, local copies, waits for them, and re-layouts, local_pass(): act0[:, 1:span:2]  9.77 us
  transfers between devices with their start and end apart: 2, of which 2 were waited for; matrix products, arithmetic and copies ran while one was open for 1% of the time, Pallas kernels for 0%

profile of v2, /device:TPU:1, one launch (start us, length us, event | category | flops | bytes accessed | tf_op | source)
XLA Modules:
  0.0 254.4 jit_solution(12782320416287695537)
XLA Ops:
  0.6 0.0 copy-start
  0.6 0.9 copy.65
  1.6 0.7 compare_and_fusion.1
  2.3 0.1 copy.68
  2.4 0.1 reshape.292
  2.4 0.8 reshape.277
  3.2 7.1 %gather_fusion.1 = s32[1024]{0:T(1024)S(1)} fusion(s32[32,32]{1,0:T(8,128)S(1)} %reshape.277, s32[1024]{0:T(1024)S(1)} %reshape.292), kind=kCustom, calls=%fused_computation.1 | custom fusion | bytes 16384 | tf_op jit(solution)/shard_map/jit(take_along_axis)/gather | solution.py:98
  10.3 0.1 reshape.295
  10.3 0.1 constant_dynamic-slice_fusion.1
  10.4 0.1 copy.89
  10.5 0.7 fusion.61
  11.3 0.6 gather_fusion
  11.9 0.1 bitcast_select_fusion
  12.0 0.5 broadcast.275
  12.5 0.7 reduce.5
  13.2 0.7 reshape.311
  13.9 13.7 %all-to-all-start = ((bf16[32,2,192]{2,1,0:T(2,128)(2,1)}), bf16[32,2,192]{2,1,0:T(2,128)(2,1)S(1)}, u32[]{:S(2)}, u32[]{:S(2)}) async-start(bf16[32,2,192]{2,1,0:T(2,128)(2,1)} %reshape.311), calls=%async_computation | async-start | bytes 65536 | tf_op jit(solution)/shard_map/all_to_all | solution.py:97
  27.6 0.1 fusion.59
  27.7 0.1 fusion.58
  27.7 0.0 copy-start.11
  27.8 8.6 %all-to-all-done = bf16[32,2,192]{2,1,0:T(2,128)(2,1)S(1)} async-done(((bf16[32,2,192]{2,1,0:T(2,128)(2,1)}), bf16[32,2,192]{2,1,0:T(2,128)(2,1)S(1)}, u32[]{:S(2)}, u32[]{:S(2)}) %all-to-all-start) | async-done | bytes 24608 | tf_op jit(solution)/shard_map/all_to_all | solution.py:97
  36.4 0.1 reshape.312
  36.5 0.1 copy.62
  36.6 0.1 reshape.276
  36.7 0.2 copy.85
  36.9 0.2 copy.86
  37.1 0.9 multiply_reduce_fusion.3
  38.1 0.1 broadcast_divide_fusion.2
  38.1 1.2 multiply_reduce_fusion.2
  39.3 0.1 add_rsqrt_fusion
  39.4 0.9 copy-done.1
  40.4 14.2 %fusion.3 = bf16[32,75,512]{2,1,0:T(8,128)(2,1)} fusion(f32[512]{0:T(512)S(1)} %copy-done.9, f32[512]{0:T(512)S(1)} %copy-done.10, f32[32,75]{1,0:T(8,128)S(1)} %fusion.58, f32[32,512]{1,0:T(8,128)S(1)} %add_rsqrt_fusion, f32[32,75,512]{2,1,0:T(8,128)S(1)} %get-tuple-element.42, f32[32,512]{1,0:T(8,128)S(1)} %broadcast_divide_fusion.2), kind=kLoop, calls=%fused_computation.7 | loop fusion | flops 87244800 | bytes 7517568 | tf_op jit(solution)/shard_map/convert_element_type | solution.py:40
  54.5 9.9 %slice.47 = bf16[32,37,512]{2,1,0:T(8,128)(2,1)} slice(bf16[32,75,512]{2,1,0:T(8,128)(2,1)} %fusion.3), slice={[0:32:1], [2:75:2], [0:512:1]} | slice | bytes 2424832 | tf_op jit(solution)/shard_map/slice | solution.py:43
  64.4 9.8 %slice.46 = bf16[32,37,512]{2,1,0:T(8,128)(2,1)} slice(bf16[32,75,512]{2,1,0:T(8,128)(2,1)} %fusion.3), slice={[0:32:1], [1:74:2], [0:512:1]} | slice | bytes 2424832 | tf_op jit(solution)/shard_map/slice | solution.py:43
  74.2 9.8 %slice.45 = bf16[32,37,512]{2,1,0:T(8,128)(2,1)} slice(bf16[32,75,512]{2,1,0:T(8,128)(2,1)} %fusion.3), slice={[0:32:1], [0:74:2], [0:512:1]} | slice | bytes 2424832 | tf_op jit(solution)/shard_map/slice | solution.py:43
  84.0 11.5 %fusion.35 = (bf16[32,37,512]{2,1,0:T(8,128)(2,1)S(1)}, bf16[32,37,512]{2,1,0:T(8,128)(2,1)S(1)}) fusion(bf16[32,37,512]{2,0,1:T(8,128)(2,1)} %param.15, f32[32,37]{1,0:T(8,128)S(1)} %fusion.59, bf16[1536,512,1]{1,0,2:T(8,128)(2,1)S(1)} %bitcast.80, bf16[32,37,512]{2,1,0:T(8,128)(2,1)} %slice.47, bf16[32,37,512]{2,1,0:T(8,128)(2,1)} %slice.46, ...), kind=kOutput, calls=%fused_computation.58 | convolution fusion | flops 1920466944 | bytes 8852096 | tf_op jit(solution)/shard_map/dot_general | solution.py:47
  95.5 4.0 %fusion.50 = f32[512,1536,1]{1,0,2:T(8,128)} fusion(bf16[32,37,512]{2,1,0:T(8,128)(2,1)S(1)} %get-tuple-element.35, bf16[32,37,512]{2,1,0:T(8,128)(2,1)S(1)} %copy-done.3, bf16[32,37,512]{2,1,0:T(8,128)(2,1)S(1)} %copy-done.4, bf16[32,37,512]{2,1,0:T(8,128)(2,1)S(1)} %copy-done.5), kind=kOutput, calls=%fused_computation.83 | convolution fusion | flops 1873182720 | bytes 7995392 | tf_op jit(solution)/shard_map/dot_general | solution.py:58
  99.5 2.3 fusion.52
  101.8 0.1 slice_bitcast_fusion.2
  101.8 0.2 slice.65
  102.1 0.2 slice_bitcast_fusion
  102.3 0.6 fusion.37
  103.0 0.8 pad_maximum_fusion
  103.8 2.8 %copy.73 = f32[32,37,2,512]{3,0,2,1:T(8,128)S(1)} copy(f32[32,37,2,512]{3,1,2,0:T(8,128)S(1)} %pad_maximum_fusion) | data formatting | bytes 9699328 | tf_op jit(solution)/shard_map/stack | solution.py:68
  106.6 2.8 %copy.74 = f32[32,74,512]{2,1,0:T(8,128)S(1)} copy(f32[32,74,512]{2,0,1:T(8,128)S(1)} %bitcast.83) | data formatting | bytes 9699328 | tf_op jit(solution)/shard_map/reshape | solution.py:68
  109.5 7.2 %multiply_reduce_fusion = (f32[512]{0:T(512)S(1)}, f32[32,512]{1,0:T(8,128)}, f32[32,512]{1,0:T(8,128)}, f32[512]{0:T(512)}, f32[32,75,512]{2,1,0:T(8,128)}) fusion(f32[32,512]{1,0:T(8,128)S(1)} %add_rsqrt_fusion, f32[32,75]{1,0:T(8,128)S(1)} %fusion.58, f32[32,75,512]{2,1,0:T(8,128)S(1)} %bitcast.82, f32[32,512]{1,0:T(8,128)S(1)} %broadcast_divide_fusion.2, ...), kind=kLoop, calls=%fused_computation.15 | loop fusion | flops 28228608 | bytes 15025536 | tf_op jit(solution)/shard_map/reduce_sum | solution.py:71
  116.7 0.2 concatenate.36
  116.9 0.9 concatenate.37
  117.8 1.0 broadcast_divide_fusion.1
  118.8 13.0 %fusion.10 = f32[512,10,1]{1,0,2:T(8,128)} fusion(f32[32,75,512]{2,1,0:T(8,128)} %get-tuple-element.31, f32[32,512]{1,0:T(8,128)S(1)} %get-tuple-element.40, f32[32,512]{1,0:T(8,128)S(1)} %get-tuple-element.39, f32[512]{0:T(512)} %param.12, f32[32,512]{1,0:T(8,128)S(1)} %add_rsqrt_fusion, f32[32,75]{1,0:T(8,128)S(1)} %fusion.58, ...), kind=kOutput, calls=%fused_computation.16 | convolution fusion | flops 158611200 | bytes 10172672 | tf_op jit(solution)/shard_map/dot_general | solution.py:77
  131.8 4.4 %concatenate.32 = f32[32,16,1548]{2,1,0:T(8,128)} concatenate(f32[32,16,1536]{2,1,0:T(8,128)} %bitcast.84, f32[32,16,10]{2,1,0:T(8,128)} %bitcast.89, f32[32,16,1]{2,1,0:T(8,128)S(1)} %concatenate.36, f32[32,16,1]{2,1,0:T(8,128)S(1)} %concatenate.37), dimensions={2} | concatenate | bytes 6340608 | tf_op jit(solution)/shard_map/concatenate | solution.py:109
  136.1 80.9 %all_to_all.24 = f32[32,16,1548]{2,1,0:T(8,128)} all-to-all(f32[32,16,1548]{2,1,0:T(8,128)} %concatenate.32), channel_id=1, replica_groups=mesh['grp'=16,'dev'=32] {'dev'}, dimensions={0} | all-to-all | bytes 6340608 | tf_op jit(solution)/shard_map/all_to_all | solution.py:112
  217.1 2.1 reduce_sum.78
  219.2 0.1 reshape.281
  219.3 20.3 %all_to_all.25 = f32[16,1,1548]{2,1,0:T(1,128)S(1)} all-to-all(f32[16,1,1548]{2,1,0:T(1,128)S(1)} %reshape.281), channel_id=1, replica_groups=mesh['grp'=16,'dev'=32] {'grp'}, dimensions={0} | all-to-all | bytes 198144 | tf_op jit(solution)/shard_map/all_to_all | solution.py:117
  239.6 0.1 reduce_sum.79
  239.7 0.7 broadcast_in_dim.19
  240.4 3.4 %all-to-all-start.3 = ((f32[16,1,1548]{2,1,0:T(1,128)}), f32[16,1,1548]{2,1,0:T(1,128)S(1)}, u32[]{:S(2)}, u32[]{:S(2)}) async-start(f32[16,1,1548]{2,1,0:T(1,128)} %broadcast_in_dim.19), calls=%async_computation.3 | async-start | bytes 212992 | tf_op jit(solution)/shard_map/all_to_all | solution.py:122
  243.8 1.4 copy.78
  245.2 7.0 %all-to-all-done.3 = f32[16,1,1548]{2,1,0:T(1,128)S(1)} async-done(((f32[16,1,1548]{2,1,0:T(1,128)}), f32[16,1,1548]{2,1,0:T(1,128)S(1)}, u32[]{:S(2)}, u32[]{:S(2)}) %all-to-all-start.3) | async-done | bytes 99104 | tf_op jit(solution)/shard_map/all_to_all | solution.py:122
  252.2 0.7 slice_reduce_fusion
  252.9 0.7 copy.80
  253.6 0.1 reshape.283
  253.7 0.7 copy.79
  (36 shorter events, 0.2 us)
Async XLA Ops:
  0.6 83.3 %copy-start = (bf16[3,512,512]{2,1,0:T(8,128)(2,1)S(1)}, bf16[3,512,512]{2,1,0:T(8,128)(2,1)}, u32[]{:S(2)}) copy-start(bf16[3,512,512]{2,1,0:T(8,128)(2,1)} %param.14) | copy-start | bytes 4718596
  3.2 8.1 %copy-start.2 = (bf16[32,384]{1,0:T(8,128)(2,1)S(1)}, bf16[32,384]{1,0:T(8,128)(2,1)}, u32[]{:S(2)}) copy-start(bf16[32,384]{1,0:T(8,128)(2,1)} %param.8) | copy-start | bytes 73732
  3.2 33.9 %copy-start.8 = (bf16[10,512]{1,0:T(8,128)(2,1)S(1)}, bf16[10,512]{1,0:T(8,128)(2,1)}, u32[]{:S(2)}) copy-start(bf16[10,512]{1,0:T(8,128)(2,1)} %param.11) | copy-start | bytes 30724
  13.9 22.5 %all-to-all-start = ((bf16[32,2,192]{2,1,0:T(2,128)(2,1)}), bf16[32,2,192]{2,1,0:T(2,128)(2,1)S(1)}, u32[]{:S(2)}, u32[]{:S(2)}) async-start(bf16[32,2,192]{2,1,0:T(2,128)(2,1)} %reshape.311), calls=%async_computation | async-start | bytes 65536 | tf_op jit(solution)/shard_map/all_to_all | solution.py:97
  27.7 11.6 %copy-start.11 = (f32[32]{0:T(128)}, f32[32]{0:T(128)S(1)}, u32[]{:S(2)}) copy-start(f32[32]{0:T(128)S(1)} %fusion.62) | copy-start | bytes 388
  36.9 2.4 copy-start.6
  37.1 2.2 copy-start.7
  37.1 3.3 %copy-start.9 = (f32[512]{0:T(512)S(1)}, f32[512]{0:T(512)}, u32[]{:S(2)}) copy-start(f32[512]{0:T(512)} %param.13) | copy-start | bytes 6148
  37.1 3.3 %copy-start.10 = (f32[512]{0:T(512)S(1)}, f32[512]{0:T(512)}, u32[]{:S(2)}) copy-start(f32[512]{0:T(512)} %param.12) | copy-start | bytes 6148
  38.1 2.3 copy-start.1
  84.0 11.5 %copy-start.3 = (bf16[32,37,512]{2,1,0:T(8,128)(2,1)S(1)}, bf16[32,37,512]{2,1,0:T(8,128)(2,1)}, u32[]{:S(2)}) copy-start(bf16[32,37,512]{2,1,0:T(8,128)(2,1)} %slice.47) | copy-start | bytes 3637252
  84.0 11.5 %copy-start.4 = (bf16[32,37,512]{2,1,0:T(8,128)(2,1)S(1)}, bf16[32,37,512]{2,1,0:T(8,128)(2,1)}, u32[]{:S(2)}) copy-start(bf16[32,37,512]{2,1,0:T(8,128)(2,1)} %slice.46) | copy-start | bytes 3637252
  84.0 11.6 %copy-start.5 = (bf16[32,37,512]{2,1,0:T(8,128)(2,1)S(1)}, bf16[32,37,512]{2,1,0:T(8,128)(2,1)}, u32[]{:S(2)}) copy-start(bf16[32,37,512]{2,1,0:T(8,128)(2,1)} %slice.45) | copy-start | bytes 3637252
  106.6 2.9 %slice-start = ((s8[5242880]{0:T(1024)(128)(4,1)}), s8[4194304]{0:T(1024)(128)(4,1)S(1)}, s32[]{:S(2)}) async-start(s8[5242880]{0:T(1024)(128)(4,1)} %bitcast.81), calls=%async_computation.4 | async-start | bytes 8388608
  106.6 2.9 %slice-start.1 = ((s8[5242880]{0:T(1024)(128)(4,1)}), s8[1048576]{0:T(1024)(128)(4,1)S(1)}, s32[]{:S(2)}) async-start(s8[5242880]{0:T(1024)(128)(4,1)} %bitcast.81), calls=%async_computation.5 | async-start | bytes 2097152
  240.4 11.8 %all-to-all-start.3 = ((f32[16,1,1548]{2,1,0:T(1,128)}), f32[16,1,1548]{2,1,0:T(1,128)S(1)}, u32[]{:S(2)}, u32[]{:S(2)}) async-start(f32[16,1,1548]{2,1,0:T(1,128)} %broadcast_in_dim.19), calls=%async_computation.3 | async-start | bytes 212992 | tf_op jit(solution)/shard_map/all_to_all | solution.py:122

commit v3 on v2

--- a/solution.py
+++ b/solution.py
@@ -1,7 +1,83 @@
+import functools
+
 import jax
 import jax.numpy as jnp
 from jax import lax
+from jax.experimental import pallas as pl
+from jax.experimental.pallas import tpu as pltpu
 from jax.sharding import PartitionSpec as P
+
+MESH = pl.DeviceIdType.MESH
+
+
+def exchange_kernel(members, src_ref, dst_ref, send_sems, recv_sems, local_sem):
+    me = lax.axis_index("dev")
+    grp = lax.axis_index("grp")
+    barrier = pltpu.get_barrier_semaphore()
+
+    def greet(step, carry):
+        peer = lax.rem(me + step, members)
+        pl.semaphore_signal(barrier, inc=1, device_id=(grp, peer), device_id_type=MESH)
+        return carry
+
+    lax.fori_loop(1, members, greet, 0)
+    pl.semaphore_wait(barrier, members - 1)
+    local = pltpu.make_async_copy(src_ref.at[me], dst_ref.at[me], local_sem)
+    local.start()
+
+    def send(step, carry):
+        peer = lax.rem(me + step, members)
+        pltpu.make_async_remote_copy(
+            src_ref=src_ref.at[peer],
+            dst_ref=dst_ref.at[me],
+            send_sem=send_sems.at[step],
+            recv_sem=recv_sems.at[step],
+            device_id=(grp, peer),
+            device_id_type=MESH,
+        ).start()
+        return carry
+
+    lax.fori_loop(1, members, send, 0)
+
+    def finish(step, carry):
+        peer = lax.rem(me + step, members)
+        sender = lax.rem(me + members - step, members)
+        pltpu.make_async_remote_copy(
+            src_ref=src_ref.at[peer],
+            dst_ref=dst_ref.at[me],
+            send_sem=send_sems.at[step],
+            recv_sem=recv_sems.at[step],
+            device_id=(grp, peer),
+            device_id_type=MESH,
+        ).wait_send()
+        pltpu.make_async_remote_copy(
+            src_ref=src_ref.at[me],
+            dst_ref=dst_ref.at[sender],
+            send_sem=send_sems.at[step],
+            recv_sem=recv_sems.at[step],
+            device_id=(grp, sender),
+            device_id_type=MESH,
+        ).wait_recv()
+        return carry
+
+    lax.fori_loop(1, members, finish, 0)
+    local.wait()
+
+
+def exchange(blocks):
+    members = blocks.shape[0]
+    return pl.pallas_call(
+        functools.partial(exchange_kernel, members),
+        out_shape=jax.ShapeDtypeStruct(blocks.shape, blocks.dtype),
+        in_specs=[pl.BlockSpec(memory_space=pl.ANY)],
+        out_specs=pl.BlockSpec(memory_space=pl.ANY),
+        scratch_shapes=[
+            pltpu.SemaphoreType.DMA((members,)),
+            pltpu.SemaphoreType.DMA((members,)),
+            pltpu.SemaphoreType.DMA,
+        ],
+        compiler_params=pltpu.CompilerParams(collective_id=0, has_side_effects=True),
+    )(blocks)
 
 
 def gelu_slope(value):
@@ -109,9 +185,7 @@
     full = jnp.concatenate([grad_kernel, small], axis=1)
     chans, span = full.shape
     width = chans // members
-    pieces = lax.all_to_all(
-        full.reshape(members, width, span), "dev", split_axis=0, concat_axis=0, tiled=True
-    )
+    pieces = exchange(full.reshape(members, width, span))
     part = jnp.sum(pieces, axis=0)
     sub = width // groups
     mine = lax.all_to_all(

time: 256 us -> 252 us (0.984)
  blocking collectives: 101 us -> 18.6 us
  Pallas kernels: 0 us -> 79.7 us
    all_to_all x1 -> x0, blocking collectives: 80.9 us -> none  [shards(): lax.all_to_all(full.reshape(members, width, span), 'dev', split_axis=0, c...]
    pallas_call x0 -> x1, Pallas kernels: none -> 79.7 us  [exchange(): pl.pallas_call(functools.partial(exchange_kernel, members), out_shape=jax...]
where the time goes in v3:
time: 252 us; the launch traced here: 251 us
  Pallas kernels  79.7 us (32%)
  local copies, waits for them, and re-layouts  58 us (23%)
  matrix products  31.6 us (13%)
  other arithmetic  29.6 us (12%)
  blocking collectives  18.6 us (7%)
  starting transfers between devices  17.1 us (7%)
  waiting for transfers between devices  15.6 us (6%)
    pallas_call x1, Pallas kernels, exchange(): pl.pallas_call(functools.partial(exchange_kernel, members), out_shape=jax...  79.7 us
    all_to_all x1, blocking collectives, shards(): lax.all_to_all(part.reshape(groups, sub, span), 'grp', split_axis=0, conc...  18.6 us
    convert_element_type x1, other arithmetic, local_pass(): act0 = (jax.nn.gelu(lifted, approximate=False) * mask0).astype(jnp.bfloat16)  14.2 us
    all_to_all x1, starting transfers between devices, shards(): lax.all_to_all(outgoing, 'dev', split_axis=0, concat_axis=0, tiled=True)  13.7 us
    dot_general x1, matrix products, local_pass(): lax.dot_general(dpre0.reshape(rows * frames0, chans), patches.astype(jnp....  13 us
    dot_general x1, matrix products, local_pass(): jnp.dot(taps, kernel, preferred_element_type=jnp.float32)  11.5 us
    slice x1, local copies, waits for them, and re-layouts, local_pass(): act0[:, 2:span + 1:2]  9.86 us
    slice x1, local copies, waits for them, and re-layouts, local_pass(): act0[:, 1:span:2]  9.77 us
  transfers between devices with their start and end apart: 2, of which 2 were waited for; matrix products, arithmetic and copies ran while one was open for 1% of the time, Pallas kernels for 0%

profile of v3, /device:TPU:1, one launch (start us, length us, event | category | flops | bytes accessed | tf_op | source)
XLA Modules:
  0.0 251.2 jit_solution(5722847122600535663)
XLA Ops:
  0.6 0.0 copy-start
  0.6 0.9 copy.65
  1.6 0.7 compare_and_fusion.1
  2.3 0.1 copy.68
  2.4 0.1 reshape.292
  2.4 0.8 reshape.277
  3.2 7.1 %gather_fusion.1 = s32[1024]{0:T(1024)S(1)} fusion(s32[32,32]{1,0:T(8,128)S(1)} %reshape.277, s32[1024]{0:T(1024)S(1)} %reshape.292), kind=kCustom, calls=%fused_computation.1 | custom fusion | bytes 16384 | tf_op jit(solution)/shard_map/jit(take_along_axis)/gather | solution.py:174
  10.3 0.1 reshape.295
  10.3 0.1 constant_dynamic-slice_fusion.1
  10.4 0.1 copy.90
  10.5 0.7 fusion.61
  11.3 0.6 gather_fusion
  11.9 0.1 bitcast_select_fusion
  12.0 0.5 broadcast.275
  12.5 0.7 reduce.5
  13.2 0.7 reshape.311
  13.9 13.7 %all-to-all-start = ((bf16[32,2,192]{2,1,0:T(2,128)(2,1)}), bf16[32,2,192]{2,1,0:T(2,128)(2,1)S(1)}, u32[]{:S(2)}, u32[]{:S(2)}) async-start(bf16[32,2,192]{2,1,0:T(2,128)(2,1)} %reshape.311), calls=%async_computation | async-start | bytes 65536 | tf_op jit(solution)/shard_map/all_to_all | solution.py:173
  27.6 0.1 fusion.59
  27.7 0.1 fusion.58
  27.7 0.0 copy-start.11
  27.8 8.6 %all-to-all-done = bf16[32,2,192]{2,1,0:T(2,128)(2,1)S(1)} async-done(((bf16[32,2,192]{2,1,0:T(2,128)(2,1)}), bf16[32,2,192]{2,1,0:T(2,128)(2,1)S(1)}, u32[]{:S(2)}, u32[]{:S(2)}) %all-to-all-start) | async-done | bytes 24608 | tf_op jit(solution)/shard_map/all_to_all | solution.py:173
  36.4 0.1 reshape.312
  36.5 0.1 copy.62
  36.6 0.1 reshape.276
  36.7 0.2 copy.86
  36.9 0.2 copy.87
  37.1 0.9 multiply_reduce_fusion.3
  38.1 0.1 broadcast_divide_fusion.2
  38.1 1.2 multiply_reduce_fusion.2
  39.3 0.1 add_rsqrt_fusion
  39.4 0.9 copy-done.1
  40.4 14.2 %fusion.3 = bf16[32,75,512]{2,1,0:T(8,128)(2,1)} fusion(f32[512]{0:T(512)S(1)} %copy-done.9, f32[512]{0:T(512)S(1)} %copy-done.10, f32[32,75]{1,0:T(8,128)S(1)} %fusion.58, f32[32,512]{1,0:T(8,128)S(1)} %add_rsqrt_fusion, f32[32,75,512]{2,1,0:T(8,128)S(1)} %get-tuple-element.42, f32[32,512]{1,0:T(8,128)S(1)} %broadcast_divide_fusion.2), kind=kLoop, calls=%fused_computation.7 | loop fusion | flops 87244800 | bytes 7517568 | tf_op jit(solution)/shard_map/convert_element_type | solution.py:116
  54.5 9.9 %slice.47 = bf16[32,37,512]{2,1,0:T(8,128)(2,1)} slice(bf16[32,75,512]{2,1,0:T(8,128)(2,1)} %fusion.3), slice={[0:32:1], [2:75:2], [0:512:1]} | slice | bytes 2424832 | tf_op jit(solution)/shard_map/slice | solution.py:119
  64.4 9.8 %slice.46 = bf16[32,37,512]{2,1,0:T(8,128)(2,1)} slice(bf16[32,75,512]{2,1,0:T(8,128)(2,1)} %fusion.3), slice={[0:32:1], [1:74:2], [0:512:1]} | slice | bytes 2424832 | tf_op jit(solution)/shard_map/slice | solution.py:119
  74.2 9.8 %slice.45 = bf16[32,37,512]{2,1,0:T(8,128)(2,1)} slice(bf16[32,75,512]{2,1,0:T(8,128)(2,1)} %fusion.3), slice={[0:32:1], [0:74:2], [0:512:1]} | slice | bytes 2424832 | tf_op jit(solution)/shard_map/slice | solution.py:119
  84.0 11.5 %fusion.35 = (bf16[32,37,512]{2,1,0:T(8,128)(2,1)S(1)}, bf16[32,37,512]{2,1,0:T(8,128)(2,1)S(1)}) fusion(bf16[32,37,512]{2,0,1:T(8,128)(2,1)} %param.15, f32[32,37]{1,0:T(8,128)S(1)} %fusion.59, bf16[1536,512,1]{1,0,2:T(8,128)(2,1)S(1)} %bitcast.79, bf16[32,37,512]{2,1,0:T(8,128)(2,1)} %slice.47, bf16[32,37,512]{2,1,0:T(8,128)(2,1)} %slice.46, ...), kind=kOutput, calls=%fused_computation.58 | convolution fusion | flops 1920466944 | bytes 8852096 | tf_op jit(solution)/shard_map/dot_general | solution.py:123
  95.5 4.0 %fusion.50 = f32[512,1536,1]{1,0,2:T(8,128)} fusion(bf16[32,37,512]{2,1,0:T(8,128)(2,1)S(1)} %get-tuple-element.35, bf16[32,37,512]{2,1,0:T(8,128)(2,1)S(1)} %copy-done.3, bf16[32,37,512]{2,1,0:T(8,128)(2,1)S(1)} %copy-done.4, bf16[32,37,512]{2,1,0:T(8,128)(2,1)S(1)} %copy-done.5), kind=kOutput, calls=%fused_computation.83 | convolution fusion | flops 1873182720 | bytes 7995392 | tf_op jit(solution)/shard_map/dot_general | solution.py:134
  99.5 2.2 fusion.52
  101.8 0.1 slice_bitcast_fusion.2
  101.8 0.2 slice.65
  102.1 0.2 slice_bitcast_fusion
  102.3 0.6 fusion.37
  103.0 0.6 pad_maximum_fusion
  103.6 2.8 %copy.73 = f32[32,37,2,512]{3,0,2,1:T(8,128)S(1)} copy(f32[32,37,2,512]{3,1,2,0:T(8,128)S(1)} %pad_maximum_fusion) | data formatting | bytes 9699328 | tf_op jit(solution)/shard_map/stack | solution.py:144
  106.5 2.8 %copy.74 = f32[32,74,512]{2,1,0:T(8,128)S(1)} copy(f32[32,74,512]{2,0,1:T(8,128)S(1)} %bitcast.82) | data formatting | bytes 9699328 | tf_op jit(solution)/shard_map/reshape | solution.py:144
  109.3 7.2 %multiply_reduce_fusion = (f32[512]{0:T(512)S(1)}, f32[32,512]{1,0:T(8,128)}, f32[32,512]{1,0:T(8,128)}, f32[512]{0:T(512)}, f32[32,75,512]{2,1,0:T(8,128)}) fusion(f32[32,512]{1,0:T(8,128)S(1)} %add_rsqrt_fusion, f32[32,75]{1,0:T(8,128)S(1)} %fusion.58, f32[32,75,512]{2,1,0:T(8,128)S(1)} %bitcast.81, f32[32,512]{1,0:T(8,128)S(1)} %broadcast_divide_fusion.2, ...), kind=kLoop, calls=%fused_computation.15 | loop fusion | flops 28228608 | bytes 15025536 | tf_op jit(solution)/shard_map/reduce_sum | solution.py:147
  116.6 0.2 concatenate.36
  116.8 0.9 concatenate.37
  117.7 1.0 broadcast_divide_fusion.1
  118.7 13.0 %fusion.10 = f32[512,10,1]{1,0,2:T(8,128)} fusion(f32[32,75,512]{2,1,0:T(8,128)} %get-tuple-element.31, f32[32,512]{1,0:T(8,128)S(1)} %get-tuple-element.40, f32[32,512]{1,0:T(8,128)S(1)} %get-tuple-element.39, f32[512]{0:T(512)} %param.12, f32[32,512]{1,0:T(8,128)S(1)} %add_rsqrt_fusion, f32[32,75]{1,0:T(8,128)S(1)} %fusion.58, ...), kind=kOutput, calls=%fused_computation.16 | convolution fusion | flops 158611200 | bytes 10172672 | tf_op jit(solution)/shard_map/dot_general | solution.py:153
  131.6 4.4 %concatenate.32.src_ref = f32[32,16,1548]{2,1,0:T(8,128)} concatenate(f32[32,16,1536]{2,1,0:T(8,128)} %bitcast.83, f32[32,16,10]{2,1,0:T(8,128)} %bitcast.88, f32[32,16,1]{2,1,0:T(8,128)S(1)} %concatenate.36, f32[32,16,1]{2,1,0:T(8,128)S(1)} %concatenate.37), dimensions={2} | concatenate | bytes 6340608 | tf_op jit(solution)/shard_map/concatenate | solution.py:185
  136.0 79.7 %shard_map.119 = f32[32,16,1548]{2,1,0:T(8,128)} custom-call(f32[32,16,1548]{2,1,0:T(8,128)} %concatenate.32.src_ref), custom_call_target="tpu_custom_call" | custom-call | tf_op jit(solution)/shard_map/pallas_call | solution.py:69
  215.7 2.1 reduce_sum.78
  217.8 0.1 reshape.281
  217.9 18.6 %all_to_all.19 = f32[16,1,1548]{2,1,0:T(1,128)S(1)} all-to-all(f32[16,1,1548]{2,1,0:T(1,128)S(1)} %reshape.281), channel_id=1, replica_groups=mesh['grp'=16,'dev'=32] {'grp'}, dimensions={0} | all-to-all | bytes 198144 | tf_op jit(solution)/shard_map/all_to_all | solution.py:191
  236.5 0.1 reduce_sum.79
  236.5 0.7 broadcast_in_dim.19
  237.2 3.4 %all-to-all-start.2 = ((f32[16,1,1548]{2,1,0:T(1,128)}), f32[16,1,1548]{2,1,0:T(1,128)S(1)}, u32[]{:S(2)}, u32[]{:S(2)}) async-start(f32[16,1,1548]{2,1,0:T(1,128)} %broadcast_in_dim.19), calls=%async_computation.2 | async-start | bytes 212992 | tf_op jit(solution)/shard_map/all_to_all | solution.py:196
  240.7 1.4 copy.78
  242.1 7.0 %all-to-all-done.2 = f32[16,1,1548]{2,1,0:T(1,128)S(1)} async-done(((f32[16,1,1548]{2,1,0:T(1,128)}), f32[16,1,1548]{2,1,0:T(1,128)S(1)}, u32[]{:S(2)}, u32[]{:S(2)}) %all-to-all-start.2) | async-done | bytes 99104 | tf_op jit(solution)/shard_map/all_to_all | solution.py:196
  249.1 0.7 slice_reduce_fusion
  249.8 0.7 copy.80
  250.5 0.1 reshape.283
  250.5 0.7 copy.79
  (36 shorter events, 0.2 us)
Async XLA Ops:
  0.6 83.3 %copy-start = (bf16[3,512,512]{2,1,0:T(8,128)(2,1)S(1)}, bf16[3,512,512]{2,1,0:T(8,128)(2,1)}, u32[]{:S(2)}) copy-start(bf16[3,512,512]{2,1,0:T(8,128)(2,1)} %param.14) | copy-start | bytes 4718596
  3.2 8.1 %copy-start.2 = (bf16[32,384]{1,0:T(8,128)(2,1)S(1)}, bf16[32,384]{1,0:T(8,128)(2,1)}, u32[]{:S(2)}) copy-start(bf16[32,384]{1,0:T(8,128)(2,1)} %param.8) | copy-start | bytes 73732
  3.2 33.9 %copy-start.8 = (bf16[10,512]{1,0:T(8,128)(2,1)S(1)}, bf16[10,512]{1,0:T(8,128)(2,1)}, u32[]{:S(2)}) copy-start(bf16[10,512]{1,0:T(8,128)(2,1)} %param.11) | copy-start | bytes 30724
  13.9 22.5 %all-to-all-start = ((bf16[32,2,192]{2,1,0:T(2,128)(2,1)}), bf16[32,2,192]{2,1,0:T(2,128)(2,1)S(1)}, u32[]{:S(2)}, u32[]{:S(2)}) async-start(bf16[32,2,192]{2,1,0:T(2,128)(2,1)} %reshape.311), calls=%async_computation | async-start | bytes 65536 | tf_op jit(solution)/shard_map/all_to_all | solution.py:173
  27.7 11.6 %copy-start.11 = (f32[32]{0:T(128)}, f32[32]{0:T(128)S(1)}, u32[]{:S(2)}) copy-start(f32[32]{0:T(128)S(1)} %fusion.62) | copy-start | bytes 388
  36.9 2.4 copy-start.6
  37.1 2.2 copy-start.7
  37.1 3.3 %copy-start.9 = (f32[512]{0:T(512)S(1)}, f32[512]{0:T(512)}, u32[]{:S(2)}) copy-start(f32[512]{0:T(512)} %param.13) | copy-start | bytes 6148
  37.1 3.3 %copy-start.10 = (f32[512]{0:T(512)S(1)}, f32[512]{0:T(512)}, u32[]{:S(2)}) copy-start(f32[512]{0:T(512)} %param.12) | copy-start | bytes 6148
  38.1 2.3 copy-start.1
  84.0 11.5 %copy-start.3 = (bf16[32,37,512]{2,1,0:T(8,128)(2,1)S(1)}, bf16[32,37,512]{2,1,0:T(8,128)(2,1)}, u32[]{:S(2)}) copy-start(bf16[32,37,512]{2,1,0:T(8,128)(2,1)} %slice.47) | copy-start | bytes 3637252
  84.0 11.5 %copy-start.4 = (bf16[32,37,512]{2,1,0:T(8,128)(2,1)S(1)}, bf16[32,37,512]{2,1,0:T(8,128)(2,1)}, u32[]{:S(2)}) copy-start(bf16[32,37,512]{2,1,0:T(8,128)(2,1)} %slice.46) | copy-start | bytes 3637252
  84.0 11.6 %copy-start.5 = (bf16[32,37,512]{2,1,0:T(8,128)(2,1)S(1)}, bf16[32,37,512]{2,1,0:T(8,128)(2,1)}, u32[]{:S(2)}) copy-start(bf16[32,37,512]{2,1,0:T(8,128)(2,1)} %slice.45) | copy-start | bytes 3637252
  106.4 2.9 %slice-start = ((s8[5242880]{0:T(1024)(128)(4,1)}), s8[4194304]{0:T(1024)(128)(4,1)S(1)}, s32[]{:S(2)}) async-start(s8[5242880]{0:T(1024)(128)(4,1)} %bitcast.80), calls=%async_computation.3 | async-start | bytes 8388608
  106.5 2.9 %slice-start.1 = ((s8[5242880]{0:T(1024)(128)(4,1)}), s8[1048576]{0:T(1024)(128)(4,1)S(1)}, s32[]{:S(2)}) async-start(s8[5242880]{0:T(1024)(128)(4,1)} %bitcast.80), calls=%async_computation.4 | async-start | bytes 2097152
  237.2 11.8 %all-to-all-start.2 = ((f32[16,1,1548]{2,1,0:T(1,128)}), f32[16,1,1548]{2,1,0:T(1,128)S(1)}, u32[]{:S(2)}, u32[]{:S(2)}) async-start(f32[16,1,1548]{2,1,0:T(1,128)} %broadcast_in_dim.19), calls=%async_computation.2 | async-start | bytes 212992 | tf_op jit(solution)/shard_map/all_to_all | solution.py:196

commit v4 on v3

--- a/solution.py
+++ b/solution.py
@@ -10,29 +10,36 @@
 MESH = pl.DeviceIdType.MESH
 
 
-def exchange_kernel(members, src_ref, dst_ref, send_sems, recv_sems, local_sem):
-    me = lax.axis_index("dev")
-    grp = lax.axis_index("grp")
+def exchange_kernel(members, axis, gather, src_ref, dst_ref, send_sems, recv_sems, local_sem):
+    me = lax.axis_index(axis)
+    other = lax.axis_index("dev" if axis == "grp" else "grp")
+
+    def where(peer):
+        return (peer, other) if axis == "grp" else (other, peer)
+
+    def source(peer):
+        return src_ref.at[0] if gather else src_ref.at[peer]
+
     barrier = pltpu.get_barrier_semaphore()
 
     def greet(step, carry):
         peer = lax.rem(me + step, members)
-        pl.semaphore_signal(barrier, inc=1, device_id=(grp, peer), device_id_type=MESH)
+        pl.semaphore_signal(barrier, inc=1, device_id=where(peer), device_id_type=MESH)
         return carry
 
     lax.fori_loop(1, members, greet, 0)
     pl.semaphore_wait(barrier, members - 1)
-    local = pltpu.make_async_copy(src_ref.at[me], dst_ref.at[me], local_sem)
+    local = pltpu.make_async_copy(source(me), dst_ref.at[me], local_sem)
     local.start()
 
     def send(step, carry):
         peer = lax.rem(me + step, members)
         pltpu.make_async_remote_copy(
-            src_ref=src_ref.at[peer],
+            src_ref=source(peer),
             dst_ref=dst_ref.at[me],
             send_sem=send_sems.at[step],
             recv_sem=recv_sems.at[step],
-            device_id=(grp, peer),
+            device_id=where(peer),
             device_id_type=MESH,
         ).start()
         return carry
@@ -43,19 +50,19 @@
         peer = lax.rem(me + step, members)
         sender = lax.rem(me + members - step, members)
         pltpu.make_async_remote_copy(
-            src_ref=src_ref.at[peer],
+            src_ref=source(peer),
             dst_ref=dst_ref.at[me],
             send_sem=send_sems.at[step],
             recv_sem=recv_sems.at[step],
-            device_id=(grp, peer),
+            device_id=where(peer),
             device_id_type=MESH,
         ).wait_send()
         pltpu.make_async_remote_copy(
-            src_ref=src_ref.at[me],
+            src_ref=source(me),
             dst_ref=dst_ref.at[sender],
             send_sem=send_sems.at[step],
             recv_sem=recv_sems.at[step],
-            device_id=(grp, sender),
+            device_id=where(sender),
             device_id_type=MESH,
         ).wait_recv()
         return carry
@@ -64,11 +71,11 @@
     local.wait()
 
 
-def exchange(blocks):
-    members = blocks.shape[0]
+def exchange(blocks, members, axis, gather, ident):
+    shape = (members,) + blocks.shape[1:]
     return pl.pallas_call(
-        functools.partial(exchange_kernel, members),
-        out_shape=jax.ShapeDtypeStruct(blocks.shape, blocks.dtype),
+        functools.partial(exchange_kernel, members, axis, gather),
+        out_shape=jax.ShapeDtypeStruct(shape, blocks.dtype),
         in_specs=[pl.BlockSpec(memory_space=pl.ANY)],
         out_specs=pl.BlockSpec(memory_space=pl.ANY),
         scratch_shapes=[
@@ -76,7 +83,7 @@
             pltpu.SemaphoreType.DMA((members,)),
             pltpu.SemaphoreType.DMA,
         ],
-        compiler_params=pltpu.CompilerParams(collective_id=0, has_side_effects=True),
+        compiler_params=pltpu.CompilerParams(collective_id=ident, has_side_effects=True),
     )(blocks)
 
 
@@ -185,16 +192,17 @@
     full = jnp.concatenate([grad_kernel, small], axis=1)
     chans, span = full.shape
     width = chans // members
-    pieces = exchange(full.reshape(members, width, span))
+    halves = full.reshape(members, 2, width // 2, span)
+    core = lax.rem(lax.axis_index("grp"), 2)
+    keep = lax.dynamic_index_in_dim(halves, core, 1, keepdims=False)
+    give = lax.dynamic_index_in_dim(halves, 1 - core, 1, keepdims=False)
+    pairs = [(g, g ^ 1) for g in range(groups)]
+    mine = keep + lax.ppermute(give, "grp", pairs)
+    pieces = exchange(mine, members, "dev", False, 0)
     part = jnp.sum(pieces, axis=0)
-    sub = width // groups
-    mine = lax.all_to_all(
-        part.reshape(groups, sub, span), "grp", split_axis=0, concat_axis=0, tiled=True
-    )
-    mine = jnp.sum(mine, axis=0)
-    spread = jnp.broadcast_to(mine[None], (groups, sub, span))
-    owned = lax.all_to_all(spread, "grp", split_axis=0, concat_axis=0, tiled=True)
-    owned = owned.reshape(width, span)
+    gathered = exchange(part[None], groups, "grp", True, 1)
+    gathered = gathered.reshape(groups // 2, 2, width // 2, span)
+    owned = jnp.sum(gathered, axis=0).reshape(width, span)
     grad_second = (
         owned[:, : taps_second * in_chans].reshape(width, taps_second, in_chans).transpose(1, 2, 0)
     )

time: 252 us -> 217 us (0.86)
  blocking collectives: 18.6 us -> 0 us
  matrix products: 31.6 us -> 21.1 us
  Pallas kernels: 79.7 us -> 72.4 us
  waiting for transfers between devices: 15.6 us -> 9.29 us
  local copies, waits for them, and re-layouts: 58 us -> 62.6 us
    all_to_all x1 -> x0, blocking collectives: 18.6 us -> none  [shards(): lax.all_to_all(part.reshape(groups, sub, span), 'grp', split_axis=0, conc...]
    dot_general x1, matrix products: 13 us -> 3.74 us  [local_pass(): lax.dot_general(dpre0.reshape(rows * frames0, chans), patches.astype(jnp....]
    pallas_call x1 -> x2, Pallas kernels: 79.7 us -> 72.4 us  [exchange(): pl.pallas_call(functools.partial(exchange_kernel, members, axis, gather),...]
    all_to_all x1 -> x0, waiting for transfers between devices: 7.01 us -> none  [shards(): lax.all_to_all(spread, 'grp', split_axis=0, concat_axis=0, tiled=True)]
    ppermute x0 -> x1, starting transfers between devices: none -> 4 us  [shards(): mine = keep + lax.ppermute(give, 'grp', pairs)]
    all_to_all x1 -> x0, starting transfers between devices: 3.4 us -> none  [shards(): lax.all_to_all(spread, 'grp', split_axis=0, concat_axis=0, tiled=True)]
    concatenate x3 -> x8, local copies, waits for them, and re-layouts: 5.44 us -> 8.39 us  [shards(): full = jnp.concatenate([grad_kernel, small], axis=1)]
    add x0 -> x1, other arithmetic: none -> 2.84 us  [shards(): mine = keep + lax.ppermute(give, 'grp', pairs)]
where the time goes in v4:
time: 217 us; the launch traced here: 216 us
  Pallas kernels  72.4 us (33%)
  local copies, waits for them, and re-layouts  62.6 us (29%)
  other arithmetic  31.5 us (15%)
  matrix products  21.1 us (10%)
  starting transfers between devices  17.7 us (8%)
  waiting for transfers between devices  9.29 us (4%)
    pallas_call x2, Pallas kernels, exchange(): pl.pallas_call(functools.partial(exchange_kernel, members, axis, gather),...  72.4 us
    convert_element_type x1, other arithmetic, local_pass(): act0 = (jax.nn.gelu(lifted, approximate=False) * mask0).astype(jnp.bfloat16)  14.2 us
    all_to_all x1, starting transfers between devices, shards(): lax.all_to_all(outgoing, 'dev', split_axis=0, concat_axis=0, tiled=True)  13.7 us
    dot_general x1, matrix products, local_pass(): jnp.dot(taps, kernel, preferred_element_type=jnp.float32)  11.9 us
    slice x1, local copies, waits for them, and re-layouts, local_pass(): act0[:, 0:span:2]  9.79 us
    slice x1, local copies, waits for them, and re-layouts, local_pass(): act0[:, 1:span:2]  9.77 us
    all_to_all x1, waiting for transfers between devices, shards(): lax.all_to_all(outgoing, 'dev', split_axis=0, concat_axis=0, tiled=True)  8.6 us
    concatenate x8, local copies, waits for them, and re-layouts, shards(): full = jnp.concatenate([grad_kernel, small], axis=1)  8.39 us
  transfers between devices with their start and end apart: 2, of which 2 were waited for; matrix products, arithmetic and copies ran while one was open for 1% of the time, Pallas kernels for 0%

profile of v4, /device:TPU:1, one launch (start us, length us, event | category | flops | bytes accessed | tf_op | source)
XLA Modules:
  0.0 215.6 jit_solution(9984227955755264756)
XLA Ops:
  0.6 0.9 copy.89
  1.6 0.8 reshape.272
  2.3 0.1 copy.92
  2.4 0.1 reshape.287
  2.5 7.1 %gather_fusion.1 = s32[1024]{0:T(1024)S(1)} fusion(s32[32,32]{1,0:T(8,128)S(1)} %reshape.272, s32[1024]{0:T(1024)S(1)} %reshape.287), kind=kCustom, calls=%fused_computation.1 | custom fusion | bytes 16384 | tf_op jit(solution)/shard_map/jit(take_along_axis)/gather | solution.py:181
  9.6 0.7 compare_and_fusion.1
  10.3 0.1 constant_dynamic-slice_fusion.1
  10.4 0.1 copy.112
  10.5 0.7 fusion.64
  11.3 0.6 gather_fusion
  11.9 0.1 bitcast_select_fusion
  12.0 0.5 broadcast.274
  12.5 0.7 reduce.4
  13.1 0.7 reshape.306
  13.9 13.7 %all-to-all-start = ((bf16[32,2,192]{2,1,0:T(2,128)(2,1)}), bf16[32,2,192]{2,1,0:T(2,128)(2,1)S(1)}, u32[]{:S(2)}, u32[]{:S(2)}) async-start(bf16[32,2,192]{2,1,0:T(2,128)(2,1)} %reshape.306), calls=%async_computation | async-start | bytes 65536 | tf_op jit(solution)/shard_map/all_to_all | solution.py:180
  27.6 0.1 fusion.62
  27.6 0.1 fusion.61
  27.7 8.6 %all-to-all-done = bf16[32,2,192]{2,1,0:T(2,128)(2,1)S(1)} async-done(((bf16[32,2,192]{2,1,0:T(2,128)(2,1)}), bf16[32,2,192]{2,1,0:T(2,128)(2,1)S(1)}, u32[]{:S(2)}, u32[]{:S(2)}) %all-to-all-start) | async-done | bytes 24608 | tf_op jit(solution)/shard_map/all_to_all | solution.py:180
  36.3 0.1 reshape.307
  36.5 0.1 copy.86
  36.7 0.2 copy.109
  36.9 0.2 copy.108
  37.1 0.9 multiply_reduce_fusion.3
  38.0 0.1 broadcast_divide_fusion.2
  38.1 1.1 multiply_reduce_fusion.2
  39.3 0.1 add_rsqrt_fusion
  39.4 1.0 copy-done.1
  40.3 14.2 %fusion.3 = bf16[32,75,512]{2,1,0:T(8,128)(2,1)} fusion(f32[512]{0:T(512)S(1)} %copy-done.6, f32[512]{0:T(512)S(1)} %copy-done.7, f32[32,75]{1,0:T(8,128)S(1)} %fusion.61, f32[32,512]{1,0:T(8,128)S(1)} %add_rsqrt_fusion, f32[32,75,512]{2,1,0:T(8,128)S(1)} %get-tuple-element.47, f32[32,512]{1,0:T(8,128)S(1)} %broadcast_divide_fusion.2), kind=kLoop, calls=%fused_computation.7 | loop fusion | flops 87244800 | bytes 7517568 | tf_op jit(solution)/shard_map/convert_element_type | solution.py:123
  54.5 8.2 %slice.47 = bf16[32,37,512]{2,1,0:T(8,128)(2,1)S(1)} slice(bf16[32,75,512]{2,1,0:T(8,128)(2,1)} %fusion.3), slice={[0:32:1], [2:75:2], [0:512:1]} | slice | bytes 2424832 | tf_op jit(solution)/shard_map/slice | solution.py:126
  62.8 9.8 %slice.46 = bf16[32,37,512]{2,1,0:T(8,128)(2,1)} slice(bf16[32,75,512]{2,1,0:T(8,128)(2,1)} %fusion.3), slice={[0:32:1], [1:74:2], [0:512:1]} | slice | bytes 2424832 | tf_op jit(solution)/shard_map/slice | solution.py:126
  72.5 9.8 %slice.45 = bf16[32,37,512]{2,1,0:T(8,128)(2,1)} slice(bf16[32,75,512]{2,1,0:T(8,128)(2,1)} %fusion.3), slice={[0:32:1], [0:74:2], [0:512:1]} | slice | bytes 2424832 | tf_op jit(solution)/shard_map/slice | solution.py:126
  82.3 11.9 %fusion.35 = (bf16[32,37,512]{2,1,0:T(8,128)(2,1)S(1)}, bf16[32,37,512]{2,1,0:T(8,128)(2,1)}) fusion(bf16[32,37,512]{2,0,1:T(8,128)(2,1)} %param.15, f32[32,37]{1,0:T(8,128)S(1)} %fusion.62, bf16[1536,512,1]{1,0,2:T(8,128)(2,1)S(1)} %bitcast.84, bf16[32,37,512]{2,1,0:T(8,128)(2,1)S(1)} %slice.47, bf16[32,37,512]{2,1,0:T(8,128)(2,1)} %slice.46, ...), kind=kOutput, calls=%fused_computation.58 | convolution fusion | flops 1920466944 | bytes 8852096 | tf_op jit(solution)/shard_map/dot_general | solution.py:130
  94.3 2.2 %fusion.50 = f32[512,1536,1]{1,0,2:T(8,128)S(1)} fusion(bf16[32,37,512]{2,1,0:T(8,128)(2,1)S(1)} %get-tuple-element.40, bf16[32,37,512]{2,1,0:T(8,128)(2,1)S(1)} %slice.47, bf16[32,37,512]{2,1,0:T(8,128)(2,1)S(1)} %copy-done.3, bf16[32,37,512]{2,1,0:T(8,128)(2,1)S(1)} %copy-done.4), kind=kOutput, calls=%fused_computation.85 | convolution fusion | flops 1873182720 | bytes 7995392 | tf_op jit(solution)/shard_map/dot_general | solution.py:141
  96.5 2.2 %fusion.52 = f32[32,37,3,512]{3,1,2,0:T(8,128)S(1)} fusion(bf16[3,512,512]{2,1,0:T(8,128)(2,1)S(1)} %copy-done, bf16[32,37,512]{2,1,0:T(8,128)(2,1)S(1)} %get-tuple-element.40), kind=kOutput, calls=%fused_computation.87 | convolution fusion | flops 1862270976 | bytes 10059776 | tf_op jit(solution)/shard_map/dot_general | solution.py:144
  98.8 0.2 slice.65
  99.1 0.2 slice_bitcast_fusion
  99.3 2.0 copy.99
  101.3 0.6 fusion.37
  101.9 0.8 pad_maximum_fusion
  102.7 2.8 %copy.97 = f32[32,37,2,512]{3,0,2,1:T(8,128)S(1)} copy(f32[32,37,2,512]{3,1,2,0:T(8,128)S(1)} %pad_maximum_fusion) | data formatting | bytes 9699328 | tf_op jit(solution)/shard_map/stack | solution.py:151
  105.6 2.8 %copy.98 = f32[32,74,512]{2,1,0:T(8,128)S(1)} copy(f32[32,74,512]{2,0,1:T(8,128)S(1)} %bitcast.87) | data formatting | bytes 9699328 | tf_op jit(solution)/shard_map/reshape | solution.py:151
  108.4 5.9 %multiply_reduce_fusion = (f32[512]{0:T(512)S(1)}, f32[32,512]{1,0:T(8,128)S(1)}, f32[32,512]{1,0:T(8,128)S(1)}, f32[512]{0:T(512)S(1)}, f32[32,75,512]{2,1,0:T(8,128)S(1)}) fusion(f32[32,512]{1,0:T(8,128)S(1)} %add_rsqrt_fusion, f32[32,75]{1,0:T(8,128)S(1)} %fusion.61, f32[32,75,512]{2,1,0:T(8,128)S(1)} %bitcast.86, ...), kind=kLoop, calls=%fused_computation.15 | loop fusion | flops 28228608 | bytes 15025536 | tf_op jit(solution)/shard_map/reduce_sum | solution.py:154
  114.3 0.1 broadcast_divide_fusion.1
  114.4 3.7 %fusion.56 = f32[512,10]{0,1:T(8,128)S(1)} fusion(f32[32,75,512]{2,1,0:T(8,128)S(1)} %get-tuple-element.36, f32[32,512]{1,0:T(8,128)S(1)} %get-tuple-element.45, f32[32,512]{1,0:T(8,128)S(1)} %get-tuple-element.44, f32[512]{0:T(512)S(1)} %copy-done.7, f32[32,512]{1,0:T(8,128)S(1)} %add_rsqrt_fusion, f32[32,75]{1,0:T(8,128)S(1)} %fusion.61, ...), kind=kOutput, calls=%fused_computation.90 | convolution fusion | flops 158611200 | bytes 10172672 | tf_op jit(solution)/shard_map/dot_general | solution.py:160
  118.1 0.5 concatenate.29
  118.7 0.5 copy.100
  119.1 0.1 concatenate.30
  119.2 0.4 copy.101
  119.7 0.1 concatenate.31
  119.8 0.4 copy.102
  120.3 4.3 %concatenate.32 = f32[32,2,8,1548]{3,2,0,1:T(8,128)} concatenate(f32[32,2,8,1536]{3,2,0,1:T(8,128)} %copy.99, f32[32,2,8,10]{3,2,0,1:T(8,128)S(1)} %copy.100, f32[32,2,8,1]{3,2,0,1:T(8,128)S(1)} %copy.101, f32[32,2,8,1]{3,2,0,1:T(8,128)S(1)} %copy.102), dimensions={3} | concatenate | bytes 6340608 | tf_op jit(solution)/shard_map/concatenate | solution.py:192
  124.6 2.8 %dynamic-slice_bitcast_fusion = f32[32,8,1548]{2,1,0:T(8,128)} fusion(f32[32,2,8,1548]{3,2,0,1:T(8,128)} %concatenate.32, s32[]{:T(128)S(6)} %select_n.74), kind=kLoop, calls=%fused_computation.84 | loop fusion | bytes 3170308 | tf_op jit(solution)/shard_map/jit(dynamic_index_in_dim)/squeeze | solution.py:198
  127.4 4.0 %collective-permute-start = (f32[32,8,1548]{2,1,0:T(8,128)}, f32[32,8,1548]{2,1,0:T(8,128)S(1)}, u32[]{:S(2)}, u32[]{:S(2)}) collective-permute-start(f32[32,8,1548]{2,1,0:T(8,128)} %dynamic-slice_bitcast_fusion), channel_id=1, source_target_pairs={{0,32},{32,0},{64,96},{96,64},{128,160},{160,128},{192,224},{224,1... | collective-permute-start | bytes 4755464 | tf_op jit(solution)/shard_map/ppermute | solution.py:200
  131.4 2.7 %copy.103 = bf16[32,37,512]{2,0,1:T(8,128)(2,1)} copy(bf16[32,37,512]{2,1,0:T(8,128)(2,1)} %get-tuple-element.41) | data formatting | bytes 2424832
  134.1 0.7 collective-permute-done
  134.8 2.8 %bitcast_add_fusion.src_ref = f32[32,8,1548]{2,1,0:T(8,128)} fusion(f32[32,8,1548]{2,1,0:T(8,128)S(1)} %collective-permute-done, f32[32,2,8,1548]{3,2,0,1:T(8,128)} %concatenate.32, s32[]{:T(128)S(6)} %select_n.73), kind=kLoop, calls=%fused_computation.83 | loop fusion | flops 396288 | bytes 4755460 | tf_op jit(solution)/shard_map/add | solution.py:200
  137.6 43.5 %shard_map.119 = f32[32,8,1548]{2,1,0:T(8,128)} custom-call(f32[32,8,1548]{2,1,0:T(8,128)} %bitcast_add_fusion.src_ref), custom_call_target="tpu_custom_call" | custom-call | tf_op jit(solution)/shard_map/pallas_call | solution.py:76
  181.1 2.2 %reduce_sum.78 = f32[8,1548]{1,0:T(8,128)} reduce(f32[32,8,1548]{2,1,0:T(8,128)} %shard_map.119, f32[]{:T(128)} %constant.58.clone.1), dimensions={0}, to_apply=%region_6.7 | reduce | flops 383904 | bytes 1634692 | tf_op jit(solution)/shard_map/reduce_sum | solution.py:202
  183.3 29.0 %shard_map.120 = f32[16,8,1548]{2,1,0:T(8,128)} custom-call(f32[1,8,1548]{2,1,0:T(8,128)} %bitcast.94), custom_call_target="tpu_custom_call" | custom-call | tf_op jit(solution)/shard_map/pallas_call | solution.py:76
  212.3 1.2 reduce_sum.79
  213.5 0.7 slice_reduce_fusion
  214.2 0.1 reshape.278
  214.3 0.7 copy.104
  215.0 0.7 copy.105
  (32 shorter events, 0.3 us)
Async XLA Ops:
  0.6 81.7 %copy-start = (bf16[3,512,512]{2,1,0:T(8,128)(2,1)S(1)}, bf16[3,512,512]{2,1,0:T(8,128)(2,1)}, u32[]{:S(2)}) copy-start(bf16[3,512,512]{2,1,0:T(8,128)(2,1)} %param.14) | copy-start | bytes 4718596
  2.5 8.8 %copy-start.2 = (bf16[32,384]{1,0:T(8,128)(2,1)S(1)}, bf16[32,384]{1,0:T(8,128)(2,1)}, u32[]{:S(2)}) copy-start(bf16[32,384]{1,0:T(8,128)(2,1)} %param.8) | copy-start | bytes 73732
  2.5 34.6 %copy-start.5 = (bf16[10,512]{1,0:T(8,128)(2,1)S(1)}, bf16[10,512]{1,0:T(8,128)(2,1)}, u32[]{:S(2)}) copy-start(bf16[10,512]{1,0:T(8,128)(2,1)} %param.11) | copy-start | bytes 30724
  13.9 22.5 %all-to-all-start = ((bf16[32,2,192]{2,1,0:T(2,128)(2,1)}), bf16[32,2,192]{2,1,0:T(2,128)(2,1)S(1)}, u32[]{:S(2)}, u32[]{:S(2)}) async-start(bf16[32,2,192]{2,1,0:T(2,128)(2,1)} %reshape.306), calls=%async_computation | async-start | bytes 65536 | tf_op jit(solution)/shard_map/all_to_all | solution.py:180
  37.1 3.3 %copy-start.6 = (f32[512]{0:T(512)S(1)}, f32[512]{0:T(512)}, u32[]{:S(2)}) copy-start(f32[512]{0:T(512)} %param.13) | copy-start | bytes 6148
  37.1 3.3 %copy-start.7 = (f32[512]{0:T(512)S(1)}, f32[512]{0:T(512)}, u32[]{:S(2)}) copy-start(f32[512]{0:T(512)} %param.12) | copy-start | bytes 6148
  38.0 2.3 %copy-start.1 = (f32[32,75,512]{2,1,0:T(8,128)}, f32[32,75,512]{2,1,0:T(8,128)S(1)}, u32[]{:S(2)}) copy-start(f32[32,75,512]{2,1,0:T(8,128)S(1)} %get-tuple-element.47) | copy-start | bytes 14745604
  82.3 11.9 %copy-start.3 = (bf16[32,37,512]{2,1,0:T(8,128)(2,1)S(1)}, bf16[32,37,512]{2,1,0:T(8,128)(2,1)}, u32[]{:S(2)}) copy-start(bf16[32,37,512]{2,1,0:T(8,128)(2,1)} %slice.46) | copy-start | bytes 3637252
  82.3 11.9 %copy-start.4 = (bf16[32,37,512]{2,1,0:T(8,128)(2,1)S(1)}, bf16[32,37,512]{2,1,0:T(8,128)(2,1)}, u32[]{:S(2)}) copy-start(bf16[32,37,512]{2,1,0:T(8,128)(2,1)} %slice.45) | copy-start | bytes 3637252
  105.5 2.9 %slice-start = ((s8[5242880]{0:T(1024)(128)(4,1)}), s8[4194304]{0:T(1024)(128)(4,1)S(1)}, s32[]{:S(2)}) async-start(s8[5242880]{0:T(1024)(128)(4,1)} %bitcast.85), calls=%async_computation.1 | async-start | bytes 8388608
  105.6 2.9 %slice-start.1 = ((s8[5242880]{0:T(1024)(128)(4,1)}), s8[1048576]{0:T(1024)(128)(4,1)S(1)}, s32[]{:S(2)}) async-start(s8[5242880]{0:T(1024)(128)(4,1)} %bitcast.85), calls=%async_computation.2 | async-start | bytes 2097152
  127.4 7.4 %collective-permute-start = (f32[32,8,1548]{2,1,0:T(8,128)}, f32[32,8,1548]{2,1,0:T(8,128)S(1)}, u32[]{:S(2)}, u32[]{:S(2)}) collective-permute-start(f32[32,8,1548]{2,1,0:T(8,128)} %dynamic-slice_bitcast_fusion), channel_id=1, source_target_pairs={{0,32},{32,0},{64,96},{96,64},{128,160},{160,128},{192,224},{224,1... | collective-permute-start | bytes 4755464 | tf_op jit(solution)/shard_map/ppermute | solution.py:200

commit v5 on v4

--- a/solution.py
+++ b/solution.py
@@ -10,12 +10,18 @@
 MESH = pl.DeviceIdType.MESH
 
 
-def exchange_kernel(members, axis, gather, src_ref, dst_ref, send_sems, recv_sems, local_sem):
-    me = lax.axis_index(axis)
-    other = lax.axis_index("dev" if axis == "grp" else "grp")
+def exchange_kernel(members, axis, stride, gather, src_ref, dst_ref, send_sems, recv_sems, local_sem):
+    if axis == "grp":
+        coord = lax.axis_index("grp")
+        me = coord // stride
+        offset = lax.rem(coord, stride)
+        other = lax.axis_index("dev")
+    else:
+        me = lax.axis_index("dev")
+        other = lax.axis_index("grp")
 
     def where(peer):
-        return (peer, other) if axis == "grp" else (other, peer)
+        return (peer * stride + offset, other) if axis == "grp" else (other, peer)
 
     def source(peer):
         return src_ref.at[0] if gather else src_ref.at[peer]
@@ -71,10 +77,10 @@
     local.wait()
 
 
-def exchange(blocks, members, axis, gather, ident):
+def exchange(blocks, members, axis, stride, gather, ident):
     shape = (members,) + blocks.shape[1:]
     return pl.pallas_call(
-        functools.partial(exchange_kernel, members, axis, gather),
+        functools.partial(exchange_kernel, members, axis, stride, gather),
         out_shape=jax.ShapeDtypeStruct(shape, blocks.dtype),
         in_specs=[pl.BlockSpec(memory_space=pl.ANY)],
         out_specs=pl.BlockSpec(memory_space=pl.ANY),
@@ -102,68 +108,76 @@
     taps_second = w_second.shape[0]
     frames0 = (samp - ker_first) // stride_first + 1
     frames1 = (frames0 - taps_second) // 2 + 1
-    blocks = wave[:, : stride_first * (frames0 + 1)].reshape(rows, frames0 + 1, stride_first)
-    patches = jnp.concatenate([blocks[:, :-1], blocks[:, 1:]], axis=2).reshape(
-        rows * frames0, ker_first
-    )
-    pre0 = jnp.dot(patches, w_first, preferred_element_type=jnp.float32).reshape(
-        rows, frames0, chans
-    )
+    pairs = (frames0 + 1) // 2
+    hop = 2 * stride_first
+    reach = hop + stride_first
+    padded = jnp.pad(wave, ((0, 0), (0, hop * (pairs + 1) - samp)))
+    blocks = padded.reshape(rows, pairs + 1, hop)
+    patches = jnp.concatenate([blocks[:, :-1], blocks[:, 1:, :stride_first]], axis=2)
+    zeros_w = jnp.zeros((stride_first, chans), w_first.dtype)
+    w_pair = jnp.concatenate(
+        [
+            jnp.concatenate([w_first, zeros_w], axis=0),
+            jnp.concatenate([zeros_w, w_first], axis=0),
+        ],
+        axis=1,
+    )
+    pre0 = jnp.einsum("rum,mc->ruc", patches, w_pair, preferred_element_type=jnp.float32)
     valid0 = (lens - ker_first) // stride_first + 1
-    mask0 = (jnp.arange(frames0, dtype=jnp.int32)[None, :] < valid0[:, None]).astype(jnp.float32)[
-        :, :, None
-    ]
-    count0 = valid0.astype(jnp.float32)[:, None, None]
-    mean0 = jnp.sum(pre0 * mask0, axis=1, keepdims=True) / count0
-    centred = (pre0 - mean0) * mask0
-    var0 = jnp.sum(centred * centred, axis=1, keepdims=True) / count0
-    inv_std = lax.rsqrt(var0 + 1e-05)
+    frame = (
+        2 * jnp.arange(pairs, dtype=jnp.int32)[:, None]
+        + (jnp.arange(2 * chans, dtype=jnp.int32) // chans)[None, :]
+    )
+    mask0 = (frame[None] < valid0[:, None, None]).astype(jnp.float32)
+    count0 = valid0.astype(jnp.float32)[:, None]
+
+    def fold(x):
+        s = jnp.sum(x, axis=1)
+        return s[:, :chans] + s[:, chans:]
+
+    def spread(x):
+        return jnp.concatenate([x, x], axis=1)[:, None, :]
+
+    mean0 = fold(pre0 * mask0) / count0
+    centred = (pre0 - spread(mean0)) * mask0
+    var0 = fold(centred * centred) / count0
+    inv_std = spread(lax.rsqrt(var0 + 1e-05))
     normed = centred * inv_std
-    lifted = normed * norm_gain + norm_bias
+    gain2 = jnp.concatenate([norm_gain, norm_gain])
+    bias2 = jnp.concatenate([norm_bias, norm_bias])
+    lifted = normed * gain2 + bias2
     act0 = (jax.nn.gelu(lifted, approximate=False) * mask0).astype(jnp.bfloat16)
-    span = 2 * frames1
-    taps = jnp.concatenate(
-        [act0[:, 0:span:2], act0[:, 1:span:2], act0[:, 2 : span + 1 : 2]], axis=2
-    )
-    taps = taps.reshape(rows * frames1, taps_second * chans)
+    taps = jnp.concatenate([act0[:, :frames1], act0[:, 1 : frames1 + 1, :chans]], axis=2)
     kernel = w_second.reshape(taps_second * chans, chans)
-    pre1 = jnp.dot(taps, kernel, preferred_element_type=jnp.float32).reshape(rows, frames1, chans)
+    pre1 = jnp.einsum("rui,io->ruo", taps, kernel, preferred_element_type=jnp.float32)
     valid1 = (valid0 - taps_second) // 2 + 1
     mask1 = (jnp.arange(frames1, dtype=jnp.int32)[None, :] < valid1[:, None]).astype(jnp.float32)[
         :, :, None
     ]
     features = (jax.nn.gelu(pre1, approximate=False) * mask1).astype(jnp.bfloat16)
-    grad1 = (
-        (cot.astype(jnp.float32) * gelu_slope(pre1) * mask1)
-        .astype(jnp.bfloat16)
-        .reshape(rows * frames1, chans)
-    )
-    grad_kernel = lax.dot_general(
-        grad1, taps, (((0,), (0,)), ((), ())), preferred_element_type=jnp.float32
-    )
-    back = lax.dot_general(
-        grad1, kernel, (((1,), (1,)), ((), ())), preferred_element_type=jnp.float32
-    )
-    back = back.reshape(rows, frames1, taps_second, chans)
-    zero_row = jnp.zeros((rows, 1, chans), jnp.float32)
-    even = back[:, :, 0] + jnp.concatenate([zero_row, back[:, :-1, 2]], axis=1)
-    odd = back[:, :, 1]
-    pieces = [jnp.stack([even, odd], axis=2).reshape(rows, span, chans), back[:, -1:, 2]]
-    dact0 = jnp.concatenate(pieces, axis=1)
+    grad1 = (cot.astype(jnp.float32) * gelu_slope(pre1) * mask1).astype(jnp.bfloat16)
+    grad_kernel = jnp.einsum("ruo,rui->oi", grad1, taps, preferred_element_type=jnp.float32)
+    back = jnp.einsum("ruo,io->rui", grad1, kernel, preferred_element_type=jnp.float32)
+    dact0 = jnp.pad(back[:, :, : 2 * chans], ((0, 0), (0, pairs - frames1), (0, 0))) + jnp.pad(
+        back[:, :, 2 * chans :], ((0, 0), (1, pairs - frames1 - 1), (0, chans))
+    )
     dlift = dact0 * gelu_slope(lifted) * mask0
-    grad_gain = jnp.sum(dlift * normed, axis=(0, 1))
-    grad_bias = jnp.sum(dlift, axis=(0, 1))
-    dnorm = dlift * norm_gain
-    first_mean = jnp.sum(dnorm, axis=1, keepdims=True) / count0
-    second_mean = jnp.sum(dnorm * normed, axis=1, keepdims=True) / count0
+    gain_terms = jnp.sum(dlift * normed, axis=(0, 1))
+    bias_terms = jnp.sum(dlift, axis=(0, 1))
+    grad_gain = gain_terms[:chans] + gain_terms[chans:]
+    grad_bias = bias_terms[:chans] + bias_terms[chans:]
+    dnorm = dlift * gain2
+    first_mean = spread(fold(dnorm) / count0)
+    second_mean = spread(fold(dnorm * normed) / count0)
     dpre0 = inv_std * (dnorm - first_mean - normed * second_mean) * mask0
-    grad_filter = lax.dot_general(
-        dpre0.reshape(rows * frames0, chans),
+    grad_pair = jnp.einsum(
+        "ruj,rum->jm",
+        dpre0,
         patches.astype(jnp.float32),
-        (((0,), (0,)), ((), ())),
         precision=lax.Precision.HIGHEST,
         preferred_element_type=jnp.float32,
     )
+    grad_filter = grad_pair[:chans, :ker_first] + grad_pair[chans:, stride_first:]
     small = jnp.concatenate([grad_filter, grad_gain[:, None], grad_bias[:, None]], axis=1)
     grads = (grad_kernel, small)
     return (features, grads)
@@ -198,11 +212,14 @@
     give = lax.dynamic_index_in_dim(halves, 1 - core, 1, keepdims=False)
     pairs = [(g, g ^ 1) for g in range(groups)]
     mine = keep + lax.ppermute(give, "grp", pairs)
-    pieces = exchange(mine, members, "dev", False, 0)
+    pieces = exchange(mine, members, "dev", 1, False, 0)
     part = jnp.sum(pieces, axis=0)
-    gathered = exchange(part[None], groups, "grp", True, 1)
-    gathered = gathered.reshape(groups // 2, 2, width // 2, span)
-    owned = jnp.sum(gathered, axis=0).reshape(width, span)
+    rows_y = groups // 2
+    scattered = exchange(part.reshape(rows_y, (width // 2) // rows_y, span), rows_y, "grp", 2, False, 1)
+    total = jnp.sum(scattered, axis=0)
+    gathered = exchange(total[None], groups, "grp", 1, True, 2)
+    gathered = gathered.reshape(rows_y, 2, (width // 2) // rows_y, span)
+    owned = gathered.transpose(1, 0, 2, 3).reshape(width, span)
     grad_second = (
         owned[:, : taps_second * in_chans].reshape(width, taps_second, in_chans).transpose(1, 2, 0)
     )

time: 217 us -> 173 us (0.80)
  local copies, waits for them, and re-layouts: 62.6 us -> 35.1 us
  waiting for transfers between devices: 9.29 us -> 0.69 us
  Pallas kernels: 72.4 us -> 68.3 us
    slice x5, local copies, waits for them, and re-layouts: 28.2 us -> 2.24 us  [the longest x2 0.89 us: local_pass(): back[:, :, 2 * chans:]]
    all_to_all x1, waiting for transfers between devices: 8.6 us -> 0.01 us  [shards(): lax.all_to_all(outgoing, 'dev', split_axis=0, concat_axis=0, tiled=True)]
    pallas_call x2 -> x3, Pallas kernels: 72.4 us -> 68.3 us  [exchange(): pl.pallas_call(functools.partial(exchange_kernel, members, axis, stride,...]
    another operation x2 -> x0, local copies, waits for them, and re-layouts: 2.88 us -> none  [the longest x1 2.81 us: local_pass(): jnp.stack([even, odd], axis=2).reshape(rows, span, chans)]
    concatenate x8 -> x4, local copies, waits for them, and re-layouts: 8.39 us -> 7.3 us  [shards(): full = jnp.concatenate([grad_kernel, small], axis=1)]
    unnamed x30 -> x20, local copies, waits for them, and re-layouts: 7.25 us -> 7.88 us
    gather x4 -> x3, local copies, waits for them, and re-layouts: 7.28 us -> 7.2 us  [shards(): jnp.take_along_axis(lengths.reshape(members, rows), order, axis=1)]
  transfers between devices with their start and end apart: 2 -> 2, of which waited for: 2 -> 1; matrix products, arithmetic and copies ran while one was open for 1% -> 7% of each run, Pallas kernels for 0% -> 0%
where the time goes in v5:
time: 173 us; the launch traced here: 172 us
  Pallas kernels  68.3 us (39%)
  local copies, waits for them, and re-layouts  35.1 us (20%)
  other arithmetic  29.4 us (17%)
  matrix products  20.7 us (12%)
  starting transfers between devices  16.6 us (10%)
    pallas_call x3, Pallas kernels, exchange(): pl.pallas_call(functools.partial(exchange_kernel, members, axis, stride,...  68.3 us
    all_to_all x1, starting transfers between devices, shards(): lax.all_to_all(outgoing, 'dev', split_axis=0, concat_axis=0, tiled=True)  13.7 us
    convert_element_type x1, other arithmetic, local_pass(): act0 = (jax.nn.gelu(lifted, approximate=False) * mask0).astype(jnp.bfloat16)  13 us
    dot_general x1, matrix products, local_pass(): jnp.einsum('rui,io->ruo', taps, kernel, preferred_element_type=jnp.float32)  11 us
    unnamed x20, local copies, waits for them, and re-layouts  7.88 us
    concatenate x4, local copies, waits for them, and re-layouts, shards(): full = jnp.concatenate([grad_kernel, small], axis=1)  7.3 us
    gather x3, local copies, waits for them, and re-layouts, shards(): jnp.take_along_axis(lengths.reshape(members, rows), order, axis=1)  7.2 us
    reduce_sum x1, other arithmetic, local_pass(): gain_terms = jnp.sum(dlift * normed, axis=(0, 1))  5.72 us
  transfers between devices with their start and end apart: 2, of which 1 were waited for; matrix products, arithmetic and copies ran while one was open for 7% of the time, Pallas kernels for 0%

profile of v5, /device:TPU:1, one launch (start us, length us, event | category | flops | bytes accessed | tf_op | source)
XLA Modules:
  0.0 171.7 jit_solution(13320896571575688162)
XLA Ops:
  0.7 0.8 fusion.80
  1.5 0.7 compare_and_fusion
  2.2 0.1 copy.68
  2.2 0.1 fusion.70
  2.4 1.4 gather_fusion
  3.7 0.1 bitcast_select_fusion
  3.8 0.5 broadcast.343
  4.3 0.7 reduce.14
  5.0 0.7 reshape.297
  5.7 13.7 %all-to-all-start = ((bf16[32,2,192]{2,1,0:T(2,128)(2,1)}), bf16[32,2,192]{2,1,0:T(2,128)(2,1)S(1)}, u32[]{:S(2)}, u32[]{:S(2)}) async-start(bf16[32,2,192]{2,1,0:T(2,128)(2,1)} %reshape.297), calls=%async_computation | async-start | bytes 65536 | tf_op jit(solution)/shard_map/all_to_all | solution.py:194
  19.4 0.7 bitcast_or_fusion
  20.2 0.7 compare_select_fusion.9
  20.9 0.8 reshape.259
  21.6 0.1 reshape.275
  21.7 7.1 %gather_fusion.1 = s32[1024]{0:T(1024)S(1)} fusion(s32[32,32]{1,0:T(8,128)S(1)} %reshape.259, s32[1024]{0:T(1024)S(1)} %reshape.275), kind=kCustom, calls=%fused_computation.1 | custom fusion | bytes 16384 | tf_op jit(solution)/shard_map/jit(take_along_axis)/gather | solution.py:195
  28.9 0.2 convert_reduce_fusion
  29.1 0.1 fusion.69
  29.2 0.1 fusion.74
  29.3 0.1 reduce.1
  29.4 0.1 broadcast_add_fusion
  29.5 0.1 reshape.298
  29.7 0.1 copy.88
  29.9 0.2 copy.86
  30.1 0.2 copy.85
  30.3 1.0 fusion.7
  31.4 0.1 fusion.56
  31.5 1.5 multiply_reduce_fusion.2
  33.0 0.1 fusion.55
  33.1 13.0 %fusion.8 = bf16[32,38,1024]{2,1,0:T(8,128)(2,1)S(1)} fusion(f32[1024]{0:T(1024)S(1)} %get-tuple-element.49, f32[1024]{0:T(1024)S(1)} %get-tuple-element.48, s32[38,1024]{1,0:T(8,128)S(1)} %broadcast_add_fusion, s32[32]{0:T(128)S(1)} %fusion.79, f32[32,1024]{1,0:T(8,128)S(1)} %pad_maximum_fusion.5, f32[32,38,1024]{2,1,0:T(8,128)S(1)} %get-tuple-element.47, ...), kind=kLoop, calls=%fused_computation.17 | loop fusion | flops 89653248 | bytes 7897216 | tf_op jit(solution)/shard_map/convert_element_type | solution.py:149
  46.1 0.7 slice.131
  46.8 11.0 %fusion.33 = (bf16[32,37,512]{2,1,0:T(8,128)(2,1)S(1)}, bf16[32,37,512]{2,1,0:T(8,128)(2,1)}) fusion(bf16[32,37,512]{2,0,1:T(8,128)(2,1)S(1)} %copy-done.5, f32[32,37]{1,0:T(8,128)S(1)} %fusion.74, bf16[1536,512,1]{1,0,2:T(8,128)(2,1)S(1)} %bitcast.47, bf16[32,37,512]{2,1,0:T(8,128)(2,1)S(1)} %slice.131, bf16[32,37,1024]{2,1,0:T(8,128)(2,1)S(1)} %bitcast.49), kind=kOutput, calls=%fused_computation.58 | convolution fusion | flops 1916829696 | bytes 8852096 | tf_op jit(solution)/shard_map/rui,io->ruo/dot_general | solution.py:152
  57.8 2.3 %fusion.48 = f32[512,1536,1]{1,0,2:T(8,128)S(1)} fusion(bf16[32,37,512]{2,1,0:T(8,128)(2,1)S(1)} %get-tuple-element.42, bf16[32,37,512]{2,1,0:T(8,128)(2,1)S(1)} %slice.131, bf16[32,37,1024]{2,1,0:T(8,128)(2,1)S(1)} %bitcast.50), kind=kOutput, calls=%fused_computation.81 | convolution fusion | flops 1869545472 | bytes 7995392 | tf_op jit(solution)/shard_map/ruo,rui->oi/dot_general | solution.py:159
  60.1 2.3 %fusion.90 = f32[32,37,1536]{2,1,0:T(8,128)S(1)} fusion(bf16[32,37,512]{2,1,0:T(8,128)(2,1)S(1)} %get-tuple-element.42, bf16[1536,512,1]{1,0,2:T(8,128)(2,1)S(1)} %bitcast.48), kind=kOutput, calls=%fused_computation.168 | convolution fusion | flops 1862270976 | bytes 10059776 | tf_op jit(solution)/shard_map/ruo,io->rui/dot_general | solution.py:160
  62.4 0.6 slice.132
  63.0 2.4 %copy-done.1 = f32[32,37,1536]{2,1,0:T(8,128)} copy-done((f32[32,37,1536]{2,1,0:T(8,128)}, f32[32,37,1536]{2,1,0:T(8,128)S(1)}, u32[]{:S(2)}) %copy-start.1) | copy-done | bytes 7274520
  65.4 2.0 %copy.76 = f32[32,2,8,1536]{3,2,0,1:T(8,128)} copy(f32[32,2,8,1536]{3,2,1,0:T(8,128)S(1)} %bitcast.51) | data formatting | bytes 6291456 | tf_op jit(solution)/shard_map/concatenate | solution.py:206
  67.4 0.9 slice-done
  68.3 5.7 %multiply_reduce_fusion = (f32[1024]{0:T(1024)S(1)}, f32[32,1024]{1,0:T(8,128)S(1)}, f32[32,1024]{1,0:T(8,128)S(1)}, f32[1024]{0:T(1024)S(1)}, f32[32,38,1024]{2,1,0:T(8,128)S(1)}) fusion(f32[32,1024]{1,0:T(8,128)S(1)} %pad_maximum_fusion.5, f32[32,38,1024]{2,1,0:T(8,128)S(1)} %get-tuple-element.47, f32[32,1024]{1,0:T(8,128)S(1)} %pad_maximum_fusion.4, ...), kind=kLoop, calls=%fused_computation.19 | loop fusion | flops 29816832 | bytes 17932416 | tf_op jit(solution)/shard_map/reduce_sum | solution.py:165
  74.0 0.1 fusion.52
  74.2 4.1 %fusion.50 = f32[1024,15]{0,1:T(8,128)S(1)} fusion(f32[32,38,1024]{2,1,0:T(8,128)S(1)} %get-tuple-element.38, f32[32,1024]{1,0:T(8,128)S(1)} %pad_maximum_fusion.7, f32[32,1024]{1,0:T(8,128)S(1)} %pad_maximum_fusion.6, f32[1024]{0:T(1024)S(1)} %get-tuple-element.48, f32[32,1024]{1,0:T(8,128)S(1)} %pad_maximum_fusion.5, ...), kind=kOutput, calls=%fused_computation.85 | convolution fusion | flops 236657920 | bytes 10743552 | tf_op jit(solution)/shard_map/ruj,rum->jm/dot_general | solution.py:173
  78.3 0.5 concatenate.53
  78.9 0.5 copy.77
  79.3 0.1 add.211
  79.4 0.4 copy.78
  79.9 0.1 add.213
  80.0 0.4 copy.79
  80.5 4.3 %concatenate.54 = f32[32,2,8,1548]{3,2,0,1:T(8,128)} concatenate(f32[32,2,8,1536]{3,2,0,1:T(8,128)} %copy.76, f32[32,2,8,10]{3,2,0,1:T(8,128)S(1)} %copy.77, f32[32,2,8,1]{3,2,0,1:T(8,128)S(1)} %copy.78, f32[32,2,8,1]{3,2,0,1:T(8,128)S(1)} %copy.79), dimensions={3} | concatenate | bytes 6340608 | tf_op jit(solution)/shard_map/concatenate | solution.py:206
  84.8 2.8 %dynamic-slice_bitcast_fusion = f32[32,8,1548]{2,1,0:T(8,128)} fusion(f32[32,2,8,1548]{3,2,0,1:T(8,128)} %concatenate.54, s32[]{:T(128)S(6)} %select_n.84), kind=kLoop, calls=%fused_computation.84 | loop fusion | bytes 3170308 | tf_op jit(solution)/shard_map/jit(dynamic_index_in_dim)/squeeze | solution.py:212
  87.6 2.9 %collective-permute-start = (f32[32,8,1548]{2,1,0:T(8,128)}, f32[32,8,1548]{2,1,0:T(8,128)S(1)}, u32[]{:S(2)}, u32[]{:S(2)}) collective-permute-start(f32[32,8,1548]{2,1,0:T(8,128)} %dynamic-slice_bitcast_fusion), channel_id=1, source_target_pairs={{0,32},{32,0},{64,96},{96,64},{128,160},{160,128},{192,224},{224,1... | collective-permute-start | bytes 4755464 | tf_op jit(solution)/shard_map/ppermute | solution.py:214
  90.5 2.7 %copy.81 = bf16[32,37,512]{2,0,1:T(8,128)(2,1)} copy(bf16[32,37,512]{2,1,0:T(8,128)(2,1)} %get-tuple-element.43) | data formatting | bytes 2424832
  93.2 0.7 collective-permute-done
  93.9 2.8 %bitcast_add_fusion.src_ref = f32[32,8,1548]{2,1,0:T(8,128)} fusion(f32[32,8,1548]{2,1,0:T(8,128)S(1)} %collective-permute-done, f32[32,2,8,1548]{3,2,0,1:T(8,128)} %concatenate.54, s32[]{:T(128)S(6)} %select_n.83), kind=kLoop, calls=%fused_computation.83 | loop fusion | flops 396288 | bytes 4755460 | tf_op jit(solution)/shard_map/add | solution.py:214
  96.7 47.2 %shard_map.119 = f32[32,8,1548]{2,1,0:T(8,128)} custom-call(f32[32,8,1548]{2,1,0:T(8,128)} %bitcast_add_fusion.src_ref), custom_call_target="tpu_custom_call" | custom-call | tf_op jit(solution)/shard_map/pallas_call | solution.py:82
  143.9 1.6 reduce_sum.78
  145.4 0.7 reshape.263.src_ref
  146.1 9.0 %shard_map.120 = f32[8,1,1548]{2,1,0:T(1,128)} custom-call(f32[8,1,1548]{2,1,0:T(1,128)} %reshape.263.src_ref), custom_call_target="tpu_custom_call" | custom-call | tf_op jit(solution)/shard_map/pallas_call | solution.py:82
  155.1 0.9 reduce_sum.79
  156.0 0.6 broadcast_in_dim.19.src_ref
  156.6 12.1 %shard_map.121 = f32[16,1,1548]{2,1,0:T(1,128)} custom-call(f32[1,1,1548]{2,1,0:T(1,128)} %broadcast_in_dim.19.src_ref), custom_call_target="tpu_custom_call" | custom-call | tf_op jit(solution)/shard_map/pallas_call | solution.py:82
  168.7 0.9 copy.91
  169.6 0.7 slice_reduce_fusion
  170.3 0.1 reshape.266
  170.4 0.7 copy.82
  171.1 0.7 copy.83
  (32 shorter events, 0.3 us)
Async XLA Ops:
  0.6 46.2 %copy-start = (bf16[3,512,512]{2,1,0:T(8,128)(2,1)S(1)}, bf16[3,512,512]{2,1,0:T(8,128)(2,1)}, u32[]{:S(2)}) copy-start(bf16[3,512,512]{2,1,0:T(8,128)(2,1)} %param.14) | copy-start | bytes 4718596
  5.7 23.8 %all-to-all-start = ((bf16[32,2,192]{2,1,0:T(2,128)(2,1)}), bf16[32,2,192]{2,1,0:T(2,128)(2,1)S(1)}, u32[]{:S(2)}, u32[]{:S(2)}) async-start(bf16[32,2,192]{2,1,0:T(2,128)(2,1)} %reshape.297), calls=%async_computation | async-start | bytes 65536 | tf_op jit(solution)/shard_map/all_to_all | solution.py:194
  21.7 7.8 %copy-start.3 = (f32[512]{0:T(512)S(1)}, f32[512]{0:T(512)}, u32[]{:S(2)}) copy-start(f32[512]{0:T(512)} %param.12) | copy-start | bytes 6148
  21.7 7.8 %copy-start.4 = (f32[512]{0:T(512)S(1)}, f32[512]{0:T(512)}, u32[]{:S(2)}) copy-start(f32[512]{0:T(512)} %param.13) | copy-start | bytes 6148
  21.7 8.6 %copy-start.2 = (bf16[10,512]{1,0:T(8,128)(2,1)S(1)}, bf16[10,512]{1,0:T(8,128)(2,1)}, u32[]{:S(2)}) copy-start(bf16[10,512]{1,0:T(8,128)(2,1)} %param.11) | copy-start | bytes 30724
  33.1 13.7 %copy-start.5 = (bf16[32,37,512]{2,0,1:T(8,128)(2,1)S(1)}, bf16[32,37,512]{2,0,1:T(8,128)(2,1)}, u32[]{:S(2)}) copy-start(bf16[32,37,512]{2,0,1:T(8,128)(2,1)} %param.15) | copy-start | bytes 3637252
  62.4 3.1 %copy-start.1 = (f32[32,37,1536]{2,1,0:T(8,128)}, f32[32,37,1536]{2,1,0:T(8,128)S(1)}, u32[]{:S(2)}) copy-start(f32[32,37,1536]{2,1,0:T(8,128)S(1)} %fusion.90) | copy-start | bytes 21823492
  65.4 2.9 %slice-start = ((f32[32,37,1536]{2,1,0:T(8,128)}), f32[32,37,512]{2,1,0:T(8,128)S(1)}, s32[]{:S(2)}) async-start(f32[32,37,1536]{2,1,0:T(8,128)} %copy-done.1), calls=%async_computation.1 | async-start | bytes 5242880 | tf_op jit(solution)/shard_map/slice | solution.py:162
  87.6 6.3 %collective-permute-start = (f32[32,8,1548]{2,1,0:T(8,128)}, f32[32,8,1548]{2,1,0:T(8,128)S(1)}, u32[]{:S(2)}, u32[]{:S(2)}) collective-permute-start(f32[32,8,1548]{2,1,0:T(8,128)} %dynamic-slice_bitcast_fusion), channel_id=1, source_target_pairs={{0,32},{32,0},{64,96},{96,64},{128,160},{160,128},{192,224},{224,1... | collective-permute-start | bytes 4755464 | tf_op jit(solution)/shard_map/ppermute | solution.py:214

commit v6 on v5

--- a/solution.py
+++ b/solution.py
@@ -10,7 +10,10 @@
 MESH = pl.DeviceIdType.MESH
 
 
-def exchange_kernel(members, axis, stride, gather, src_ref, dst_ref, send_sems, recv_sems, local_sem):
+def exchange_kernel(members, axis, stride, gather, count, *refs):
+    srcs = refs[:count]
+    dsts = refs[count : 2 * count]
+    send_sems, recv_sems, local_sems = refs[2 * count :]
     if axis == "grp":
         coord = lax.axis_index("grp")
         me = coord // stride
@@ -23,8 +26,18 @@
     def where(peer):
         return (peer * stride + offset, other) if axis == "grp" else (other, peer)
 
-    def source(peer):
-        return src_ref.at[0] if gather else src_ref.at[peer]
+    def source(a, peer):
+        return srcs[a].at[0] if gather else srcs[a].at[peer]
+
+    def remote(a, step, peer, src_peer, slot):
+        return pltpu.make_async_remote_copy(
+            src_ref=source(a, src_peer),
+            dst_ref=dsts[a].at[slot],
+            send_sem=send_sems.at[a, step],
+            recv_sem=recv_sems.at[a, step],
+            device_id=where(peer),
+            device_id_type=MESH,
+        )
 
     barrier = pltpu.get_barrier_semaphore()
 
@@ -35,19 +48,16 @@
 
     lax.fori_loop(1, members, greet, 0)
     pl.semaphore_wait(barrier, members - 1)
-    local = pltpu.make_async_copy(source(me), dst_ref.at[me], local_sem)
-    local.start()
+    locals_ = [
+        pltpu.make_async_copy(source(a, me), dsts[a].at[me], local_sems.at[a]) for a in range(count)
+    ]
+    for local in locals_:
+        local.start()
 
     def send(step, carry):
         peer = lax.rem(me + step, members)
-        pltpu.make_async_remote_copy(
-            src_ref=source(peer),
-            dst_ref=dst_ref.at[me],
-            send_sem=send_sems.at[step],
-            recv_sem=recv_sems.at[step],
-            device_id=where(peer),
-            device_id_type=MESH,
-        ).start()
+        for a in range(count):
+            remote(a, step, peer, peer, me).start()
         return carry
 
     lax.fori_loop(1, members, send, 0)
@@ -55,42 +65,31 @@
     def finish(step, carry):
         peer = lax.rem(me + step, members)
         sender = lax.rem(me + members - step, members)
-        pltpu.make_async_remote_copy(
-            src_ref=source(peer),
-            dst_ref=dst_ref.at[me],
-            send_sem=send_sems.at[step],
-            recv_sem=recv_sems.at[step],
-            device_id=where(peer),
-            device_id_type=MESH,
-        ).wait_send()
-        pltpu.make_async_remote_copy(
-            src_ref=source(me),
-            dst_ref=dst_ref.at[sender],
-            send_sem=send_sems.at[step],
-            recv_sem=recv_sems.at[step],
-            device_id=where(sender),
-            device_id_type=MESH,
-        ).wait_recv()
+        for a in range(count):
+            remote(a, step, peer, peer, me).wait_send()
+            remote(a, step, sender, me, sender).wait_recv()
         return carry
 
     lax.fori_loop(1, members, finish, 0)
-    local.wait()
+    for local in locals_:
+        local.wait()
 
 
 def exchange(blocks, members, axis, stride, gather, ident):
-    shape = (members,) + blocks.shape[1:]
+    count = len(blocks)
+    shapes = [jax.ShapeDtypeStruct((members,) + b.shape[1:], b.dtype) for b in blocks]
     return pl.pallas_call(
-        functools.partial(exchange_kernel, members, axis, stride, gather),
-        out_shape=jax.ShapeDtypeStruct(shape, blocks.dtype),
-        in_specs=[pl.BlockSpec(memory_space=pl.ANY)],
-        out_specs=pl.BlockSpec(memory_space=pl.ANY),
+        functools.partial(exchange_kernel, members, axis, stride, gather, count),
+        out_shape=shapes,
+        in_specs=[pl.BlockSpec(memory_space=pl.ANY)] * count,
+        out_specs=[pl.BlockSpec(memory_space=pl.ANY)] * count,
         scratch_shapes=[
-            pltpu.SemaphoreType.DMA((members,)),
-            pltpu.SemaphoreType.DMA((members,)),
-            pltpu.SemaphoreType.DMA,
+            pltpu.SemaphoreType.DMA((count, members)),
+            pltpu.SemaphoreType.DMA((count, members)),
+            pltpu.SemaphoreType.DMA((count,)),
         ],
         compiler_params=pltpu.CompilerParams(collective_id=ident, has_side_effects=True),
-    )(blocks)
+    )(*blocks)
 
 
 def gelu_slope(value):
@@ -156,7 +155,12 @@
     ]
     features = (jax.nn.gelu(pre1, approximate=False) * mask1).astype(jnp.bfloat16)
     grad1 = (cot.astype(jnp.float32) * gelu_slope(pre1) * mask1).astype(jnp.bfloat16)
-    grad_kernel = jnp.einsum("ruo,rui->oi", grad1, taps, preferred_element_type=jnp.float32)
+    members = lax.axis_size("dev")
+    width = chans // members
+    split = grad1.reshape(rows, frames1, members, 2, width // 2)
+    grad_kernel = jnp.einsum(
+        "rudhj,rui->hdji", split, taps, preferred_element_type=jnp.float32
+    )
     back = jnp.einsum("ruo,io->rui", grad1, kernel, preferred_element_type=jnp.float32)
     dact0 = jnp.pad(back[:, :, : 2 * chans], ((0, 0), (0, pairs - frames1), (0, 0))) + jnp.pad(
         back[:, :, 2 * chans :], ((0, 0), (1, pairs - frames1 - 1), (0, chans))
@@ -179,6 +183,7 @@
     )
     grad_filter = grad_pair[:chans, :ker_first] + grad_pair[chans:, stride_first:]
     small = jnp.concatenate([grad_filter, grad_gain[:, None], grad_bias[:, None]], axis=1)
+    small = small.reshape(members, 2, width // 2, small.shape[1]).transpose(1, 0, 2, 3)
     grads = (grad_kernel, small)
     return (features, grads)
 
@@ -192,9 +197,14 @@
     dealt = own_order.reshape(share, members).T.reshape(rows)
     outgoing = jnp.take(wave, dealt, axis=0)
     arrived = lax.all_to_all(outgoing, "dev", split_axis=0, concat_axis=0, tiled=True)
-    group_lens = jnp.take_along_axis(lengths.reshape(members, rows), order, axis=1)
-    group_lens = group_lens.reshape(members, share, members)
-    lens = lax.dynamic_index_in_dim(group_lens, member, 2, keepdims=False).reshape(rows)
+    picks = lax.dynamic_index_in_dim(
+        order.reshape(members, share, members), member, 2, keepdims=False
+    )
+    slots = jnp.arange(rows, dtype=jnp.int32)
+    hits = picks[:, :, None] == slots[None, None, :]
+    lens = jnp.sum(
+        jnp.where(hits, lengths.reshape(members, 1, rows), 0), axis=2, dtype=jnp.int32
+    ).reshape(rows)
     features, (grad_kernel, small) = local_pass(
         arrived, lens, w_first, norm_gain, norm_bias, w_second, cot
     )
@@ -203,21 +213,32 @@
     ker_first = w_first.shape[0]
     members = lax.axis_size("dev")
     groups = lax.axis_size("grp")
-    full = jnp.concatenate([grad_kernel, small], axis=1)
-    chans, span = full.shape
+    core = lax.rem(lax.axis_index("grp"), 2)
+    pairs = [(g, g ^ 1) for g in range(groups)]
+
+    def pair_sum(halves):
+        keep = lax.dynamic_index_in_dim(halves, core, 0, keepdims=False)
+        give = lax.dynamic_index_in_dim(halves, 1 - core, 0, keepdims=False)
+        return keep + lax.ppermute(give, "grp", pairs)
+
+    mine_kernel = pair_sum(grad_kernel).astype(jnp.bfloat16)
+    mine_small = pair_sum(small)
+    pieces_kernel, pieces_small = exchange(
+        [mine_kernel, mine_small], members, "dev", 1, False, 0
+    )
+    part = jnp.concatenate(
+        [jnp.sum(pieces_kernel.astype(jnp.float32), axis=0), jnp.sum(pieces_small, axis=0)],
+        axis=1,
+    )
+    chans = w_second.shape[2]
     width = chans // members
-    halves = full.reshape(members, 2, width // 2, span)
-    core = lax.rem(lax.axis_index("grp"), 2)
-    keep = lax.dynamic_index_in_dim(halves, core, 1, keepdims=False)
-    give = lax.dynamic_index_in_dim(halves, 1 - core, 1, keepdims=False)
-    pairs = [(g, g ^ 1) for g in range(groups)]
-    mine = keep + lax.ppermute(give, "grp", pairs)
-    pieces = exchange(mine, members, "dev", 1, False, 0)
-    part = jnp.sum(pieces, axis=0)
+    span = part.shape[1]
     rows_y = groups // 2
-    scattered = exchange(part.reshape(rows_y, (width // 2) // rows_y, span), rows_y, "grp", 2, False, 1)
+    (scattered,) = exchange(
+        [part.reshape(rows_y, (width // 2) // rows_y, span)], rows_y, "grp", 2, False, 1
+    )
     total = jnp.sum(scattered, axis=0)
-    gathered = exchange(total[None], groups, "grp", 1, True, 2)
+    (gathered,) = exchange([total[None]], groups, "grp", 1, True, 2)
     gathered = gathered.reshape(rows_y, 2, (width // 2) // rows_y, span)
     owned = gathered.transpose(1, 0, 2, 3).reshape(width, span)
     grad_second = (

time: 173 us -> 168 us (0.971)
  Pallas kernels: 68.3 us -> 49.3 us
  matrix products: 20.7 us -> 26.9 us
  waiting for transfers between devices: 0.69 us -> 5.93 us
  local copies, waits for them, and re-layouts: 35.1 us -> 30.3 us
  other arithmetic: 29.4 us -> 34.1 us
  starting transfers between devices: 16.6 us -> 19.8 us
    pallas_call x3, Pallas kernels: 68.3 us -> 49.3 us  [exchange(): pl.pallas_call(functools.partial(exchange_kernel, members, axis, stride,...]
    reduce_sum x1 -> x2, other arithmetic: 1.51 us -> 8.87 us  [fold(): s = jnp.sum(x, axis=1)]
    gather x3 -> x0, local copies, waits for them, and re-layouts: 7.2 us -> none  [shards(): jnp.take_along_axis(lengths.reshape(members, rows), order, axis=1)]
    all_to_all x1, waiting for transfers between devices: 0.01 us -> 5.92 us  [shards(): lax.all_to_all(outgoing, 'dev', split_axis=0, concat_axis=0, tiled=True)]
    concatenate x4 -> x2, local copies, waits for them, and re-layouts: 7.3 us -> 2.35 us  [local_pass(): jnp.concatenate([grad_filter, grad_gain[:, None], grad_bias[:, None]], ax...]
    reduce_sum x2 -> x3, other arithmetic: 7.27 us -> 2.38 us  [the longest x1 1.26 us: shards(): jnp.sum(pieces_kernel.astype(jnp.float32), axis=0)]
    convert_element_type x0 -> x1, local copies, waits for them, and re-layouts: none -> 4.77 us  [local_pass(): (cot.astype(jnp.float32) * gelu_slope(pre1) * mask1).astype(jnp.bfloat16)]
    unnamed x20 -> x38, local copies, waits for them, and re-layouts: 7.88 us -> 12 us
  transfers between devices with their start and end apart: 2 -> 3, of which waited for: 1 -> 1; matrix products, arithmetic and copies ran while one was open for 7% -> 17% of each run, Pallas kernels for 0% -> 0%
where the time goes in v6:
time: 168 us; the launch traced here: 167 us
  Pallas kernels  49.3 us (29%)
  other arithmetic  34.1 us (20%)
  local copies, waits for them, and re-layouts  30.3 us (18%)
  matrix products  26.9 us (16%)
  starting transfers between devices  19.8 us (12%)
  waiting for transfers between devices  5.93 us (4%)
    pallas_call x3, Pallas kernels, exchange(): pl.pallas_call(functools.partial(exchange_kernel, members, axis, stride,...  49.3 us
    all_to_all x1, starting transfers between devices, shards(): lax.all_to_all(outgoing, 'dev', split_axis=0, concat_axis=0, tiled=True)  13.7 us
    convert_element_type x1, other arithmetic, local_pass(): act0 = (jax.nn.gelu(lifted, approximate=False) * mask0).astype(jnp.bfloat16)  12.9 us
    unnamed x38, local copies, waits for them, and re-layouts  12 us
    dot_general x1, matrix products, local_pass(): jnp.einsum('rui,io->ruo', taps, kernel, preferred_element_type=jnp.float32)  11.9 us
    reduce_sum x2, other arithmetic, fold(): s = jnp.sum(x, axis=1)  8.87 us
    dot_general x1, matrix products, local_pass(): jnp.einsum('ruj,rum->jm', dpre0, patches.astype(jnp.float32), precision=l...  6.96 us
    ppermute x2, starting transfers between devices, pair_sum(): return keep + lax.ppermute(give, 'grp', pairs)  6.09 us
  transfers between devices with their start and end apart: 3, of which 1 were waited for; matrix products, arithmetic and copies ran while one was open for 17% of the time, Pallas kernels for 0%

profile of v6, /device:TPU:1, one launch (start us, length us, event | category | flops | bytes accessed | tf_op | source)
XLA Modules:
  0.0 167.4 jit_solution(1517763682429216858)
XLA Ops:
  0.7 0.8 fusion.80
  1.5 0.7 compare_and_fusion
  2.2 1.4 gather_fusion
  3.5 0.1 bitcast_select_fusion
  3.6 0.5 broadcast.387
  4.1 0.7 reduce.8
  4.8 0.7 reshape.347
  5.5 13.7 %all-to-all-start = ((bf16[32,2,192]{2,1,0:T(2,128)(2,1)}), bf16[32,2,192]{2,1,0:T(2,128)(2,1)S(1)}, u32[]{:S(2)}, u32[]{:S(2)}) async-start(bf16[32,2,192]{2,1,0:T(2,128)(2,1)} %reshape.347), calls=%async_computation | async-start | bytes 65536 | tf_op jit(solution)/shard_map/all_to_all | solution.py:199
  19.2 0.9 dynamic-slice_reduce_fusion
  20.1 0.8 reshape.323
  20.9 0.2 select_reduce_fusion
  21.1 0.1 fusion.76
  21.2 0.1 broadcast_add_fusion
  21.3 0.8 pad_maximum_fusion.12
  22.1 5.9 %all-to-all-done = bf16[32,2,192]{2,1,0:T(2,128)(2,1)S(1)} async-done(((bf16[32,2,192]{2,1,0:T(2,128)(2,1)}), bf16[32,2,192]{2,1,0:T(2,128)(2,1)S(1)}, u32[]{:S(2)}, u32[]{:S(2)}) %all-to-all-start) | async-done | bytes 24608 | tf_op jit(solution)/shard_map/all_to_all | solution.py:199
  28.0 0.1 reshape.348
  28.1 0.1 copy.112
  28.4 0.2 copy.110
  28.5 0.2 copy.109
  28.8 1.8 %fusion.7 = (f32[32,1024]{1,0:T(8,128)S(1)}, f32[32,38,1024]{2,1,0:T(8,128)S(1)}) fusion(s32[38,1024]{1,0:T(8,128)S(1)} %broadcast_add_fusion, s32[32]{0:T(128)S(1)} %get-tuple-element.55, bf16[10,512]{1,0:T(8,128)(2,1)} %param.11, bf16[32,38,5]{1,2,0:T(8,128)(2,1)S(1)} %copy.110, bf16[32,38,10]{1,2,0:T(8,128)(2,1)S(1)} %copy.109), kind=kOutput, calls=%fused_computation.15 | convolution fusion | flops 41254144 | bytes 5314304 | tf_op jit(solution)/shard_map/rum,mc->ruc/dot_general | solution.py:124
  30.6 0.1 fusion.64
  30.7 1.4 multiply_reduce_fusion.2
  32.2 0.1 fusion.63
  32.3 0.7 copy-done.7
  33.0 12.9 %fusion.8 = bf16[32,38,1024]{2,1,0:T(8,128)(2,1)S(1)} fusion(f32[1024]{0:T(1024)S(1)} %get-tuple-element.59, f32[1024]{0:T(1024)S(1)} %get-tuple-element.58, s32[38,1024]{1,0:T(8,128)S(1)} %broadcast_add_fusion, s32[32]{0:T(128)S(1)} %get-tuple-element.55, f32[32,1024]{1,0:T(8,128)S(1)} %pad_maximum_fusion.5, f32[32,38,1024]{2,1,0:T(8,128)S(1)} %get-tuple-element.57, ...), kind=kLoop, calls=%fused_computation.16 | loop fusion | flops 89653248 | bytes 7897216 | tf_op jit(solution)/shard_map/convert_element_type | solution.py:148
  45.9 0.7 slice.129
  46.7 11.9 %fusion.41 = (bf16[32,37,512]{2,1,0:T(8,128)(2,1)}, bf16[32,37,512]{2,1,0:T(8,128)(2,1)}) fusion(bf16[32,37,512]{2,0,1:T(8,128)(2,1)S(1)} %copy-done.12, f32[32,37]{1,0:T(8,128)S(1)} %fusion.76, bf16[1536,512,1]{1,0,2:T(8,128)(2,1)S(1)} %bitcast.60, bf16[32,37,512]{2,1,0:T(8,128)(2,1)S(1)} %slice.129, bf16[32,37,1024]{2,1,0:T(8,128)(2,1)S(1)} %bitcast.64), kind=kOutput, calls=%fused_computation.61 | convolution fusion | flops 1916829696 | bytes 8852096 | tf_op jit(solution)/shard_map/rui,io->ruo/dot_general | solution.py:151
  58.6 4.8 %copy.90 = bf16[32,37,512]{1,2,0:T(8,128)(2,1)} copy(bf16[32,37,512]{2,1,0:T(8,128)(2,1)} %get-tuple-element.48) | data formatting | bytes 2424832 | tf_op jit(solution)/shard_map/convert_element_type | solution.py:157
  63.4 3.6 %fusion.91 = f32[32,37,1536]{2,1,0:T(8,128)S(1)} fusion(bf16[32,37,512]{2,1,0:T(8,128)(2,1)} %get-tuple-element.48, bf16[1536,512,1]{1,0,2:T(8,128)(2,1)S(1)} %bitcast.61), kind=kOutput, calls=%fused_computation.166 | convolution fusion | flops 1862270976 | bytes 10059776 | tf_op jit(solution)/shard_map/ruo,io->rui/dot_general | solution.py:164
  67.0 4.0 %copy-done.2 = f32[32,37,1536]{2,1,0:T(8,128)} copy-done((f32[32,37,1536]{2,1,0:T(8,128)}, f32[32,37,1536]{2,1,0:T(8,128)S(1)}, u32[]{:S(2)}) %copy-start.2) | copy-done | bytes 7274520
  71.0 1.0 copy-done.5
  72.0 0.8 copy-done.4
  72.8 2.6 %fusion.26 = f32[1536,32,2,8]{0,3,1,2:T(8,128)S(1)} fusion(bf16[32,37,32,2,8]{1,4,3,2,0:T(8,128)(2,1)S(1)} %bitcast.66, bf16[32,37,512]{2,1,0:T(8,128)(2,1)S(1)} %slice.129, bf16[32,37,1024]{2,1,0:T(8,128)(2,1)S(1)} %bitcast.65), kind=kOutput, calls=%fused_computation.50 | convolution fusion | flops 1869545472 | bytes 7995392 | tf_op jit(solution)/shard_map/rudhj,rui->hdji/dot_general | solution.py:161
  75.4 1.3 dynamic-slice_bitcast_fusion
  76.7 4.2 %collective-permute-start = (f32[32,8,1536]{2,1,0:T(8,128)}, f32[32,8,1536]{2,1,0:T(8,128)S(1)}, u32[]{:S(2)}, u32[]{:S(2)}) collective-permute-start(f32[32,8,1536]{2,1,0:T(8,128)} %dynamic-slice_bitcast_fusion), channel_id=1, source_target_pairs={{0,32},{32,0},{64,96},{96,64},{128,160},{160,128},{192,224},{224,1... | collective-permute-start | bytes 4718600 | tf_op jit(solution)/shard_map/ppermute | solution.py:222
  81.0 7.5 %multiply_reduce_fusion.1 = (f32[32,1024]{1,0:T(8,128)}, f32[1024]{0:T(1024)S(1)}, f32[32,1024]{1,0:T(8,128)}, f32[1024]{0:T(1024)S(1)}, f32[32,38,1024]{2,1,0:T(8,128)}) fusion(f32[1024]{0:T(1024)S(1)} %get-tuple-element.58, f32[32,1024]{1,0:T(8,128)S(1)} %copy-done.8, f32[32,38,1024]{2,1,0:T(8,128)S(1)} %bitcast.63, f32[32,1024]{1,0:T(8,128)S(1)} %pad_maximum_fusion.4, ...), kind=kLoop, calls=%fused_computation.22 | loop fusion | flops 29816832 | bytes 17932416 | tf_op jit(solution)/shard_map/reduce_sum | solution.py:134
  88.4 0.6 slice_add_fusion.6
  89.0 0.1 add.227
  89.1 0.1 copy.96
  89.2 0.8 add.225
  90.0 0.7 copy.95
  90.7 1.0 fusion.60
  91.8 7.0 %fusion.58 = f32[1024,15]{0,1:T(8,128)S(1)} fusion(f32[32,38,1024]{2,1,0:T(8,128)} %get-tuple-element.45, f32[32,1024]{1,0:T(8,128)S(1)} %pad_maximum_fusion.7, f32[32,1024]{1,0:T(8,128)S(1)} %pad_maximum_fusion.6, f32[1024]{0:T(1024)S(1)} %get-tuple-element.58, f32[32,1024]{1,0:T(8,128)} %copy-done.7, s32[38,1024]{1,0:T(8,128)S(1)} %broadcast_add_fusion, ...), kind=kOutput, calls=%fused_computation.89 | convolution fusion | flops 236657920 | bytes 10743552 | tf_op jit(solution)/shard_map/ruj,rum->jm/dot_general | solution.py:177
  98.7 1.2 concatenate.53
  100.0 1.1 copy.94
  101.1 0.8 copy.98
  101.9 1.9 %collective-permute-start.1 = (f32[32,8,12]{2,1,0:T(8,128)}, f32[32,8,12]{2,1,0:T(8,128)}, u32[]{:S(2)}, u32[]{:S(2)}) collective-permute-start(f32[32,8,12]{2,1,0:T(8,128)} %bitcast.19), channel_id=1, source_target_pairs={{0,32},{32,0},{64,96},{96,64},{128,160},{160,128},{192,224},{224,1... | collective-permute-start | bytes 36872 | tf_op jit(solution)/shard_map/ppermute | solution.py:222
  103.8 2.7 %copy.100 = bf16[32,37,512]{2,0,1:T(8,128)(2,1)} copy(bf16[32,37,512]{2,1,0:T(8,128)(2,1)} %get-tuple-element.49) | data formatting | bytes 2424832
  106.6 0.1 copy.97
  106.7 1.6 bitcast_add_fusion.1.refs_1_
  108.3 2.5 %fusion.57.refs_0_ = bf16[32,8,1536]{2,1,0:T(8,128)(2,1)} fusion(f32[32,8,1536]{2,1,0:T(8,128)S(1)} %collective-permute-done, f32[1536,32,2,8]{0,3,1,2:T(8,128)} %copy-done.6, s32[]{:T(128)S(6)} %select_n.94), kind=kLoop, calls=%fused_computation.86 | loop fusion | flops 786432 | bytes 3932164 | tf_op jit(solution)/shard_map/convert_element_type | solution.py:224
  110.7 27.5 %shard_map.119 = (bf16[32,8,1536]{2,1,0:T(8,128)(2,1)}, f32[32,8,12]{2,1,0:T(8,128)}) custom-call(bf16[32,8,1536]{2,1,0:T(8,128)(2,1)} %fusion.57.refs_0_, f32[32,8,12]{2,1,0:T(8,128)} %bitcast_add_fusion.1.refs_1_), custom_call_target="tpu_custom_call" | custom-call | tf_op jit(solution)/shard_map/pallas_call | solution.py:81
  138.3 1.3 convert_reduce_fusion
  139.5 0.9 reduce_sum.98
  140.5 0.7 reshape.327.refs_0_
  141.1 8.7 %shard_map.120 = f32[8,1,1548]{2,1,0:T(1,128)} custom-call(f32[8,1,1548]{2,1,0:T(1,128)} %reshape.327.refs_0_), custom_call_target="tpu_custom_call" | custom-call | tf_op jit(solution)/shard_map/pallas_call | solution.py:81
  149.8 0.9 reduce_sum.99
  150.7 0.6 broadcast_in_dim.19.refs_0_
  151.3 13.1 %shard_map.121 = f32[16,1,1548]{2,1,0:T(1,128)} custom-call(f32[1,1,1548]{2,1,0:T(1,128)} %broadcast_in_dim.19.refs_0_), custom_call_target="tpu_custom_call" | custom-call | tf_op jit(solution)/shard_map/pallas_call | solution.py:81
  164.4 0.9 copy.119
  165.3 0.7 slice_reduce_fusion
  166.0 0.7 copy.102
  166.7 0.1 reshape.330
  166.8 0.7 copy.101
  (53 shorter events, 0.3 us)
Async XLA Ops:
  0.6 46.0 %copy-start = (bf16[3,512,512]{2,1,0:T(8,128)(2,1)S(1)}, bf16[3,512,512]{2,1,0:T(8,128)(2,1)}, u32[]{:S(2)}) copy-start(bf16[3,512,512]{2,1,0:T(8,128)(2,1)} %param.14) | copy-start | bytes 4718596
  5.5 22.5 %all-to-all-start = ((bf16[32,2,192]{2,1,0:T(2,128)(2,1)}), bf16[32,2,192]{2,1,0:T(2,128)(2,1)S(1)}, u32[]{:S(2)}, u32[]{:S(2)}) async-start(bf16[32,2,192]{2,1,0:T(2,128)(2,1)} %reshape.347), calls=%async_computation | async-start | bytes 65536 | tf_op jit(solution)/shard_map/all_to_all | solution.py:199
  21.1 11.0 %copy-start.11 = (f32[32]{0:T(128)}, f32[32]{0:T(128)S(1)}, u32[]{:S(2)}) copy-start(f32[32]{0:T(128)S(1)} %get-tuple-element.54) | copy-start | bytes 388
  28.8 1.8 %copy-start.9 = (bf16[32,38,10]{1,2,0:T(8,128)(2,1)}, bf16[32,38,10]{1,2,0:T(8,128)(2,1)S(1)}, u32[]{:S(2)}) copy-start(bf16[32,38,10]{1,2,0:T(8,128)(2,1)S(1)} %copy.109) | copy-start | bytes 72964
  30.6 15.3 %copy-start.1 = (f32[32,38,1024]{2,1,0:T(8,128)}, f32[32,38,1024]{2,1,0:T(8,128)S(1)}, u32[]{:S(2)}) copy-start(f32[32,38,1024]{2,1,0:T(8,128)S(1)} %get-tuple-element.57) | copy-start | bytes 14942212
  32.3 0.7 copy-start.7
  33.0 13.7 %copy-start.12 = (bf16[32,37,512]{2,0,1:T(8,128)(2,1)S(1)}, bf16[32,37,512]{2,0,1:T(8,128)(2,1)}, u32[]{:S(2)}) copy-start(bf16[32,37,512]{2,0,1:T(8,128)(2,1)} %param.15) | copy-start | bytes 3637252
  45.9 12.7 %copy-start.3 = (bf16[32,38,1024]{2,1,0:T(8,128)(2,1)}, bf16[32,38,1024]{2,1,0:T(8,128)(2,1)S(1)}, u32[]{:S(2)}) copy-start(bf16[32,38,1024]{2,1,0:T(8,128)(2,1)S(1)} %fusion.8) | copy-start | bytes 7471108
  67.0 4.0 %copy-start.2 = (f32[32,37,1536]{2,1,0:T(8,128)}, f32[32,37,1536]{2,1,0:T(8,128)S(1)}, u32[]{:S(2)}) copy-start(f32[32,37,1536]{2,1,0:T(8,128)S(1)} %fusion.91) | copy-start | bytes 21823492
  67.0 5.0 %copy-start.5 = (bf16[32,37,512]{1,2,0:T(8,128)(2,1)S(1)}, bf16[32,37,512]{1,2,0:T(8,128)(2,1)}, u32[]{:S(2)}) copy-start(bf16[32,37,512]{1,2,0:T(8,128)(2,1)} %copy.90) | copy-start | bytes 3637252
  67.0 5.8 %copy-start.4 = (bf16[32,38,1024]{2,1,0:T(8,128)(2,1)S(1)}, bf16[32,38,1024]{2,1,0:T(8,128)(2,1)}, u32[]{:S(2)}) copy-start(bf16[32,38,1024]{2,1,0:T(8,128)(2,1)} %copy-done.3) | copy-start | bytes 7471108
  67.0 13.9 %slice-start = ((s8[5242880]{0:T(1024)(128)(4,1)}), s8[4194304]{0:T(1024)(128)(4,1)S(1)}, s32[]{:S(2)}) async-start(s8[5242880]{0:T(1024)(128)(4,1)} %bitcast.62), calls=%async_computation.1 | async-start | bytes 8388608
  72.8 8.1 %slice-start.1 = ((s8[5242880]{0:T(1024)(128)(4,1)}), s8[1048576]{0:T(1024)(128)(4,1)S(1)}, s32[]{:S(2)}) async-start(s8[5242880]{0:T(1024)(128)(4,1)} %bitcast.62), calls=%async_computation.2 | async-start | bytes 2097152
  72.8 8.1 %slice-start.2 = ((f32[32,37,1536]{2,1,0:T(8,128)}), f32[32,37,512]{2,1,0:T(8,128)S(1)}, s32[]{:S(2)}) async-start(f32[32,37,1536]{2,1,0:T(8,128)} %copy-done.2), calls=%async_computation.3 | async-start | bytes 5242880 | tf_op jit(solution)/shard_map/slice | solution.py:166
  72.8 8.1 %slice-start.3 = ((f32[32,37,1536]{2,1,0:T(8,128)}), f32[32,37,1024]{2,1,0:T(8,128)S(1)}, s32[]{:S(2)}) async-start(f32[32,37,1536]{2,1,0:T(8,128)} %copy-done.2), calls=%async_computation.4 | async-start | bytes 10485760 | tf_op jit(solution)/shard_map/slice | solution.py:165
  72.8 8.1 %copy-start.8 = (f32[32,1024]{1,0:T(8,128)S(1)}, f32[32,1024]{1,0:T(8,128)}, u32[]{:S(2)}) copy-start(f32[32,1024]{1,0:T(8,128)} %copy-done.7) | copy-start | bytes 393220
  75.4 13.0 %copy-start.6 = (f32[1536,32,2,8]{0,3,1,2:T(8,128)}, f32[1536,32,2,8]{0,3,1,2:T(8,128)S(1)}, u32[]{:S(2)}) copy-start(f32[1536,32,2,8]{0,3,1,2:T(8,128)S(1)} %fusion.26) | copy-start | bytes 9437188
  76.7 31.5 %collective-permute-start = (f32[32,8,1536]{2,1,0:T(8,128)}, f32[32,8,1536]{2,1,0:T(8,128)S(1)}, u32[]{:S(2)}, u32[]{:S(2)}) collective-permute-start(f32[32,8,1536]{2,1,0:T(8,128)} %dynamic-slice_bitcast_fusion), channel_id=1, source_target_pairs={{0,32},{32,0},{64,96},{96,64},{128,160},{160,128},{192,224},{224,1... | collective-permute-start | bytes 4718600 | tf_op jit(solution)/shard_map/ppermute | solution.py:222
  91.7 9.3 %copy-start.10 = (f32[32,2,8,1]{0,2,3,1:T(8,128)S(1)}, f32[32,2,8,1]{0,2,3,1:T(8,128)}, u32[]{:S(2)}) copy-start(f32[32,2,8,1]{0,2,3,1:T(8,128)} %copy.95) | copy-start | bytes 6148
  101.9 4.8 %collective-permute-start.1 = (f32[32,8,12]{2,1,0:T(8,128)}, f32[32,8,12]{2,1,0:T(8,128)}, u32[]{:S(2)}, u32[]{:S(2)}) collective-permute-start(f32[32,8,12]{2,1,0:T(8,128)} %bitcast.19), channel_id=1, source_target_pairs={{0,32},{32,0},{64,96},{96,64},{128,160},{160,128},{192,224},{224,1... | collective-permute-start | bytes 36872 | tf_op jit(solution)/shard_map/ppermute | solution.py:222

commit v7 on v6

--- a/solution.py
+++ b/solution.py
@@ -157,10 +157,8 @@
     grad1 = (cot.astype(jnp.float32) * gelu_slope(pre1) * mask1).astype(jnp.bfloat16)
     members = lax.axis_size("dev")
     width = chans // members
-    split = grad1.reshape(rows, frames1, members, 2, width // 2)
-    grad_kernel = jnp.einsum(
-        "rudhj,rui->hdji", split, taps, preferred_element_type=jnp.float32
-    )
+    grad_kernel = jnp.einsum("ruo,rui->oi", grad1, taps, preferred_element_type=jnp.float32)
+    grad_kernel = grad_kernel.reshape(members, 2, width // 2, -1).transpose(1, 0, 2, 3)
     back = jnp.einsum("ruo,io->rui", grad1, kernel, preferred_element_type=jnp.float32)
     dact0 = jnp.pad(back[:, :, : 2 * chans], ((0, 0), (0, pairs - frames1), (0, 0))) + jnp.pad(
         back[:, :, 2 * chans :], ((0, 0), (1, pairs - frames1 - 1), (0, chans))
@@ -174,13 +172,11 @@
     first_mean = spread(fold(dnorm) / count0)
     second_mean = spread(fold(dnorm * normed) / count0)
     dpre0 = inv_std * (dnorm - first_mean - normed * second_mean) * mask0
+    high = dpre0.astype(jnp.bfloat16)
+    low = (dpre0 - high.astype(jnp.float32)).astype(jnp.bfloat16)
     grad_pair = jnp.einsum(
-        "ruj,rum->jm",
-        dpre0,
-        patches.astype(jnp.float32),
-        precision=lax.Precision.HIGHEST,
-        preferred_element_type=jnp.float32,
-    )
+        "ruj,rum->jm", high, patches, preferred_element_type=jnp.float32
+    ) + jnp.einsum("ruj,rum->jm", low, patches, preferred_element_type=jnp.float32)
     grad_filter = grad_pair[:chans, :ker_first] + grad_pair[chans:, stride_first:]
     small = jnp.concatenate([grad_filter, grad_gain[:, None], grad_bias[:, None]], axis=1)
     small = small.reshape(members, 2, width // 2, small.shape[1]).transpose(1, 0, 2, 3)

time: 168 us -> 155 us (0.923)
  local copies, waits for them, and re-layouts: 30.3 us -> 19.9 us
  other arithmetic: 34.1 us -> 31.6 us
    unnamed x38 -> x30, local copies, waits for them, and re-layouts: 12 us -> 5.49 us
    convert_element_type x1 -> x0, local copies, waits for them, and re-layouts: 4.77 us -> none  [local_pass(): (cot.astype(jnp.float32) * gelu_slope(pre1) * mask1).astype(jnp.bfloat16)]
    dot_general x2 -> x3, matrix products: 9.54 us -> 11.4 us  [the longest x1 6.44 us: local_pass(): jnp.einsum('ruj,rum->jm', low, patches, preferred_element_type=jnp.float32)]
  transfers between devices with their start and end apart: 3 -> 3, of which waited for: 1 -> 1; matrix products, arithmetic and copies ran while one was open for 17% -> 18% of each run, Pallas kernels for 0% -> 0%
where the time goes in v7:
time: 155 us; the launch traced here: 154 us
  Pallas kernels  49.3 us (32%)
  other arithmetic  31.6 us (20%)
  matrix products  26.5 us (17%)
  local copies, waits for them, and re-layouts  19.9 us (13%)
  starting transfers between devices  19.7 us (13%)
  waiting for transfers between devices  5.94 us (4%)
    pallas_call x3, Pallas kernels, exchange(): pl.pallas_call(functools.partial(exchange_kernel, members, axis, stride,...  49.3 us
    all_to_all x1, starting transfers between devices, shards(): lax.all_to_all(outgoing, 'dev', split_axis=0, concat_axis=0, tiled=True)  13.7 us
    convert_element_type x1, other arithmetic, local_pass(): act0 = (jax.nn.gelu(lifted, approximate=False) * mask0).astype(jnp.bfloat16)  13 us
    dot_general x1, matrix products, local_pass(): jnp.einsum('rui,io->ruo', taps, kernel, preferred_element_type=jnp.float32)  11 us
    reduce_sum x2, other arithmetic, fold(): s = jnp.sum(x, axis=1)  7.22 us
    dot_general x1, matrix products, local_pass(): jnp.einsum('ruj,rum->jm', low, patches, preferred_element_type=jnp.float32)  6.44 us
    ppermute x2, starting transfers between devices, pair_sum(): return keep + lax.ppermute(give, 'grp', pairs)  6.02 us
    all_to_all x1, waiting for transfers between devices, shards(): lax.all_to_all(outgoing, 'dev', split_axis=0, concat_axis=0, tiled=True)  5.93 us
  transfers between devices with their start and end apart: 3, of which 1 were waited for; matrix products, arithmetic and copies ran while one was open for 18% of the time, Pallas kernels for 0%

profile of v7, /device:TPU:1, one launch (start us, length us, event | category | flops | bytes accessed | tf_op | source)
XLA Modules:
  0.0 154.0 jit_solution(7123366214020423047)
XLA Ops:
  0.6 0.0 copy-start
  0.7 0.8 fusion.68
  1.5 0.7 compare_and_fusion
  2.2 1.4 gather_fusion
  3.5 0.1 bitcast_select_fusion
  3.6 0.5 broadcast.391
  4.1 0.7 reduce.8
  4.8 0.7 reshape.351
  5.5 13.7 %all-to-all-start = ((bf16[32,2,192]{2,1,0:T(2,128)(2,1)}), bf16[32,2,192]{2,1,0:T(2,128)(2,1)S(1)}, u32[]{:S(2)}, u32[]{:S(2)}) async-start(bf16[32,2,192]{2,1,0:T(2,128)(2,1)} %reshape.351), calls=%async_computation | async-start | bytes 65536 | tf_op jit(solution)/shard_map/all_to_all | solution.py:195
  19.2 0.9 dynamic-slice_reduce_fusion
  20.1 0.8 reshape.327
  20.9 0.2 select_reduce_fusion
  21.1 0.1 fusion.64
  21.2 0.1 broadcast_add_fusion
  21.3 0.8 pad_maximum_fusion.10
  22.1 5.9 %all-to-all-done = bf16[32,2,192]{2,1,0:T(2,128)(2,1)S(1)} async-done(((bf16[32,2,192]{2,1,0:T(2,128)(2,1)}), bf16[32,2,192]{2,1,0:T(2,128)(2,1)S(1)}, u32[]{:S(2)}, u32[]{:S(2)}) %all-to-all-start) | async-done | bytes 24608 | tf_op jit(solution)/shard_map/all_to_all | solution.py:195
  28.0 0.1 reshape.352
  28.1 0.1 copy.98
  28.4 0.2 copy.94
  28.5 0.2 copy.93
  28.8 0.0 copy-start.5
  28.8 1.8 %fusion.7 = (f32[32,1024]{1,0:T(8,128)S(1)}, f32[32,38,1024]{2,1,0:T(8,128)S(1)}) fusion(s32[38,1024]{1,0:T(8,128)S(1)} %broadcast_add_fusion, s32[32]{0:T(128)S(1)} %get-tuple-element.55, bf16[10,512]{1,0:T(8,128)(2,1)} %param.11, bf16[32,38,5]{1,2,0:T(8,128)(2,1)S(1)} %copy.94, bf16[32,38,10]{1,2,0:T(8,128)(2,1)S(1)} %copy.93), kind=kOutput, calls=%fused_computation.15 | convolution fusion | flops 41254144 | bytes 5314304 | tf_op jit(solution)/shard_map/rum,mc->ruc/dot_general | solution.py:124
  30.6 0.1 fusion.52
  30.7 1.5 multiply_reduce_fusion.2
  32.2 0.1 fusion.51
  32.4 13.0 %fusion.8 = bf16[32,38,1024]{2,1,0:T(8,128)(2,1)S(1)} fusion(f32[1024]{0:T(1024)S(1)} %get-tuple-element.59, f32[1024]{0:T(1024)S(1)} %get-tuple-element.58, s32[38,1024]{1,0:T(8,128)S(1)} %broadcast_add_fusion, s32[32]{0:T(128)S(1)} %get-tuple-element.55, f32[32,1024]{1,0:T(8,128)S(1)} %pad_maximum_fusion.5, f32[32,38,1024]{2,1,0:T(8,128)S(1)} %get-tuple-element.57, ...), kind=kLoop, calls=%fused_computation.16 | loop fusion | flops 89653248 | bytes 7897216 | tf_op jit(solution)/shard_map/convert_element_type | solution.py:148
  45.3 0.7 slice.129
  46.1 11.0 %fusion.27 = (bf16[32,37,512]{2,1,0:T(8,128)(2,1)S(1)}, bf16[32,37,512]{2,1,0:T(8,128)(2,1)}) fusion(bf16[32,37,512]{2,0,1:T(8,128)(2,1)S(1)} %copy-done.10, f32[32,37]{1,0:T(8,128)S(1)} %fusion.64, bf16[1536,512,1]{1,0,2:T(8,128)(2,1)S(1)} %bitcast.58, bf16[32,37,512]{2,1,0:T(8,128)(2,1)S(1)} %slice.129, bf16[32,37,1024]{2,1,0:T(8,128)(2,1)S(1)} %bitcast.60), kind=kOutput, calls=%fused_computation.52 | convolution fusion | flops 1916829696 | bytes 8852096 | tf_op jit(solution)/shard_map/rui,io->ruo/dot_general | solution.py:151
  57.1 2.3 %fusion.36 = f32[512,1536,1]{1,0,2:T(8,128)S(1)} fusion(bf16[32,37,512]{2,1,0:T(8,128)(2,1)S(1)} %get-tuple-element.48, bf16[32,37,512]{2,1,0:T(8,128)(2,1)S(1)} %slice.129, bf16[32,37,1024]{2,1,0:T(8,128)(2,1)S(1)} %bitcast.61), kind=kOutput, calls=%fused_computation.69 | convolution fusion | flops 1869545472 | bytes 7995392 | tf_op jit(solution)/shard_map/ruo,rui->oi/dot_general | solution.py:160
  59.4 2.3 %fusion.78 = f32[32,37,1536]{2,1,0:T(8,128)S(1)} fusion(bf16[32,37,512]{2,1,0:T(8,128)(2,1)S(1)} %get-tuple-element.48, bf16[1536,512,1]{1,0,2:T(8,128)(2,1)S(1)} %bitcast.59), kind=kOutput, calls=%fused_computation.155 | convolution fusion | flops 1862270976 | bytes 10059776 | tf_op jit(solution)/shard_map/ruo,io->rui/dot_general | solution.py:162
  61.6 0.2 slice.131
  61.9 0.6 slice.130
  62.6 1.3 dynamic-slice_bitcast_fusion
  63.9 4.1 %collective-permute-start = (f32[32,8,1536]{2,1,0:T(8,128)}, f32[32,8,1536]{2,1,0:T(8,128)S(1)}, u32[]{:S(2)}, u32[]{:S(2)}) collective-permute-start(f32[32,8,1536]{2,1,0:T(8,128)} %dynamic-slice_bitcast_fusion), channel_id=1, source_target_pairs={{0,32},{32,0},{64,96},{96,64},{128,160},{160,128},{192,224},{224,1... | collective-permute-start | bytes 4718600 | tf_op jit(solution)/shard_map/ppermute | solution.py:218
  68.0 5.7 %multiply_reduce_fusion.1 = (f32[32,1024]{1,0:T(8,128)S(1)}, f32[1024]{0:T(1024)S(1)}, f32[32,1024]{1,0:T(8,128)S(1)}, f32[1024]{0:T(1024)S(1)}, f32[32,38,1024]{2,1,0:T(8,128)S(1)}) fusion(f32[1024]{0:T(1024)S(1)} %get-tuple-element.58, f32[32,1024]{1,0:T(8,128)S(1)} %pad_maximum_fusion.5, f32[32,38,1024]{2,1,0:T(8,128)S(1)} %get-tuple-element.57, ...), kind=kLoop, calls=%fused_computation.19 | loop fusion | flops 29816832 | bytes 17932416 | tf_op jit(solution)/shard_map/reduce_sum | solution.py:134
  73.7 0.6 slice_add_fusion.6
  74.3 0.1 fusion.48
  74.5 2.7 %fusion.42 = f32[1024,15]{0,1:T(8,128)} fusion(bf16[32,38,5]{1,2,0:T(8,128)(2,1)S(1)} %copy.94, bf16[32,38,10]{1,2,0:T(8,128)(2,1)S(1)} %copy-done.6, f32[32,38,1024]{2,1,0:T(8,128)S(1)} %get-tuple-element.45, f32[32,1024]{1,0:T(8,128)S(1)} %pad_maximum_fusion.7, f32[32,1024]{1,0:T(8,128)S(1)} %pad_maximum_fusion.6, f32[1024]{0:T(1024)S(1)} %get-tuple-element.58, ...), kind=kOutput, calls=%fused_computation.78 | convolution fusion | flops 51125504 | bytes 10743552 | tf_op jit(solution)/shard_map/ruj,rum->jm/dot_general | solution.py:177
  77.2 0.1 add.231
  77.3 0.1 copy.85
  77.4 0.8 add.229
  78.2 0.7 copy.84
  78.9 6.4 %fusion.46 = f32[1024,15]{0,1:T(8,128)S(1)} fusion(f32[1024,15]{0,1:T(8,128)} %fusion.42, bf16[32,38,5]{1,2,0:T(8,128)(2,1)S(1)} %copy.94, bf16[32,38,10]{1,2,0:T(8,128)(2,1)} %copy-done.5, f32[32,38,1024]{2,1,0:T(8,128)} %copy-done.2, f32[32,1024]{1,0:T(8,128)} %copy-done.8, f32[32,1024]{1,0:T(8,128)} %copy-done.7, f32[1024]{0:T(1024)S(1)} %get-tuple-element.58, ...), kind=kOutput, calls=%fused_computation.80 | convolution fusion | flops 54876416 | bytes 10804992 | tf_op jit(solution)/shard_map/ruj,rum->jm/dot_general | solution.py:179
  85.3 1.2 concatenate.53
  86.6 1.1 copy.83
  87.7 0.8 copy.87
  88.5 1.9 %collective-permute-start.1 = (f32[32,8,12]{2,1,0:T(8,128)}, f32[32,8,12]{2,1,0:T(8,128)}, u32[]{:S(2)}, u32[]{:S(2)}) collective-permute-start(f32[32,8,12]{2,1,0:T(8,128)} %bitcast.16), channel_id=1, source_target_pairs={{0,32},{32,0},{64,96},{96,64},{128,160},{160,128},{192,224},{224,1... | collective-permute-start | bytes 36872 | tf_op jit(solution)/shard_map/ppermute | solution.py:218
  90.4 2.7 %copy.89 = bf16[32,37,512]{2,0,1:T(8,128)(2,1)} copy(bf16[32,37,512]{2,1,0:T(8,128)(2,1)} %get-tuple-element.49) | data formatting | bytes 2424832
  93.1 0.1 copy.86
  93.3 1.6 %bitcast_add_fusion.1.refs_1_ = f32[32,8,12]{2,1,0:T(8,128)} fusion(f32[32,8,12]{2,1,0:T(8,128)} %collective-permute-done.1, f32[32,1,8,12]{3,2,0,1:T(8,128)S(1)} %copy.86), kind=kLoop, calls=%fused_computation.86 | loop fusion | flops 3072 | bytes 36864 | tf_op jit(solution)/shard_map/add | solution.py:218
  94.8 2.5 %fusion.38.refs_0_ = bf16[32,8,1536]{2,1,0:T(8,128)(2,1)} fusion(f32[32,8,1536]{2,1,0:T(8,128)S(1)} %collective-permute-done, f32[32,2,8,1536]{3,2,1,0:T(8,128)} %bitcast.63, s32[]{:T(128)S(6)} %select_n.94), kind=kLoop, calls=%fused_computation.72 | loop fusion | flops 786432 | bytes 3932164 | tf_op jit(solution)/shard_map/convert_element_type | solution.py:220
  97.3 27.6 %shard_map.119 = (bf16[32,8,1536]{2,1,0:T(8,128)(2,1)}, f32[32,8,12]{2,1,0:T(8,128)}) custom-call(bf16[32,8,1536]{2,1,0:T(8,128)(2,1)} %fusion.38.refs_0_, f32[32,8,12]{2,1,0:T(8,128)} %bitcast_add_fusion.1.refs_1_), custom_call_target="tpu_custom_call" | custom-call | tf_op jit(solution)/shard_map/pallas_call | solution.py:81
  124.9 1.3 convert_reduce_fusion
  126.1 0.9 reduce_sum.98
  127.1 0.7 reshape.331.refs_0_
  127.7 8.7 %shard_map.120 = f32[8,1,1548]{2,1,0:T(1,128)} custom-call(f32[8,1,1548]{2,1,0:T(1,128)} %reshape.331.refs_0_), custom_call_target="tpu_custom_call" | custom-call | tf_op jit(solution)/shard_map/pallas_call | solution.py:81
  136.4 0.9 reduce_sum.99
  137.3 0.6 broadcast_in_dim.19.refs_0_
  137.9 13.1 %shard_map.121 = f32[16,1,1548]{2,1,0:T(1,128)} custom-call(f32[1,1,1548]{2,1,0:T(1,128)} %broadcast_in_dim.19.refs_0_), custom_call_target="tpu_custom_call" | custom-call | tf_op jit(solution)/shard_map/pallas_call | solution.py:81
  151.0 0.9 copy.101
  151.9 0.7 slice_reduce_fusion
  152.6 0.7 copy.91
  153.3 0.1 reshape.334
  153.3 0.7 copy.90
  (42 shorter events, 0.3 us)
Async XLA Ops:
  0.6 45.4 %copy-start = (bf16[3,512,512]{2,1,0:T(8,128)(2,1)S(1)}, bf16[3,512,512]{2,1,0:T(8,128)(2,1)}, u32[]{:S(2)}) copy-start(bf16[3,512,512]{2,1,0:T(8,128)(2,1)} %param.14) | copy-start | bytes 4718596
  5.5 22.5 %all-to-all-start = ((bf16[32,2,192]{2,1,0:T(2,128)(2,1)}), bf16[32,2,192]{2,1,0:T(2,128)(2,1)S(1)}, u32[]{:S(2)}, u32[]{:S(2)}) async-start(bf16[32,2,192]{2,1,0:T(2,128)(2,1)} %reshape.351), calls=%async_computation | async-start | bytes 65536 | tf_op jit(solution)/shard_map/all_to_all | solution.py:195
  28.8 1.8 %copy-start.5 = (bf16[32,38,10]{1,2,0:T(8,128)(2,1)}, bf16[32,38,10]{1,2,0:T(8,128)(2,1)S(1)}, u32[]{:S(2)}) copy-start(bf16[32,38,10]{1,2,0:T(8,128)(2,1)S(1)} %copy.93) | copy-start | bytes 72964
  30.6 43.9 %copy-start.1 = (f32[32,38,1024]{2,1,0:T(8,128)}, f32[32,38,1024]{2,1,0:T(8,128)S(1)}, u32[]{:S(2)}) copy-start(f32[32,38,1024]{2,1,0:T(8,128)S(1)} %get-tuple-element.57) | copy-start | bytes 14942212
  32.3 42.1 %copy-start.4 = (f32[32,1024]{1,0:T(8,128)}, f32[32,1024]{1,0:T(8,128)S(1)}, u32[]{:S(2)}) copy-start(f32[32,1024]{1,0:T(8,128)S(1)} %pad_maximum_fusion.5) | copy-start | bytes 393220
  32.4 13.7 %copy-start.10 = (bf16[32,37,512]{2,0,1:T(8,128)(2,1)S(1)}, bf16[32,37,512]{2,0,1:T(8,128)(2,1)}, u32[]{:S(2)}) copy-start(bf16[32,37,512]{2,0,1:T(8,128)(2,1)} %param.15) | copy-start | bytes 3637252
  59.4 3.2 %copy-start.3 = (f32[512,1536,1]{1,0,2:T(8,128)}, f32[512,1536,1]{1,0,2:T(8,128)S(1)}, u32[]{:S(2)}) copy-start(f32[512,1536,1]{1,0,2:T(8,128)S(1)} %fusion.36) | copy-start | bytes 9437188
  63.9 10.7 %copy-start.6 = (bf16[32,38,10]{1,2,0:T(8,128)(2,1)S(1)}, bf16[32,38,10]{1,2,0:T(8,128)(2,1)}, u32[]{:S(2)}) copy-start(bf16[32,38,10]{1,2,0:T(8,128)(2,1)} %copy-done.5) | copy-start | bytes 72964
  63.9 31.0 %collective-permute-start = (f32[32,8,1536]{2,1,0:T(8,128)}, f32[32,8,1536]{2,1,0:T(8,128)S(1)}, u32[]{:S(2)}, u32[]{:S(2)}) collective-permute-start(f32[32,8,1536]{2,1,0:T(8,128)} %dynamic-slice_bitcast_fusion), channel_id=1, source_target_pairs={{0,32},{32,0},{64,96},{96,64},{128,160},{160,128},{192,224},{224,1... | collective-permute-start | bytes 4718600 | tf_op jit(solution)/shard_map/ppermute | solution.py:218
  73.7 3.5 %copy-start.2 = (f32[32,38,1024]{2,1,0:T(8,128)}, f32[32,38,1024]{2,1,0:T(8,128)S(1)}, u32[]{:S(2)}) copy-start(f32[32,38,1024]{2,1,0:T(8,128)S(1)} %get-tuple-element.45) | copy-start | bytes 14942212
  74.4 2.7 %copy-start.7 = (f32[32,1024]{1,0:T(8,128)}, f32[32,1024]{1,0:T(8,128)S(1)}, u32[]{:S(2)}) copy-start(f32[32,1024]{1,0:T(8,128)S(1)} %pad_maximum_fusion.6) | copy-start | bytes 393220
  74.5 2.7 %copy-start.8 = (f32[32,1024]{1,0:T(8,128)}, f32[32,1024]{1,0:T(8,128)S(1)}, u32[]{:S(2)}) copy-start(f32[32,1024]{1,0:T(8,128)S(1)} %pad_maximum_fusion.7) | copy-start | bytes 393220
  78.8 8.8 %copy-start.9 = (f32[32,2,8,1]{0,2,3,1:T(8,128)S(1)}, f32[32,2,8,1]{0,2,3,1:T(8,128)}, u32[]{:S(2)}) copy-start(f32[32,2,8,1]{0,2,3,1:T(8,128)} %copy.84) | copy-start | bytes 6148
  88.5 4.8 %collective-permute-start.1 = (f32[32,8,12]{2,1,0:T(8,128)}, f32[32,8,12]{2,1,0:T(8,128)}, u32[]{:S(2)}, u32[]{:S(2)}) collective-permute-start(f32[32,8,12]{2,1,0:T(8,128)} %bitcast.16), channel_id=1, source_target_pairs={{0,32},{32,0},{64,96},{96,64},{128,160},{160,128},{192,224},{224,1... | collective-permute-start | bytes 36872 | tf_op jit(solution)/shard_map/ppermute | solution.py:218

commit v8 on v7

--- a/solution.py
+++ b/solution.py
@@ -90,6 +90,101 @@
         ],
         compiler_params=pltpu.CompilerParams(collective_id=ident, has_side_effects=True),
     )(*blocks)
+
+
+def reduce_gather_kernel(rows_y, src_ref, out_ref, stage, total, sends, recvs, shares, gets, local_sems):
+    coord = lax.axis_index("grp")
+    other = lax.axis_index("dev")
+    groups = 2 * rows_y
+    me = coord // 2
+    core = lax.rem(coord, 2)
+    barrier = pltpu.get_barrier_semaphore()
+
+    def greet(step, carry):
+        peer = lax.rem(coord + step, groups)
+        pl.semaphore_signal(barrier, inc=1, device_id=(peer, other), device_id_type=MESH)
+        return carry
+
+    lax.fori_loop(1, groups, greet, 0)
+    pl.semaphore_wait(barrier, groups - 1)
+    own = pltpu.make_async_copy(src_ref.at[me], stage.at[me], local_sems.at[0])
+    own.start()
+
+    def scatter(step, peer, src_peer, slot):
+        return pltpu.make_async_remote_copy(
+            src_ref=src_ref.at[src_peer],
+            dst_ref=stage.at[slot],
+            send_sem=sends.at[step],
+            recv_sem=recvs.at[step],
+            device_id=(peer * 2 + core, other),
+            device_id_type=MESH,
+        )
+
+    def send_part(step, carry):
+        peer = lax.rem(me + step, rows_y)
+        scatter(step, peer, peer, me).start()
+        return carry
+
+    lax.fori_loop(1, rows_y, send_part, 0)
+
+    def finish_part(step, carry):
+        peer = lax.rem(me + step, rows_y)
+        sender = lax.rem(me + rows_y - step, rows_y)
+        scatter(step, peer, peer, me).wait_send()
+        scatter(step, sender, me, sender).wait_recv()
+        return carry
+
+    lax.fori_loop(1, rows_y, finish_part, 0)
+    own.wait()
+    total[...] = jnp.sum(stage[...], axis=0)
+    mine = pltpu.make_async_copy(total, out_ref.at[coord], local_sems.at[1])
+    mine.start()
+
+    def spread(step, peer, slot):
+        return pltpu.make_async_remote_copy(
+            src_ref=total,
+            dst_ref=out_ref.at[slot],
+            send_sem=shares.at[step],
+            recv_sem=gets.at[step],
+            device_id=(peer, other),
+            device_id_type=MESH,
+        )
+
+    def send_total(step, carry):
+        spread(step, lax.rem(coord + step, groups), coord).start()
+        return carry
+
+    lax.fori_loop(1, groups, send_total, 0)
+
+    def finish_total(step, carry):
+        spread(step, lax.rem(coord + step, groups), coord).wait_send()
+        sender = lax.rem(coord + groups - step, groups)
+        spread(step, sender, sender).wait_recv()
+        return carry
+
+    lax.fori_loop(1, groups, finish_total, 0)
+    mine.wait()
+
+
+def reduce_gather(part, ident):
+    rows_y, depth, span = part.shape
+    groups = 2 * rows_y
+    return pl.pallas_call(
+        functools.partial(reduce_gather_kernel, rows_y),
+        out_shape=jax.ShapeDtypeStruct((groups, depth, span), part.dtype),
+        in_specs=[pl.BlockSpec(memory_space=pl.ANY)],
+        out_specs=pl.BlockSpec(memory_space=pl.ANY),
+        scratch_shapes=[
+            pltpu.VMEM((rows_y, depth, span), part.dtype),
+            pltpu.VMEM((depth, span), part.dtype),
+            pltpu.SemaphoreType.DMA((rows_y,)),
+            pltpu.SemaphoreType.DMA((rows_y,)),
+            pltpu.SemaphoreType.DMA((groups,)),
+            pltpu.SemaphoreType.DMA((groups,)),
+            pltpu.SemaphoreType.DMA((2,)),
+        ],
+        compiler_params=pltpu.CompilerParams(collective_id=ident, has_side_effects=True),
+    )(part)
 
 
 def gelu_slope(value):
@@ -230,11 +325,7 @@
     width = chans // members
     span = part.shape[1]
     rows_y = groups // 2
-    (scattered,) = exchange(
-        [part.reshape(rows_y, (width // 2) // rows_y, span)], rows_y, "grp", 2, False, 1
-    )
-    total = jnp.sum(scattered, axis=0)
-    (gathered,) = exchange([total[None]], groups, "grp", 1, True, 2)
+    gathered = reduce_gather(part.reshape(rows_y, (width // 2) // rows_y, span), 1)
     gathered = gathered.reshape(rows_y, 2, (width // 2) // rows_y, span)
     owned = gathered.transpose(1, 0, 2, 3).reshape(width, span)
     grad_second = (

time: 155 us -> 151 us (0.974)
  Pallas kernels: 49.3 us -> 46.5 us
    pallas_call x3 -> x1, Pallas kernels: 49.3 us -> 27.6 us  [exchange(): pl.pallas_call(functools.partial(exchange_kernel, members, axis, stride,...]
    pallas_call x0 -> x1, Pallas kernels: none -> 19 us  [reduce_gather(): pl.pallas_call(functools.partial(reduce_gather_kernel, rows_y), out_shape...]
where the time goes in v8:
time: 151 us; the launch traced here: 150 us
  Pallas kernels  46.5 us (31%)
  other arithmetic  30.7 us (20%)
  matrix products  26.5 us (18%)
  starting transfers between devices  19.7 us (13%)
  local copies, waits for them, and re-layouts  19.3 us (13%)
  waiting for transfers between devices  5.94 us (4%)
    pallas_call x1, Pallas kernels, exchange(): pl.pallas_call(functools.partial(exchange_kernel, members, axis, stride,...  27.6 us
    pallas_call x1, Pallas kernels, reduce_gather(): pl.pallas_call(functools.partial(reduce_gather_kernel, rows_y), out_shape...  19 us
    all_to_all x1, starting transfers between devices, shards(): lax.all_to_all(outgoing, 'dev', split_axis=0, concat_axis=0, tiled=True)  13.7 us
    convert_element_type x1, other arithmetic, local_pass(): act0 = (jax.nn.gelu(lifted, approximate=False) * mask0).astype(jnp.bfloat16)  13 us
    dot_general x1, matrix products, local_pass(): jnp.einsum('rui,io->ruo', taps, kernel, preferred_element_type=jnp.float32)  11 us
    reduce_sum x2, other arithmetic, fold(): s = jnp.sum(x, axis=1)  7.22 us
    dot_general x1, matrix products, local_pass(): jnp.einsum('ruj,rum->jm', low, patches, preferred_element_type=jnp.float32)  6.44 us
    ppermute x2, starting transfers between devices, pair_sum(): return keep + lax.ppermute(give, 'grp', pairs)  6.02 us
  transfers between devices with their start and end apart: 3, of which 1 were waited for; matrix products, arithmetic and copies ran while one was open for 18% of the time, Pallas kernels for 0%

profile of v8, /device:TPU:1, one launch (start us, length us, event | category | flops | bytes accessed | tf_op | source)
XLA Modules:
  0.0 149.8 jit_solution(16718617376984279133)
XLA Ops:
  0.6 0.0 copy-start
  0.7 0.8 fusion.68
  1.5 0.7 compare_and_fusion
  2.2 1.4 gather_fusion
  3.5 0.1 bitcast_select_fusion
  3.6 0.5 broadcast.391
  4.1 0.7 reduce.7
  4.8 0.7 reshape.349
  5.5 13.7 %all-to-all-start = ((bf16[32,2,192]{2,1,0:T(2,128)(2,1)}), bf16[32,2,192]{2,1,0:T(2,128)(2,1)S(1)}, u32[]{:S(2)}, u32[]{:S(2)}) async-start(bf16[32,2,192]{2,1,0:T(2,128)(2,1)} %reshape.349), calls=%async_computation | async-start | bytes 65536 | tf_op jit(solution)/shard_map/all_to_all | solution.py:290
  19.2 0.9 dynamic-slice_reduce_fusion
  20.1 0.8 reshape.325
  20.9 0.2 select_reduce_fusion
  21.1 0.1 fusion.64
  21.2 0.1 broadcast_add_fusion
  21.3 0.8 pad_maximum_fusion.10
  22.1 5.9 %all-to-all-done = bf16[32,2,192]{2,1,0:T(2,128)(2,1)S(1)} async-done(((bf16[32,2,192]{2,1,0:T(2,128)(2,1)}), bf16[32,2,192]{2,1,0:T(2,128)(2,1)S(1)}, u32[]{:S(2)}, u32[]{:S(2)}) %all-to-all-start) | async-done | bytes 24608 | tf_op jit(solution)/shard_map/all_to_all | solution.py:290
  28.0 0.1 reshape.350
  28.1 0.1 copy.98
  28.4 0.2 copy.94
  28.5 0.2 copy.93
  28.8 0.0 copy-start.5
  28.8 1.8 %fusion.7 = (f32[32,1024]{1,0:T(8,128)S(1)}, f32[32,38,1024]{2,1,0:T(8,128)S(1)}) fusion(s32[38,1024]{1,0:T(8,128)S(1)} %broadcast_add_fusion, s32[32]{0:T(128)S(1)} %get-tuple-element.55, bf16[10,512]{1,0:T(8,128)(2,1)} %param.11, bf16[32,38,5]{1,2,0:T(8,128)(2,1)S(1)} %copy.94, bf16[32,38,10]{1,2,0:T(8,128)(2,1)S(1)} %copy.93), kind=kOutput, calls=%fused_computation.15 | convolution fusion | flops 41254144 | bytes 5314304 | tf_op jit(solution)/shard_map/rum,mc->ruc/dot_general | solution.py:219
  30.6 0.1 fusion.52
  30.7 1.5 %multiply_reduce_fusion.2 = f32[32,1024]{1,0:T(8,128)S(1)} fusion(f32[32,38,1024]{2,1,0:T(8,128)S(1)} %get-tuple-element.57, f32[32,1024]{1,0:T(8,128)S(1)} %pad_maximum_fusion.4, s32[38,1024]{1,0:T(8,128)S(1)} %broadcast_add_fusion, s32[32]{0:T(128)S(1)} %get-tuple-element.55), kind=kLoop, calls=%fused_computation.34 | loop fusion | flops 6193152 | bytes 5398656 | tf_op jit(solution)/shard_map/reduce_sum | solution.py:229
  32.2 0.1 fusion.51
  32.4 0.0 copy-start.10
  32.4 13.0 %fusion.8 = bf16[32,38,1024]{2,1,0:T(8,128)(2,1)S(1)} fusion(f32[1024]{0:T(1024)S(1)} %get-tuple-element.59, f32[1024]{0:T(1024)S(1)} %get-tuple-element.58, s32[38,1024]{1,0:T(8,128)S(1)} %broadcast_add_fusion, s32[32]{0:T(128)S(1)} %get-tuple-element.55, f32[32,1024]{1,0:T(8,128)S(1)} %pad_maximum_fusion.5, f32[32,38,1024]{2,1,0:T(8,128)S(1)} %get-tuple-element.57, ...), kind=kLoop, calls=%fused_computation.16 | loop fusion | flops 89653248 | bytes 7897216 | tf_op jit(solution)/shard_map/convert_element_type | solution.py:243
  45.3 0.7 slice.129
  46.1 11.0 %fusion.27 = (bf16[32,37,512]{2,1,0:T(8,128)(2,1)S(1)}, bf16[32,37,512]{2,1,0:T(8,128)(2,1)}) fusion(bf16[32,37,512]{2,0,1:T(8,128)(2,1)S(1)} %copy-done.10, f32[32,37]{1,0:T(8,128)S(1)} %fusion.64, bf16[1536,512,1]{1,0,2:T(8,128)(2,1)S(1)} %bitcast.58, bf16[32,37,512]{2,1,0:T(8,128)(2,1)S(1)} %slice.129, bf16[32,37,1024]{2,1,0:T(8,128)(2,1)S(1)} %bitcast.60), kind=kOutput, calls=%fused_computation.52 | convolution fusion | flops 1916829696 | bytes 8852096 | tf_op jit(solution)/shard_map/rui,io->ruo/dot_general | solution.py:246
  57.1 2.3 %fusion.36 = f32[512,1536,1]{1,0,2:T(8,128)S(1)} fusion(bf16[32,37,512]{2,1,0:T(8,128)(2,1)S(1)} %get-tuple-element.48, bf16[32,37,512]{2,1,0:T(8,128)(2,1)S(1)} %slice.129, bf16[32,37,1024]{2,1,0:T(8,128)(2,1)S(1)} %bitcast.61), kind=kOutput, calls=%fused_computation.69 | convolution fusion | flops 1869545472 | bytes 7995392 | tf_op jit(solution)/shard_map/ruo,rui->oi/dot_general | solution.py:255
  59.4 2.3 %fusion.78 = f32[32,37,1536]{2,1,0:T(8,128)S(1)} fusion(bf16[32,37,512]{2,1,0:T(8,128)(2,1)S(1)} %get-tuple-element.48, bf16[1536,512,1]{1,0,2:T(8,128)(2,1)S(1)} %bitcast.59), kind=kOutput, calls=%fused_computation.155 | convolution fusion | flops 1862270976 | bytes 10059776 | tf_op jit(solution)/shard_map/ruo,io->rui/dot_general | solution.py:257
  61.6 0.2 slice.131
  61.9 0.6 slice.130
  62.6 1.3 dynamic-slice_bitcast_fusion
  63.9 4.1 %collective-permute-start = (f32[32,8,1536]{2,1,0:T(8,128)}, f32[32,8,1536]{2,1,0:T(8,128)S(1)}, u32[]{:S(2)}, u32[]{:S(2)}) collective-permute-start(f32[32,8,1536]{2,1,0:T(8,128)} %dynamic-slice_bitcast_fusion), channel_id=1, source_target_pairs={{0,32},{32,0},{64,96},{96,64},{128,160},{160,128},{192,224},{224,1... | collective-permute-start | bytes 4718600 | tf_op jit(solution)/shard_map/ppermute | solution.py:313
  68.0 5.7 %multiply_reduce_fusion.1 = (f32[32,1024]{1,0:T(8,128)S(1)}, f32[1024]{0:T(1024)S(1)}, f32[32,1024]{1,0:T(8,128)S(1)}, f32[1024]{0:T(1024)S(1)}, f32[32,38,1024]{2,1,0:T(8,128)S(1)}) fusion(f32[1024]{0:T(1024)S(1)} %get-tuple-element.58, f32[32,1024]{1,0:T(8,128)S(1)} %pad_maximum_fusion.5, f32[32,38,1024]{2,1,0:T(8,128)S(1)} %get-tuple-element.57, ...), kind=kLoop, calls=%fused_computation.19 | loop fusion | flops 29816832 | bytes 17932416 | tf_op jit(solution)/shard_map/reduce_sum | solution.py:229
  73.7 0.6 slice_add_fusion.6
  74.3 0.1 fusion.48
  74.5 2.7 %fusion.42 = f32[1024,15]{0,1:T(8,128)} fusion(bf16[32,38,5]{1,2,0:T(8,128)(2,1)S(1)} %copy.94, bf16[32,38,10]{1,2,0:T(8,128)(2,1)S(1)} %copy-done.6, f32[32,38,1024]{2,1,0:T(8,128)S(1)} %get-tuple-element.45, f32[32,1024]{1,0:T(8,128)S(1)} %pad_maximum_fusion.7, f32[32,1024]{1,0:T(8,128)S(1)} %pad_maximum_fusion.6, f32[1024]{0:T(1024)S(1)} %get-tuple-element.58, ...), kind=kOutput, calls=%fused_computation.78 | convolution fusion | flops 51125504 | bytes 10743552 | tf_op jit(solution)/shard_map/ruj,rum->jm/dot_general | solution.py:272
  77.2 0.1 add.231
  77.3 0.1 copy.85
  77.4 0.8 add.229
  78.2 0.7 copy.84
  78.9 6.4 %fusion.46 = f32[1024,15]{0,1:T(8,128)S(1)} fusion(f32[1024,15]{0,1:T(8,128)} %fusion.42, bf16[32,38,5]{1,2,0:T(8,128)(2,1)S(1)} %copy.94, bf16[32,38,10]{1,2,0:T(8,128)(2,1)} %copy-done.5, f32[32,38,1024]{2,1,0:T(8,128)} %copy-done.2, f32[32,1024]{1,0:T(8,128)} %copy-done.8, f32[32,1024]{1,0:T(8,128)} %copy-done.7, f32[1024]{0:T(1024)S(1)} %get-tuple-element.58, ...), kind=kOutput, calls=%fused_computation.80 | convolution fusion | flops 54876416 | bytes 10804992 | tf_op jit(solution)/shard_map/ruj,rum->jm/dot_general | solution.py:274
  85.3 1.2 concatenate.53
  86.6 1.1 copy.83
  87.7 0.8 copy.87
  88.5 1.9 %collective-permute-start.1 = (f32[32,8,12]{2,1,0:T(8,128)}, f32[32,8,12]{2,1,0:T(8,128)}, u32[]{:S(2)}, u32[]{:S(2)}) collective-permute-start(f32[32,8,12]{2,1,0:T(8,128)} %bitcast.16), channel_id=1, source_target_pairs={{0,32},{32,0},{64,96},{96,64},{128,160},{160,128},{192,224},{224,1... | collective-permute-start | bytes 36872 | tf_op jit(solution)/shard_map/ppermute | solution.py:313
  90.4 2.7 %copy.89 = bf16[32,37,512]{2,0,1:T(8,128)(2,1)} copy(bf16[32,37,512]{2,1,0:T(8,128)(2,1)} %get-tuple-element.49) | data formatting | bytes 2424832
  93.1 0.1 copy.86
  93.3 0.0 collective-permute-done.1
  93.3 1.6 %bitcast_add_fusion.1.refs_1_ = f32[32,8,12]{2,1,0:T(8,128)} fusion(f32[32,8,12]{2,1,0:T(8,128)} %collective-permute-done.1, f32[32,1,8,12]{3,2,0,1:T(8,128)S(1)} %copy.86), kind=kLoop, calls=%fused_computation.86 | loop fusion | flops 3072 | bytes 36864 | tf_op jit(solution)/shard_map/add | solution.py:313
  94.8 0.0 collective-permute-done
  94.8 2.5 %fusion.38.refs_0_ = bf16[32,8,1536]{2,1,0:T(8,128)(2,1)} fusion(f32[32,8,1536]{2,1,0:T(8,128)S(1)} %collective-permute-done, f32[32,2,8,1536]{3,2,1,0:T(8,128)} %bitcast.63, s32[]{:T(128)S(6)} %select_n.94), kind=kLoop, calls=%fused_computation.72 | loop fusion | flops 786432 | bytes 3932164 | tf_op jit(solution)/shard_map/convert_element_type | solution.py:315
  97.3 27.6 %shard_map.119 = (bf16[32,8,1536]{2,1,0:T(8,128)(2,1)}, f32[32,8,12]{2,1,0:T(8,128)}) custom-call(bf16[32,8,1536]{2,1,0:T(8,128)(2,1)} %fusion.38.refs_0_, f32[32,8,12]{2,1,0:T(8,128)} %bitcast_add_fusion.1.refs_1_), custom_call_target="tpu_custom_call" | custom-call | tf_op jit(solution)/shard_map/pallas_call | solution.py:81
  124.9 1.3 convert_reduce_fusion
  126.1 0.9 reduce_sum.89
  127.1 0.7 reshape.329.src_ref
  127.7 19.0 %shard_map.120 = f32[16,1,1548]{2,1,0:T(1,128)} custom-call(f32[8,1,1548]{2,1,0:T(1,128)} %reshape.329.src_ref), custom_call_target="tpu_custom_call" | custom-call | tf_op jit(solution)/shard_map/pallas_call | solution.py:172
  146.7 0.9 copy.101
  147.6 0.7 slice_reduce_fusion
  148.3 0.7 copy.91
  149.0 0.1 reshape.332
  149.1 0.7 copy.90
  (39 shorter events, 0.3 us)
Async XLA Ops:
  0.6 45.4 %copy-start = (bf16[3,512,512]{2,1,0:T(8,128)(2,1)S(1)}, bf16[3,512,512]{2,1,0:T(8,128)(2,1)}, u32[]{:S(2)}) copy-start(bf16[3,512,512]{2,1,0:T(8,128)(2,1)} %param.14) | copy-start | bytes 4718596
  5.5 22.5 %all-to-all-start = ((bf16[32,2,192]{2,1,0:T(2,128)(2,1)}), bf16[32,2,192]{2,1,0:T(2,128)(2,1)S(1)}, u32[]{:S(2)}, u32[]{:S(2)}) async-start(bf16[32,2,192]{2,1,0:T(2,128)(2,1)} %reshape.349), calls=%async_computation | async-start | bytes 65536 | tf_op jit(solution)/shard_map/all_to_all | solution.py:290
  28.8 1.8 %copy-start.5 = (bf16[32,38,10]{1,2,0:T(8,128)(2,1)}, bf16[32,38,10]{1,2,0:T(8,128)(2,1)S(1)}, u32[]{:S(2)}) copy-start(bf16[32,38,10]{1,2,0:T(8,128)(2,1)S(1)} %copy.93) | copy-start | bytes 72964
  30.6 43.9 %copy-start.1 = (f32[32,38,1024]{2,1,0:T(8,128)}, f32[32,38,1024]{2,1,0:T(8,128)S(1)}, u32[]{:S(2)}) copy-start(f32[32,38,1024]{2,1,0:T(8,128)S(1)} %get-tuple-element.57) | copy-start | bytes 14942212
  32.3 42.1 %copy-start.4 = (f32[32,1024]{1,0:T(8,128)}, f32[32,1024]{1,0:T(8,128)S(1)}, u32[]{:S(2)}) copy-start(f32[32,1024]{1,0:T(8,128)S(1)} %pad_maximum_fusion.5) | copy-start | bytes 393220
  32.4 13.7 %copy-start.10 = (bf16[32,37,512]{2,0,1:T(8,128)(2,1)S(1)}, bf16[32,37,512]{2,0,1:T(8,128)(2,1)}, u32[]{:S(2)}) copy-start(bf16[32,37,512]{2,0,1:T(8,128)(2,1)} %param.15) | copy-start | bytes 3637252
  59.4 3.2 %copy-start.3 = (f32[512,1536,1]{1,0,2:T(8,128)}, f32[512,1536,1]{1,0,2:T(8,128)S(1)}, u32[]{:S(2)}) copy-start(f32[512,1536,1]{1,0,2:T(8,128)S(1)} %fusion.36) | copy-start | bytes 9437188
  63.9 10.7 %copy-start.6 = (bf16[32,38,10]{1,2,0:T(8,128)(2,1)S(1)}, bf16[32,38,10]{1,2,0:T(8,128)(2,1)}, u32[]{:S(2)}) copy-start(bf16[32,38,10]{1,2,0:T(8,128)(2,1)} %copy-done.5) | copy-start | bytes 72964
  63.9 31.0 %collective-permute-start = (f32[32,8,1536]{2,1,0:T(8,128)}, f32[32,8,1536]{2,1,0:T(8,128)S(1)}, u32[]{:S(2)}, u32[]{:S(2)}) collective-permute-start(f32[32,8,1536]{2,1,0:T(8,128)} %dynamic-slice_bitcast_fusion), channel_id=1, source_target_pairs={{0,32},{32,0},{64,96},{96,64},{128,160},{160,128},{192,224},{224,1... | collective-permute-start | bytes 4718600 | tf_op jit(solution)/shard_map/ppermute | solution.py:313
  73.7 3.5 %copy-start.2 = (f32[32,38,1024]{2,1,0:T(8,128)}, f32[32,38,1024]{2,1,0:T(8,128)S(1)}, u32[]{:S(2)}) copy-start(f32[32,38,1024]{2,1,0:T(8,128)S(1)} %get-tuple-element.45) | copy-start | bytes 14942212
  74.4 2.7 %copy-start.7 = (f32[32,1024]{1,0:T(8,128)}, f32[32,1024]{1,0:T(8,128)S(1)}, u32[]{:S(2)}) copy-start(f32[32,1024]{1,0:T(8,128)S(1)} %pad_maximum_fusion.6) | copy-start | bytes 393220
  74.5 2.7 %copy-start.8 = (f32[32,1024]{1,0:T(8,128)}, f32[32,1024]{1,0:T(8,128)S(1)}, u32[]{:S(2)}) copy-start(f32[32,1024]{1,0:T(8,128)S(1)} %pad_maximum_fusion.7) | copy-start | bytes 393220
  78.8 8.8 %copy-start.9 = (f32[32,2,8,1]{0,2,3,1:T(8,128)S(1)}, f32[32,2,8,1]{0,2,3,1:T(8,128)}, u32[]{:S(2)}) copy-start(f32[32,2,8,1]{0,2,3,1:T(8,128)} %copy.84) | copy-start | bytes 6148
  88.5 4.8 %collective-permute-start.1 = (f32[32,8,12]{2,1,0:T(8,128)}, f32[32,8,12]{2,1,0:T(8,128)}, u32[]{:S(2)}, u32[]{:S(2)}) collective-permute-start(f32[32,8,12]{2,1,0:T(8,128)} %bitcast.16), channel_id=1, source_target_pairs={{0,32},{32,0},{64,96},{96,64},{128,160},{160,128},{192,224},{224,1... | collective-permute-start | bytes 36872 | tf_op jit(solution)/shard_map/ppermute | solution.py:313

commit v9 on v8

--- a/solution.py
+++ b/solution.py
@@ -192,6 +192,10 @@
         0.5 * (1.0 + lax.erf(value * 0.7071067811865476))
         + value * jnp.exp(-0.5 * value * value) * 0.3989422804014327
     )
+
+
+def slope_from(value, cdf):
+    return cdf + value * jnp.exp(-0.5 * value * value) * 0.3989422804014327
 
 
 def local_pass(wave, lens, w_first, norm_gain, norm_bias, w_second, cot):
@@ -240,7 +244,8 @@
     gain2 = jnp.concatenate([norm_gain, norm_gain])
     bias2 = jnp.concatenate([norm_bias, norm_bias])
     lifted = normed * gain2 + bias2
-    act0 = (jax.nn.gelu(lifted, approximate=False) * mask0).astype(jnp.bfloat16)
+    cdf0 = 0.5 * (1.0 + lax.erf(lifted * 0.7071067811865476))
+    act0 = (lifted * cdf0 * mask0).astype(jnp.bfloat16)
     taps = jnp.concatenate([act0[:, :frames1], act0[:, 1 : frames1 + 1, :chans]], axis=2)
     kernel = w_second.reshape(taps_second * chans, chans)
     pre1 = jnp.einsum("rui,io->ruo", taps, kernel, preferred_element_type=jnp.float32)
@@ -248,8 +253,9 @@
     mask1 = (jnp.arange(frames1, dtype=jnp.int32)[None, :] < valid1[:, None]).astype(jnp.float32)[
         :, :, None
     ]
-    features = (jax.nn.gelu(pre1, approximate=False) * mask1).astype(jnp.bfloat16)
-    grad1 = (cot.astype(jnp.float32) * gelu_slope(pre1) * mask1).astype(jnp.bfloat16)
+    cdf1 = 0.5 * (1.0 + lax.erf(pre1 * 0.7071067811865476))
+    features = (pre1 * cdf1 * mask1).astype(jnp.bfloat16)
+    grad1 = (cot.astype(jnp.float32) * slope_from(pre1, cdf1) * mask1).astype(jnp.bfloat16)
     members = lax.axis_size("dev")
     width = chans // members
     grad_kernel = jnp.einsum("ruo,rui->oi", grad1, taps, preferred_element_type=jnp.float32)
@@ -258,7 +264,7 @@
     dact0 = jnp.pad(back[:, :, : 2 * chans], ((0, 0), (0, pairs - frames1), (0, 0))) + jnp.pad(
         back[:, :, 2 * chans :], ((0, 0), (1, pairs - frames1 - 1), (0, chans))
     )
-    dlift = dact0 * gelu_slope(lifted) * mask0
+    dlift = dact0 * slope_from(lifted, cdf0) * mask0
     gain_terms = jnp.sum(dlift * normed, axis=(0, 1))
     bias_terms = jnp.sum(dlift, axis=(0, 1))
     grad_gain = gain_terms[:chans] + gain_terms[chans:]
@@ -287,7 +293,8 @@
     own_order = lax.dynamic_index_in_dim(order, member, 0, keepdims=False)
     dealt = own_order.reshape(share, members).T.reshape(rows)
     outgoing = jnp.take(wave, dealt, axis=0)
-    arrived = lax.all_to_all(outgoing, "dev", split_axis=0, concat_axis=0, tiled=True)
+    (arrived,) = exchange([outgoing.reshape(members, share, -1)], members, "dev", 1, False, 3)
+    arrived = arrived.reshape(rows, -1)
     picks = lax.dynamic_index_in_dim(
         order.reshape(members, share, members), member, 2, keepdims=False
     )

time: 151 us -> 139 us (0.921)
  Pallas kernels: 46.5 us -> 66.3 us
  starting transfers between devices: 19.7 us -> 5.56 us
  other arithmetic: 30.7 us -> 18.5 us
  waiting for transfers between devices: 5.94 us -> 0.01 us
  local copies, waits for them, and re-layouts: 19.3 us -> 23.5 us
  matrix products: 26.5 us -> 23.6 us
    pallas_call x1 -> x2, Pallas kernels: 27.6 us -> 46.5 us  [exchange(): pl.pallas_call(functools.partial(exchange_kernel, members, axis, stride,...]
    all_to_all x1 -> x0, starting transfers between devices: 13.7 us -> none  [shards(): lax.all_to_all(outgoing, 'dev', split_axis=0, concat_axis=0, tiled=True)]
    convert_element_type x1, other arithmetic: 13 us -> 2.46 us  [local_pass(): act0 = (lifted * cdf0 * mask0).astype(jnp.bfloat16)]
    all_to_all x1 -> x0, waiting for transfers between devices: 5.93 us -> none  [shards(): lax.all_to_all(outgoing, 'dev', split_axis=0, concat_axis=0, tiled=True)]
    dot_general x1, matrix products: 11 us -> 5.22 us  [local_pass(): jnp.einsum('rui,io->ruo', taps, kernel, preferred_element_type=jnp.float32)]
    unnamed x30 -> x38, local copies, waits for them, and re-layouts: 5.49 us -> 8.87 us
    dot_general x1, matrix products: 2.3 us -> 3.99 us  [local_pass(): jnp.einsum('ruo,rui->oi', grad1, taps, preferred_element_type=jnp.float32)]
  transfers between devices with their start and end apart: 3 -> 2, of which waited for: 1 -> 0; matrix products, arithmetic and copies ran while one was open for 18% -> 20% of each run, Pallas kernels for 0% -> 0%
where the time goes in v9:
time: 139 us
  Pallas kernels  66.3 us (48%)
  matrix products  23.6 us (17%)
  local copies, waits for them, and re-layouts  23.5 us (17%)
  other arithmetic  18.5 us (13%)
  starting transfers between devices  5.56 us (4%)
    pallas_call x2, Pallas kernels, exchange(): pl.pallas_call(functools.partial(exchange_kernel, members, axis, stride,...  46.5 us
    pallas_call x1, Pallas kernels, reduce_gather(): pl.pallas_call(functools.partial(reduce_gather_kernel, rows_y), out_shape...  19.8 us
    unnamed x38, local copies, waits for them, and re-layouts  8.87 us
    reduce_sum x2, other arithmetic, fold(): s = jnp.sum(x, axis=1)  7.13 us
    dot_general x1, matrix products, local_pass(): jnp.einsum('ruj,rum->jm', low, patches, preferred_element_type=jnp.float32)  6.44 us
    ppermute x2, starting transfers between devices, pair_sum(): return keep + lax.ppermute(give, 'grp', pairs)  5.56 us
    dot_general x1, matrix products, local_pass(): jnp.einsum('rui,io->ruo', taps, kernel, preferred_element_type=jnp.float32)  5.22 us
    dot_general x1, matrix products, local_pass(): jnp.einsum('ruo,rui->oi', grad1, taps, preferred_element_type=jnp.float32)  3.99 us
  transfers between devices with their start and end apart: 2, of which 0 were waited for; matrix products, arithmetic and copies ran while one was open for 20% of the time, Pallas kernels for 0%

profile of v9, /device:TPU:1, one launch (start us, length us, event | category | flops | bytes accessed | tf_op | source)
XLA Modules:
  0.0 138.6 jit_solution(17909567062542242665)
XLA Ops:
  0.6 0.0 copy-start
  0.7 0.8 fusion.48
  1.5 0.7 compare_and_fusion
  2.2 0.9 dynamic-slice_reduce_fusion
  3.1 1.4 gather_fusion
  4.5 0.7 broadcast_select_fusion.refs_0_
  5.2 19.0 %shard_map.119 = bf16[32,1,384]{2,1,0:T(2,128)(2,1)} custom-call(bf16[32,1,384]{2,1,0:T(2,128)(2,1)} %broadcast_select_fusion.refs_0_), custom_call_target="tpu_custom_call" | custom-call | tf_op jit(solution)/shard_map/pallas_call | solution.py:81
  24.2 0.9 copy.86
  25.3 0.8 reshape.327
  26.0 0.2 select_reduce_fusion
  26.3 0.1 fusion.44
  26.3 0.2 copy.82
  26.5 0.2 copy.81
  26.8 0.1 broadcast_add_fusion
  26.9 0.0 copy-start.10
  26.9 0.0 copy-start.11
  26.9 1.8 %fusion.5 = (f32[32,1024]{1,0:T(8,128)S(1)}, f32[32,38,1024]{2,1,0:T(8,128)S(1)}) fusion(s32[38,1024]{1,0:T(8,128)S(1)} %broadcast_add_fusion, s32[32]{0:T(128)S(1)} %get-tuple-element.50, bf16[10,512]{1,0:T(8,128)(2,1)} %param.11, bf16[32,38,5]{1,2,0:T(8,128)(2,1)S(1)} %copy.82, bf16[32,38,10]{1,2,0:T(8,128)(2,1)S(1)} %copy.81), kind=kOutput, calls=%fused_computation.12 | convolution fusion | flops 41254144 | bytes 5314304 | tf_op jit(solution)/shard_map/rum,mc->ruc/dot_general | solution.py:223
  28.7 0.1 fusion.32
  28.8 1.4 %multiply_reduce_fusion.2 = f32[32,1024]{1,0:T(8,128)S(1)} fusion(f32[32,38,1024]{2,1,0:T(8,128)S(1)} %get-tuple-element.52, f32[32,1024]{1,0:T(8,128)S(1)} %pad_maximum_fusion.4, s32[38,1024]{1,0:T(8,128)S(1)} %broadcast_add_fusion, s32[32]{0:T(128)S(1)} %get-tuple-element.50), kind=kLoop, calls=%fused_computation.19 | loop fusion | flops 6193152 | bytes 5398656 | tf_op jit(solution)/shard_map/reduce_sum | solution.py:233
  30.2 0.1 fusion.31
  30.3 0.0 copy-start.3
  30.4 0.7 copy-done.3
  31.1 2.5 %fusion.6 = bf16[32,38,1024]{2,1,0:T(8,128)(2,1)S(1)} fusion(f32[1024]{0:T(1024)S(1)} %get-tuple-element.54, f32[1024]{0:T(1024)S(1)} %get-tuple-element.53, s32[38,1024]{1,0:T(8,128)S(1)} %broadcast_add_fusion, s32[32]{0:T(128)S(1)} %get-tuple-element.50, f32[32,1024]{1,0:T(8,128)S(1)} %pad_maximum_fusion.5, f32[32,38,1024]{2,1,0:T(8,128)S(1)} %get-tuple-element.52, ...), kind=kLoop, calls=%fused_computation.13 | loop fusion | flops 14942208 | bytes 7897216 | tf_op jit(solution)/shard_map/convert_element_type | solution.py:248
  33.5 0.7 slice.129
  34.3 5.2 %fusion.14 = (bf16[32,37,512]{2,1,0:T(8,128)(2,1)S(1)}, bf16[32,37,512]{2,1,0:T(8,128)(2,1)}) fusion(bf16[32,37,512]{2,0,1:T(8,128)(2,1)S(1)} %copy-done.12, f32[32,37]{1,0:T(8,128)S(1)} %fusion.44, bf16[1536,512,1]{1,0,2:T(8,128)(2,1)S(1)} %bitcast.57, bf16[32,37,512]{2,1,0:T(8,128)(2,1)S(1)} %slice.129, bf16[32,37,1024]{2,1,0:T(8,128)(2,1)S(1)} %bitcast.61), kind=kOutput, calls=%fused_computation.30 | convolution fusion | flops 1878638592 | bytes 8852096 | tf_op jit(solution)/shard_map/rui,io->ruo/dot_general | solution.py:251
  39.5 1.1 copy-done.13
  40.6 4.0 %fusion.16 = f32[512,1536,1]{1,0,2:T(8,128)} fusion(bf16[32,37,512]{2,1,0:T(8,128)(2,1)S(1)} %get-tuple-element.43, bf16[32,37,512]{2,1,0:T(8,128)(2,1)S(1)} %slice.129, bf16[32,37,1024]{2,1,0:T(8,128)(2,1)S(1)} %bitcast.62), kind=kOutput, calls=%fused_computation.34 | convolution fusion | flops 1869545472 | bytes 7995392 | tf_op jit(solution)/shard_map/ruo,rui->oi/dot_general | solution.py:261
  44.6 2.7 %dynamic-slice_bitcast_fusion = f32[32,8,1536]{2,1,0:T(8,128)} fusion(f32[32,2,8,1536]{3,2,1,0:T(8,128)} %bitcast.63, s32[]{:T(128)S(6)} %select_n.95), kind=kLoop, calls=%fused_computation.39 | loop fusion | bytes 3145732 | tf_op jit(solution)/shard_map/jit(dynamic_index_in_dim)/squeeze | solution.py:319
  47.2 3.7 %collective-permute-start = (f32[32,8,1536]{2,1,0:T(8,128)}, f32[32,8,1536]{2,1,0:T(8,128)S(1)}, u32[]{:S(2)}, u32[]{:S(2)}) collective-permute-start(f32[32,8,1536]{2,1,0:T(8,128)} %dynamic-slice_bitcast_fusion), channel_id=1, source_target_pairs={{0,32},{32,0},{64,96},{96,64},{128,160},{160,128},{192,224},{224,1... | collective-permute-start | bytes 4718600 | tf_op jit(solution)/shard_map/ppermute | solution.py:320
  50.9 3.6 %fusion.58 = f32[32,37,1536]{2,1,0:T(8,128)S(1)} fusion(bf16[32,37,512]{2,1,0:T(8,128)(2,1)} %copy-done.13, bf16[1536,512,1]{1,0,2:T(8,128)(2,1)S(1)} %bitcast.58), kind=kOutput, calls=%fused_computation.120 | convolution fusion | flops 1862270976 | bytes 10059776 | tf_op jit(solution)/shard_map/ruo,io->rui/dot_general | solution.py:263
  54.5 0.2 slice.131
  54.7 0.0 slice-start.1
  54.8 0.0 copy-start.4
  54.8 0.6 slice.130
  55.4 1.3 slice-done
  56.7 0.4 slice-done.1
  57.0 5.7 %multiply_reduce_fusion.1 = (f32[32,1024]{1,0:T(8,128)S(1)}, f32[1024]{0:T(1024)S(1)}, f32[32,1024]{1,0:T(8,128)S(1)}, f32[1024]{0:T(1024)S(1)}, f32[32,38,1024]{2,1,0:T(8,128)S(1)}) fusion(f32[1024]{0:T(1024)S(1)} %get-tuple-element.53, f32[32,1024]{1,0:T(8,128)S(1)} %copy-done.4, f32[32,38,1024]{2,1,0:T(8,128)S(1)} %bitcast.60, ...), kind=kLoop, calls=%fused_computation.16 | loop fusion | flops 29816832 | bytes 17932416 | tf_op jit(solution)/shard_map/reduce_sum | solution.py:233
  62.8 0.6 slice_add_fusion.6
  63.4 0.1 fusion.28
  63.5 2.6 %fusion.22 = f32[1024,15]{0,1:T(8,128)} fusion(bf16[32,38,5]{1,2,0:T(8,128)(2,1)S(1)} %copy.82, bf16[32,38,10]{1,2,0:T(8,128)(2,1)S(1)} %copy-done.6, f32[32,38,1024]{2,1,0:T(8,128)S(1)} %get-tuple-element.40, f32[32,1024]{1,0:T(8,128)S(1)} %pad_maximum_fusion.7, f32[32,1024]{1,0:T(8,128)S(1)} %pad_maximum_fusion.6, f32[1024]{0:T(1024)S(1)} %get-tuple-element.53, ...), kind=kOutput, calls=%fused_computation.43 | convolution fusion | flops 51125504 | bytes 10743552 | tf_op jit(solution)/shard_map/ruj,rum->jm/dot_general | solution.py:278
  66.2 0.1 add.239
  66.3 0.1 copy.73
  66.4 0.8 add.237
  67.2 0.7 copy.72
  67.8 6.4 %fusion.26 = f32[1024,15]{0,1:T(8,128)S(1)} fusion(f32[1024,15]{0,1:T(8,128)} %fusion.22, bf16[32,38,5]{1,2,0:T(8,128)(2,1)S(1)} %copy.82, bf16[32,38,10]{1,2,0:T(8,128)(2,1)} %copy-done.5, f32[32,38,1024]{2,1,0:T(8,128)} %copy-done.2, f32[32,1024]{1,0:T(8,128)} %copy-done.8, f32[32,1024]{1,0:T(8,128)} %copy-done.7, f32[1024]{0:T(1024)S(1)} %get-tuple-element.53, ...), kind=kOutput, calls=%fused_computation.45 | convolution fusion | flops 54876416 | bytes 10804992 | tf_op jit(solution)/shard_map/ruj,rum->jm/dot_general | solution.py:280
  74.3 1.2 concatenate.53
  75.5 1.1 copy.71
  76.7 0.8 copy.75
  77.5 1.9 %collective-permute-start.1 = (f32[32,8,12]{2,1,0:T(8,128)}, f32[32,8,12]{2,1,0:T(8,128)S(1)}, u32[]{:S(2)}, u32[]{:S(2)}) collective-permute-start(f32[32,8,12]{2,1,0:T(8,128)} %bitcast.71), channel_id=1, source_target_pairs={{0,32},{32,0},{64,96},{96,64},{128,160},{160,128},{192,224},{224,1... | collective-permute-start | bytes 36872 | tf_op jit(solution)/shard_map/ppermute | solution.py:320
  79.4 2.7 %copy.77 = bf16[32,37,512]{2,0,1:T(8,128)(2,1)} copy(bf16[32,37,512]{2,1,0:T(8,128)(2,1)} %get-tuple-element.44) | data formatting | bytes 2424832
  82.1 0.1 copy.74
  82.3 0.7 bitcast_add_fusion.1.refs_1_
  82.9 0.0 collective-permute-done
  82.9 2.5 %fusion.18.refs_0_ = bf16[32,8,1536]{2,1,0:T(8,128)(2,1)} fusion(f32[32,8,1536]{2,1,0:T(8,128)S(1)} %collective-permute-done, f32[32,2,8,1536]{3,2,1,0:T(8,128)} %bitcast.64, s32[]{:T(128)S(6)} %select_n.94), kind=kLoop, calls=%fused_computation.37 | loop fusion | flops 786432 | bytes 3932164 | tf_op jit(solution)/shard_map/convert_element_type | solution.py:322
  85.4 27.5 %shard_map.120 = (bf16[32,8,1536]{2,1,0:T(8,128)(2,1)}, f32[32,8,12]{2,1,0:T(8,128)}) custom-call(bf16[32,8,1536]{2,1,0:T(8,128)(2,1)} %fusion.18.refs_0_, f32[32,8,12]{2,1,0:T(8,128)} %bitcast_add_fusion.1.refs_1_), custom_call_target="tpu_custom_call" | custom-call | tf_op jit(solution)/shard_map/pallas_call | solution.py:81
  112.9 1.3 convert_reduce_fusion
  114.2 0.9 reduce_sum.89
  115.1 0.7 reshape.332.src_ref
  115.8 19.8 %shard_map.121 = f32[16,1,1548]{2,1,0:T(1,128)} custom-call(f32[8,1,1548]{2,1,0:T(1,128)} %reshape.332.src_ref), custom_call_target="tpu_custom_call" | custom-call | tf_op jit(solution)/shard_map/pallas_call | solution.py:172
  135.6 0.9 copy.90
  136.5 0.7 slice_reduce_fusion
  137.2 0.7 copy.79
  137.9 0.1 reshape.335
  138.0 0.7 copy.78
  (45 shorter events, 0.3 us)
Async XLA Ops:
  0.6 33.6 %copy-start = (bf16[3,512,512]{2,1,0:T(8,128)(2,1)S(1)}, bf16[3,512,512]{2,1,0:T(8,128)(2,1)}, u32[]{:S(2)}) copy-start(bf16[3,512,512]{2,1,0:T(8,128)(2,1)} %param.14) | copy-start | bytes 4718596
  26.8 3.5 %copy-start.5 = (bf16[32,38,10]{1,2,0:T(8,128)(2,1)}, bf16[32,38,10]{1,2,0:T(8,128)(2,1)S(1)}, u32[]{:S(2)}) copy-start(bf16[32,38,10]{1,2,0:T(8,128)(2,1)S(1)} %copy.81) | copy-start | bytes 72964
  26.9 3.5 %copy-start.10 = (f32[512]{0:T(512)S(1)}, f32[512]{0:T(512)}, u32[]{:S(2)}) copy-start(f32[512]{0:T(512)} %param.12) | copy-start | bytes 6148
  26.9 3.5 %copy-start.11 = (f32[512]{0:T(512)S(1)}, f32[512]{0:T(512)}, u32[]{:S(2)}) copy-start(f32[512]{0:T(512)} %param.13) | copy-start | bytes 6148
  28.7 4.9 %copy-start.1 = (f32[32,38,1024]{2,1,0:T(8,128)}, f32[32,38,1024]{2,1,0:T(8,128)S(1)}, u32[]{:S(2)}) copy-start(f32[32,38,1024]{2,1,0:T(8,128)S(1)} %get-tuple-element.52) | copy-start | bytes 14942212
  30.3 0.7 copy-start.3
  31.1 3.2 %copy-start.12 = (bf16[32,37,512]{2,0,1:T(8,128)(2,1)S(1)}, bf16[32,37,512]{2,0,1:T(8,128)(2,1)}, u32[]{:S(2)}) copy-start(bf16[32,37,512]{2,0,1:T(8,128)(2,1)} %param.15) | copy-start | bytes 3637252
  39.5 1.1 copy-start.13
  47.2 35.7 %collective-permute-start = (f32[32,8,1536]{2,1,0:T(8,128)}, f32[32,8,1536]{2,1,0:T(8,128)S(1)}, u32[]{:S(2)}, u32[]{:S(2)}) collective-permute-start(f32[32,8,1536]{2,1,0:T(8,128)} %dynamic-slice_bitcast_fusion), channel_id=1, source_target_pairs={{0,32},{32,0},{64,96},{96,64},{128,160},{160,128},{192,224},{224,1... | collective-permute-start | bytes 4718600 | tf_op jit(solution)/shard_map/ppermute | solution.py:320
  54.5 2.2 %slice-start = ((s8[5242880]{0:T(1024)(128)(4,1)}), s8[4194304]{0:T(1024)(128)(4,1)S(1)}, s32[]{:S(2)}) async-start(s8[5242880]{0:T(1024)(128)(4,1)} %bitcast.59), calls=%async_computation | async-start | bytes 8388608
  54.7 2.3 %slice-start.1 = ((s8[5242880]{0:T(1024)(128)(4,1)}), s8[1048576]{0:T(1024)(128)(4,1)S(1)}, s32[]{:S(2)}) async-start(s8[5242880]{0:T(1024)(128)(4,1)} %bitcast.59), calls=%async_computation.1 | async-start | bytes 2097152
  54.8 2.3 %copy-start.4 = (f32[32,1024]{1,0:T(8,128)S(1)}, f32[32,1024]{1,0:T(8,128)}, u32[]{:S(2)}) copy-start(f32[32,1024]{1,0:T(8,128)} %copy-done.3) | copy-start | bytes 393220
  57.0 6.5 %copy-start.6 = (bf16[32,38,10]{1,2,0:T(8,128)(2,1)S(1)}, bf16[32,38,10]{1,2,0:T(8,128)(2,1)}, u32[]{:S(2)}) copy-start(bf16[32,38,10]{1,2,0:T(8,128)(2,1)} %copy-done.5) | copy-start | bytes 72964
  62.8 3.4 %copy-start.2 = (f32[32,38,1024]{2,1,0:T(8,128)}, f32[32,38,1024]{2,1,0:T(8,128)S(1)}, u32[]{:S(2)}) copy-start(f32[32,38,1024]{2,1,0:T(8,128)S(1)} %get-tuple-element.40) | copy-start | bytes 14942212
  63.5 2.7 %copy-start.7 = (f32[32,1024]{1,0:T(8,128)}, f32[32,1024]{1,0:T(8,128)S(1)}, u32[]{:S(2)}) copy-start(f32[32,1024]{1,0:T(8,128)S(1)} %pad_maximum_fusion.6) | copy-start | bytes 393220
  63.5 2.6 %copy-start.8 = (f32[32,1024]{1,0:T(8,128)}, f32[32,1024]{1,0:T(8,128)S(1)}, u32[]{:S(2)}) copy-start(f32[32,1024]{1,0:T(8,128)S(1)} %pad_maximum_fusion.7) | copy-start | bytes 393220
  67.8 8.8 %copy-start.9 = (f32[32,2,8,1]{0,2,3,1:T(8,128)S(1)}, f32[32,2,8,1]{0,2,3,1:T(8,128)}, u32[]{:S(2)}) copy-start(f32[32,2,8,1]{0,2,3,1:T(8,128)} %copy.72) | copy-start | bytes 6148
  77.5 4.8 %collective-permute-start.1 = (f32[32,8,12]{2,1,0:T(8,128)}, f32[32,8,12]{2,1,0:T(8,128)S(1)}, u32[]{:S(2)}, u32[]{:S(2)}) collective-permute-start(f32[32,8,12]{2,1,0:T(8,128)} %bitcast.71), channel_id=1, source_target_pairs={{0,32},{32,0},{64,96},{96,64},{128,160},{160,128},{192,224},{224,1... | collective-permute-start | bytes 36872 | tf_op jit(solution)/shard_map/ppermute | solution.py:320

commit v10 on v9

--- a/solution.py
+++ b/solution.py
@@ -276,9 +276,9 @@
     high = dpre0.astype(jnp.bfloat16)
     low = (dpre0 - high.astype(jnp.float32)).astype(jnp.bfloat16)
     grad_pair = jnp.einsum(
-        "ruj,rum->jm", high, patches, preferred_element_type=jnp.float32
-    ) + jnp.einsum("ruj,rum->jm", low, patches, preferred_element_type=jnp.float32)
-    grad_filter = grad_pair[:chans, :ker_first] + grad_pair[chans:, stride_first:]
+        "rum,ruj->mj", patches, high, preferred_element_type=jnp.float32
+    ) + jnp.einsum("rum,ruj->mj", patches, low, preferred_element_type=jnp.float32)
+    grad_filter = (grad_pair[:ker_first, :chans] + grad_pair[stride_first:, chans:]).T
     small = jnp.concatenate([grad_filter, grad_gain[:, None], grad_bias[:, None]], axis=1)
     small = small.reshape(members, 2, width // 2, small.shape[1]).transpose(1, 0, 2, 3)
     grads = (grad_kernel, small)

time: 139 us -> 140 us (level)
  no operation moved by 1% of the time
where the time goes in v10:
time: 140 us; the launch traced here: 139 us
  Pallas kernels  66.3 us (47%)
  matrix products  23.7 us (17%)
  local copies, waits for them, and re-layouts  23.5 us (17%)
  other arithmetic  18.5 us (13%)
  starting transfers between devices  5.56 us (4%)
    pallas_call x2, Pallas kernels, exchange(): pl.pallas_call(functools.partial(exchange_kernel, members, axis, stride,...  46.5 us
    pallas_call x1, Pallas kernels, reduce_gather(): pl.pallas_call(functools.partial(reduce_gather_kernel, rows_y), out_shape...  19.8 us
    unnamed x38, local copies, waits for them, and re-layouts  8.87 us
    reduce_sum x2, other arithmetic, fold(): s = jnp.sum(x, axis=1)  7.13 us
    dot_general x1, matrix products, local_pass(): jnp.einsum('rum,ruj->mj', patches, low, preferred_element_type=jnp.float32)  6.46 us
    ppermute x2, starting transfers between devices, pair_sum(): return keep + lax.ppermute(give, 'grp', pairs)  5.56 us
    dot_general x1, matrix products, local_pass(): jnp.einsum('rui,io->ruo', taps, kernel, preferred_element_type=jnp.float32)  5.22 us
    dot_general x1, matrix products, local_pass(): jnp.einsum('ruo,rui->oi', grad1, taps, preferred_element_type=jnp.float32)  3.99 us
  transfers between devices with their start and end apart: 2, of which 0 were waited for; matrix products, arithmetic and copies ran while one was open for 20% of the time, Pallas kernels for 0%

profile of v10, /device:TPU:1, one launch (start us, length us, event | category | flops | bytes accessed | tf_op | source)
XLA Modules:
  0.0 138.7 jit_solution(17223531948538461577)
XLA Ops:
  0.6 0.0 copy-start
  0.7 0.8 fusion.49
  1.5 0.7 compare_and_fusion
  2.2 0.9 dynamic-slice_reduce_fusion
  3.1 1.4 gather_fusion
  4.5 0.7 broadcast_select_fusion.refs_0_
  5.2 19.0 %shard_map.119 = bf16[32,1,384]{2,1,0:T(2,128)(2,1)} custom-call(bf16[32,1,384]{2,1,0:T(2,128)(2,1)} %broadcast_select_fusion.refs_0_), custom_call_target="tpu_custom_call" | custom-call | tf_op jit(solution)/shard_map/pallas_call | solution.py:81
  24.2 0.9 copy.86
  25.3 0.8 reshape.327
  26.0 0.2 select_reduce_fusion
  26.3 0.1 fusion.45
  26.3 0.2 copy.82
  26.5 0.2 copy.81
  26.8 0.1 broadcast_add_fusion
  26.9 0.0 copy-start.10
  26.9 0.0 copy-start.11
  26.9 1.8 %fusion.5 = (f32[32,1024]{1,0:T(8,128)S(1)}, f32[32,38,1024]{2,1,0:T(8,128)S(1)}) fusion(s32[38,1024]{1,0:T(8,128)S(1)} %broadcast_add_fusion, s32[32]{0:T(128)S(1)} %get-tuple-element.50, bf16[10,512]{1,0:T(8,128)(2,1)} %param.11, bf16[32,38,5]{1,2,0:T(8,128)(2,1)S(1)} %copy.82, bf16[32,38,10]{1,2,0:T(8,128)(2,1)S(1)} %copy.81), kind=kOutput, calls=%fused_computation.12 | convolution fusion | flops 41254144 | bytes 5314304 | tf_op jit(solution)/shard_map/rum,mc->ruc/dot_general | solution.py:223
  28.7 0.1 fusion.32
  28.8 1.4 %multiply_reduce_fusion.2 = f32[32,1024]{1,0:T(8,128)S(1)} fusion(f32[32,38,1024]{2,1,0:T(8,128)S(1)} %get-tuple-element.52, f32[32,1024]{1,0:T(8,128)S(1)} %pad_maximum_fusion.4, s32[38,1024]{1,0:T(8,128)S(1)} %broadcast_add_fusion, s32[32]{0:T(128)S(1)} %get-tuple-element.50), kind=kLoop, calls=%fused_computation.19 | loop fusion | flops 6193152 | bytes 5398656 | tf_op jit(solution)/shard_map/reduce_sum | solution.py:233
  30.2 0.1 fusion.31
  30.3 0.0 copy-start.3
  30.4 0.7 copy-done.3
  31.1 2.5 %fusion.6 = bf16[32,38,1024]{2,1,0:T(8,128)(2,1)S(1)} fusion(f32[1024]{0:T(1024)S(1)} %get-tuple-element.54, f32[1024]{0:T(1024)S(1)} %get-tuple-element.53, s32[38,1024]{1,0:T(8,128)S(1)} %broadcast_add_fusion, s32[32]{0:T(128)S(1)} %get-tuple-element.50, f32[32,1024]{1,0:T(8,128)S(1)} %pad_maximum_fusion.5, f32[32,38,1024]{2,1,0:T(8,128)S(1)} %get-tuple-element.52, ...), kind=kLoop, calls=%fused_computation.13 | loop fusion | flops 14942208 | bytes 7897216 | tf_op jit(solution)/shard_map/convert_element_type | solution.py:248
  33.5 0.7 slice.129
  34.3 5.2 %fusion.14 = (bf16[32,37,512]{2,1,0:T(8,128)(2,1)S(1)}, bf16[32,37,512]{2,1,0:T(8,128)(2,1)}) fusion(bf16[32,37,512]{2,0,1:T(8,128)(2,1)S(1)} %copy-done.12, f32[32,37]{1,0:T(8,128)S(1)} %fusion.45, bf16[1536,512,1]{1,0,2:T(8,128)(2,1)S(1)} %bitcast.59, bf16[32,37,512]{2,1,0:T(8,128)(2,1)S(1)} %slice.129, bf16[32,37,1024]{2,1,0:T(8,128)(2,1)S(1)} %bitcast.63), kind=kOutput, calls=%fused_computation.30 | convolution fusion | flops 1878638592 | bytes 8852096 | tf_op jit(solution)/shard_map/rui,io->ruo/dot_general | solution.py:251
  39.5 1.1 copy-done.13
  40.6 4.0 %fusion.16 = f32[512,1536,1]{1,0,2:T(8,128)} fusion(bf16[32,37,512]{2,1,0:T(8,128)(2,1)S(1)} %get-tuple-element.43, bf16[32,37,512]{2,1,0:T(8,128)(2,1)S(1)} %slice.129, bf16[32,37,1024]{2,1,0:T(8,128)(2,1)S(1)} %bitcast.64), kind=kOutput, calls=%fused_computation.34 | convolution fusion | flops 1869545472 | bytes 7995392 | tf_op jit(solution)/shard_map/ruo,rui->oi/dot_general | solution.py:261
  44.6 2.7 %dynamic-slice_bitcast_fusion = f32[32,8,1536]{2,1,0:T(8,128)} fusion(f32[32,2,8,1536]{3,2,1,0:T(8,128)} %bitcast.65, s32[]{:T(128)S(6)} %select_n.95), kind=kLoop, calls=%fused_computation.39 | loop fusion | bytes 3145732 | tf_op jit(solution)/shard_map/jit(dynamic_index_in_dim)/squeeze | solution.py:319
  47.2 3.7 %collective-permute-start = (f32[32,8,1536]{2,1,0:T(8,128)}, f32[32,8,1536]{2,1,0:T(8,128)S(1)}, u32[]{:S(2)}, u32[]{:S(2)}) collective-permute-start(f32[32,8,1536]{2,1,0:T(8,128)} %dynamic-slice_bitcast_fusion), channel_id=1, source_target_pairs={{0,32},{32,0},{64,96},{96,64},{128,160},{160,128},{192,224},{224,1... | collective-permute-start | bytes 4718600 | tf_op jit(solution)/shard_map/ppermute | solution.py:320
  50.9 3.6 %fusion.59 = f32[32,37,1536]{2,1,0:T(8,128)S(1)} fusion(bf16[32,37,512]{2,1,0:T(8,128)(2,1)} %copy-done.13, bf16[1536,512,1]{1,0,2:T(8,128)(2,1)S(1)} %bitcast.60), kind=kOutput, calls=%fused_computation.121 | convolution fusion | flops 1862270976 | bytes 10059776 | tf_op jit(solution)/shard_map/ruo,io->rui/dot_general | solution.py:263
  54.5 0.2 slice.131
  54.7 0.0 slice-start.1
  54.8 0.0 copy-start.4
  54.8 0.6 slice.130
  55.4 1.3 slice-done
  56.7 0.4 slice-done.1
  57.0 5.7 %multiply_reduce_fusion.1 = (f32[32,1024]{1,0:T(8,128)S(1)}, f32[1024]{0:T(1024)S(1)}, f32[32,1024]{1,0:T(8,128)S(1)}, f32[1024]{0:T(1024)S(1)}, f32[32,38,1024]{2,1,0:T(8,128)S(1)}) fusion(f32[1024]{0:T(1024)S(1)} %get-tuple-element.53, f32[32,1024]{1,0:T(8,128)S(1)} %copy-done.4, f32[32,38,1024]{2,1,0:T(8,128)S(1)} %bitcast.62, ...), kind=kLoop, calls=%fused_computation.16 | loop fusion | flops 29816832 | bytes 17932416 | tf_op jit(solution)/shard_map/reduce_sum | solution.py:233
  62.8 0.6 slice_add_fusion.6
  63.4 0.1 fusion.28
  63.5 2.7 %fusion.22 = f32[15,1024]{1,0:T(8,128)} fusion(bf16[32,38,5]{1,2,0:T(8,128)(2,1)S(1)} %copy.82, bf16[32,38,10]{1,2,0:T(8,128)(2,1)S(1)} %copy-done.6, f32[32,38,1024]{2,1,0:T(8,128)S(1)} %get-tuple-element.40, f32[32,1024]{1,0:T(8,128)S(1)} %pad_maximum_fusion.7, f32[32,1024]{1,0:T(8,128)S(1)} %pad_maximum_fusion.6, f32[1024]{0:T(1024)S(1)} %get-tuple-element.53, ...), kind=kOutput, calls=%fused_computation.43 | convolution fusion | flops 51125504 | bytes 10743552 | tf_op jit(solution)/shard_map/rum,ruj->mj/dot_general | solution.py:278
  66.2 0.1 add.239
  66.4 0.1 copy.73
  66.4 0.8 add.237
  67.2 0.7 copy.72
  67.9 6.5 %fusion.26 = f32[15,1024]{1,0:T(8,128)S(1)} fusion(f32[15,1024]{1,0:T(8,128)} %fusion.22, bf16[32,38,5]{1,2,0:T(8,128)(2,1)S(1)} %copy.82, bf16[32,38,10]{1,2,0:T(8,128)(2,1)} %copy-done.5, f32[32,38,1024]{2,1,0:T(8,128)} %copy-done.2, f32[32,1024]{1,0:T(8,128)} %copy-done.8, f32[32,1024]{1,0:T(8,128)} %copy-done.7, f32[1024]{0:T(1024)S(1)} %get-tuple-element.53, ...), kind=kOutput, calls=%fused_computation.45 | convolution fusion | flops 54876416 | bytes 10804992 | tf_op jit(solution)/shard_map/rum,ruj->mj/dot_general | solution.py:280
  74.4 1.2 concatenate.53
  75.6 1.1 copy.71
  76.8 0.8 copy.75
  77.6 1.9 %collective-permute-start.1 = (f32[32,8,12]{2,1,0:T(8,128)}, f32[32,8,12]{2,1,0:T(8,128)S(1)}, u32[]{:S(2)}, u32[]{:S(2)}) collective-permute-start(f32[32,8,12]{2,1,0:T(8,128)} %bitcast.73), channel_id=1, source_target_pairs={{0,32},{32,0},{64,96},{96,64},{128,160},{160,128},{192,224},{224,1... | collective-permute-start | bytes 36872 | tf_op jit(solution)/shard_map/ppermute | solution.py:320
  79.5 2.7 %copy.77 = bf16[32,37,512]{2,0,1:T(8,128)(2,1)} copy(bf16[32,37,512]{2,1,0:T(8,128)(2,1)} %get-tuple-element.44) | data formatting | bytes 2424832
  82.2 0.1 copy.74
  82.3 0.7 bitcast_add_fusion.1.refs_1_
  83.0 0.0 collective-permute-done
  83.0 2.5 %fusion.18.refs_0_ = bf16[32,8,1536]{2,1,0:T(8,128)(2,1)} fusion(f32[32,8,1536]{2,1,0:T(8,128)S(1)} %collective-permute-done, f32[32,2,8,1536]{3,2,1,0:T(8,128)} %bitcast.66, s32[]{:T(128)S(6)} %select_n.94), kind=kLoop, calls=%fused_computation.37 | loop fusion | flops 786432 | bytes 3932164 | tf_op jit(solution)/shard_map/convert_element_type | solution.py:322
  85.5 27.5 %shard_map.120 = (bf16[32,8,1536]{2,1,0:T(8,128)(2,1)}, f32[32,8,12]{2,1,0:T(8,128)}) custom-call(bf16[32,8,1536]{2,1,0:T(8,128)(2,1)} %fusion.18.refs_0_, f32[32,8,12]{2,1,0:T(8,128)} %bitcast_add_fusion.1.refs_1_), custom_call_target="tpu_custom_call" | custom-call | tf_op jit(solution)/shard_map/pallas_call | solution.py:81
  113.0 1.3 convert_reduce_fusion
  114.3 0.9 reduce_sum.89
  115.2 0.7 reshape.332.src_ref
  115.9 19.8 %shard_map.121 = f32[16,1,1548]{2,1,0:T(1,128)} custom-call(f32[8,1,1548]{2,1,0:T(1,128)} %reshape.332.src_ref), custom_call_target="tpu_custom_call" | custom-call | tf_op jit(solution)/shard_map/pallas_call | solution.py:172
  135.7 0.9 copy.90
  136.6 0.7 slice_reduce_fusion
  137.3 0.7 copy.79
  138.0 0.1 reshape.335
  138.1 0.7 copy.78
  (45 shorter events, 0.3 us)
Async XLA Ops:
  0.6 33.6 %copy-start = (bf16[3,512,512]{2,1,0:T(8,128)(2,1)S(1)}, bf16[3,512,512]{2,1,0:T(8,128)(2,1)}, u32[]{:S(2)}) copy-start(bf16[3,512,512]{2,1,0:T(8,128)(2,1)} %param.14) | copy-start | bytes 4718596
  26.8 3.5 %copy-start.5 = (bf16[32,38,10]{1,2,0:T(8,128)(2,1)}, bf16[32,38,10]{1,2,0:T(8,128)(2,1)S(1)}, u32[]{:S(2)}) copy-start(bf16[32,38,10]{1,2,0:T(8,128)(2,1)S(1)} %copy.81) | copy-start | bytes 72964
  26.9 3.5 %copy-start.10 = (f32[512]{0:T(512)S(1)}, f32[512]{0:T(512)}, u32[]{:S(2)}) copy-start(f32[512]{0:T(512)} %param.12) | copy-start | bytes 6148
  26.9 3.5 %copy-start.11 = (f32[512]{0:T(512)S(1)}, f32[512]{0:T(512)}, u32[]{:S(2)}) copy-start(f32[512]{0:T(512)} %param.13) | copy-start | bytes 6148
  28.7 4.9 %copy-start.1 = (f32[32,38,1024]{2,1,0:T(8,128)}, f32[32,38,1024]{2,1,0:T(8,128)S(1)}, u32[]{:S(2)}) copy-start(f32[32,38,1024]{2,1,0:T(8,128)S(1)} %get-tuple-element.52) | copy-start | bytes 14942212
  30.3 0.7 copy-start.3
  31.1 3.2 %copy-start.12 = (bf16[32,37,512]{2,0,1:T(8,128)(2,1)S(1)}, bf16[32,37,512]{2,0,1:T(8,128)(2,1)}, u32[]{:S(2)}) copy-start(bf16[32,37,512]{2,0,1:T(8,128)(2,1)} %param.15) | copy-start | bytes 3637252
  39.5 1.1 copy-start.13
  47.2 35.8 %collective-permute-start = (f32[32,8,1536]{2,1,0:T(8,128)}, f32[32,8,1536]{2,1,0:T(8,128)S(1)}, u32[]{:S(2)}, u32[]{:S(2)}) collective-permute-start(f32[32,8,1536]{2,1,0:T(8,128)} %dynamic-slice_bitcast_fusion), channel_id=1, source_target_pairs={{0,32},{32,0},{64,96},{96,64},{128,160},{160,128},{192,224},{224,1... | collective-permute-start | bytes 4718600 | tf_op jit(solution)/shard_map/ppermute | solution.py:320
  54.5 2.2 %slice-start = ((s8[5242880]{0:T(1024)(128)(4,1)}), s8[4194304]{0:T(1024)(128)(4,1)S(1)}, s32[]{:S(2)}) async-start(s8[5242880]{0:T(1024)(128)(4,1)} %bitcast.61), calls=%async_computation | async-start | bytes 8388608
  54.7 2.3 %slice-start.1 = ((s8[5242880]{0:T(1024)(128)(4,1)}), s8[1048576]{0:T(1024)(128)(4,1)S(1)}, s32[]{:S(2)}) async-start(s8[5242880]{0:T(1024)(128)(4,1)} %bitcast.61), calls=%async_computation.1 | async-start | bytes 2097152
  54.8 2.3 %copy-start.4 = (f32[32,1024]{1,0:T(8,128)S(1)}, f32[32,1024]{1,0:T(8,128)}, u32[]{:S(2)}) copy-start(f32[32,1024]{1,0:T(8,128)} %copy-done.3) | copy-start | bytes 393220
  57.0 6.5 %copy-start.6 = (bf16[32,38,10]{1,2,0:T(8,128)(2,1)S(1)}, bf16[32,38,10]{1,2,0:T(8,128)(2,1)}, u32[]{:S(2)}) copy-start(bf16[32,38,10]{1,2,0:T(8,128)(2,1)} %copy-done.5) | copy-start | bytes 72964
  62.8 3.5 %copy-start.2 = (f32[32,38,1024]{2,1,0:T(8,128)}, f32[32,38,1024]{2,1,0:T(8,128)S(1)}, u32[]{:S(2)}) copy-start(f32[32,38,1024]{2,1,0:T(8,128)S(1)} %get-tuple-element.40) | copy-start | bytes 14942212
  63.5 2.7 %copy-start.7 = (f32[32,1024]{1,0:T(8,128)}, f32[32,1024]{1,0:T(8,128)S(1)}, u32[]{:S(2)}) copy-start(f32[32,1024]{1,0:T(8,128)S(1)} %pad_maximum_fusion.6) | copy-start | bytes 393220
  63.5 2.7 %copy-start.8 = (f32[32,1024]{1,0:T(8,128)}, f32[32,1024]{1,0:T(8,128)S(1)}, u32[]{:S(2)}) copy-start(f32[32,1024]{1,0:T(8,128)S(1)} %pad_maximum_fusion.7) | copy-start | bytes 393220
  67.9 8.8 %copy-start.9 = (f32[32,2,8,1]{0,2,3,1:T(8,128)S(1)}, f32[32,2,8,1]{0,2,3,1:T(8,128)}, u32[]{:S(2)}) copy-start(f32[32,2,8,1]{0,2,3,1:T(8,128)} %copy.72) | copy-start | bytes 6148
  77.6 4.8 %collective-permute-start.1 = (f32[32,8,12]{2,1,0:T(8,128)}, f32[32,8,12]{2,1,0:T(8,128)S(1)}, u32[]{:S(2)}, u32[]{:S(2)}) collective-permute-start(f32[32,8,12]{2,1,0:T(8,128)} %bitcast.73), channel_id=1, source_target_pairs={{0,32},{32,0},{64,96},{96,64},{128,160},{160,128},{192,224},{224,1... | collective-permute-start | bytes 36872 | tf_op jit(solution)/shard_map/ppermute | solution.py:320

commit v11 on v9

--- a/solution.py
+++ b/solution.py
@@ -321,12 +321,16 @@
 
     mine_kernel = pair_sum(grad_kernel).astype(jnp.bfloat16)
     mine_small = pair_sum(small)
-    pieces_kernel, pieces_small = exchange(
-        [mine_kernel, mine_small], members, "dev", 1, False, 0
-    )
+    small_high = mine_small.astype(jnp.bfloat16)
+    small_low = (mine_small - small_high.astype(jnp.float32)).astype(jnp.bfloat16)
+    (pieces,) = exchange(
+        [jnp.concatenate([mine_kernel, small_high, small_low], axis=2)], members, "dev", 1, False, 0
+    )
+    sums = jnp.sum(pieces.astype(jnp.float32), axis=0)
+    extra = small.shape[-1]
+    lead = sums.shape[1] - 2 * extra
     part = jnp.concatenate(
-        [jnp.sum(pieces_kernel.astype(jnp.float32), axis=0), jnp.sum(pieces_small, axis=0)],
-        axis=1,
+        [sums[:, :lead], sums[:, lead : lead + extra] + sums[:, lead + extra :]], axis=1
     )
     chans = w_second.shape[2]
     width = chans // members

time: 139 us -> 137 us (0.986)
  Pallas kernels: 66.3 us -> 64.4 us
    concatenate x0 -> x1, local copies, waits for them, and re-layouts: none -> 1.79 us  [shards(): jnp.concatenate([mine_kernel, small_high, small_low], axis=2)]
    pallas_call x2, Pallas kernels: 46.5 us -> 44.7 us  [exchange(): pl.pallas_call(functools.partial(exchange_kernel, members, axis, stride,...]
    convert_element_type x0 -> x1, other arithmetic: none -> 1.56 us  [shards(): (mine_small - small_high.astype(jnp.float32)).astype(jnp.bfloat16)]
  transfers between devices with their start and end apart: 2 -> 2, of which waited for: 0 -> 0; matrix products, arithmetic and copies ran while one was open for 20% -> 21% of each run, Pallas kernels for 0% -> 0%
where the time goes in v11:
time: 137 us; the launch traced here: 136 us
  Pallas kernels  64.4 us (47%)
  matrix products  23.6 us (17%)
  local copies, waits for them, and re-layouts  23.5 us (17%)
  other arithmetic  18.2 us (13%)
  starting transfers between devices  5.58 us (4%)
    pallas_call x2, Pallas kernels, exchange(): pl.pallas_call(functools.partial(exchange_kernel, members, axis, stride,...  44.7 us
    pallas_call x1, Pallas kernels, reduce_gather(): pl.pallas_call(functools.partial(reduce_gather_kernel, rows_y), out_shape...  19.7 us
    unnamed x38, local copies, waits for them, and re-layouts  8.19 us
    reduce_sum x2, other arithmetic, fold(): s = jnp.sum(x, axis=1)  7.13 us
    dot_general x1, matrix products, local_pass(): jnp.einsum('ruj,rum->jm', low, patches, preferred_element_type=jnp.float32)  6.44 us
    ppermute x2, starting transfers between devices, pair_sum(): return keep + lax.ppermute(give, 'grp', pairs)  5.58 us
    dot_general x1, matrix products, local_pass(): jnp.einsum('rui,io->ruo', taps, kernel, preferred_element_type=jnp.float32)  5.22 us
    dot_general x1, matrix products, local_pass(): jnp.einsum('ruo,rui->oi', grad1, taps, preferred_element_type=jnp.float32)  3.99 us
  transfers between devices with their start and end apart: 2, of which 0 were waited for; matrix products, arithmetic and copies ran while one was open for 21% of the time, Pallas kernels for 0%

profile of v11, /device:TPU:1, one launch (start us, length us, event | category | flops | bytes accessed | tf_op | source)
XLA Modules:
  0.0 136.4 jit_solution(15251288857165055848)
XLA Ops:
  0.6 0.0 copy-start
  0.7 0.8 fusion.49
  1.5 0.7 compare_and_fusion
  2.2 0.9 dynamic-slice_reduce_fusion
  3.1 1.4 %gather_fusion = bf16[32,384]{1,0:T(8,128)(2,1)S(1)} fusion(bf16[32,384]{1,0:T(8,128)(2,1)} %param.8, s32[1024]{0:T(1024)S(1)} %pad_clamp_fusion), kind=kCustom, calls=%fused_computation | custom fusion | bytes 49280 | tf_op jit(solution)/shard_map/jit(_take)/gather | solution.py:295
  4.5 0.7 broadcast_select_fusion.refs_0_
  5.2 19.0 %shard_map.119 = bf16[32,1,384]{2,1,0:T(2,128)(2,1)} custom-call(bf16[32,1,384]{2,1,0:T(2,128)(2,1)} %broadcast_select_fusion.refs_0_), custom_call_target="tpu_custom_call" | custom-call | tf_op jit(solution)/shard_map/pallas_call | solution.py:81
  24.2 0.9 copy.86
  25.3 0.8 reshape.327
  26.0 0.2 select_reduce_fusion
  26.3 0.1 fusion.45
  26.3 0.2 copy.82
  26.5 0.2 copy.81
  26.8 0.1 broadcast_add_fusion
  26.9 0.0 copy-start.10
  26.9 0.0 copy-start.11
  26.9 1.8 %fusion.5 = (f32[32,1024]{1,0:T(8,128)S(1)}, f32[32,38,1024]{2,1,0:T(8,128)S(1)}) fusion(s32[38,1024]{1,0:T(8,128)S(1)} %broadcast_add_fusion, s32[32]{0:T(128)S(1)} %get-tuple-element.48, bf16[10,512]{1,0:T(8,128)(2,1)} %param.11, bf16[32,38,5]{1,2,0:T(8,128)(2,1)S(1)} %copy.82, bf16[32,38,10]{1,2,0:T(8,128)(2,1)S(1)} %copy.81), kind=kOutput, calls=%fused_computation.12 | convolution fusion | flops 41254144 | bytes 5314304 | tf_op jit(solution)/shard_map/rum,mc->ruc/dot_general | solution.py:223
  28.7 0.1 fusion.32
  28.8 1.4 %multiply_reduce_fusion.2 = f32[32,1024]{1,0:T(8,128)S(1)} fusion(f32[32,38,1024]{2,1,0:T(8,128)S(1)} %get-tuple-element.50, f32[32,1024]{1,0:T(8,128)S(1)} %pad_maximum_fusion.4, s32[38,1024]{1,0:T(8,128)S(1)} %broadcast_add_fusion, s32[32]{0:T(128)S(1)} %get-tuple-element.48), kind=kLoop, calls=%fused_computation.19 | loop fusion | flops 6193152 | bytes 5398656 | tf_op jit(solution)/shard_map/reduce_sum | solution.py:233
  30.2 0.1 fusion.31
  30.3 0.0 copy-start.3
  30.4 0.0 copy-start.12
  30.4 2.5 %fusion.6 = bf16[32,38,1024]{2,1,0:T(8,128)(2,1)S(1)} fusion(f32[1024]{0:T(1024)S(1)} %get-tuple-element.52, f32[1024]{0:T(1024)S(1)} %get-tuple-element.51, s32[38,1024]{1,0:T(8,128)S(1)} %broadcast_add_fusion, s32[32]{0:T(128)S(1)} %get-tuple-element.48, f32[32,1024]{1,0:T(8,128)S(1)} %pad_maximum_fusion.5, f32[32,38,1024]{2,1,0:T(8,128)S(1)} %get-tuple-element.50, ...), kind=kLoop, calls=%fused_computation.13 | loop fusion | flops 14942208 | bytes 7897216 | tf_op jit(solution)/shard_map/convert_element_type | solution.py:248
  32.9 0.7 slice.141
  33.6 5.2 %fusion.14 = (bf16[32,37,512]{2,1,0:T(8,128)(2,1)S(1)}, bf16[32,37,512]{2,1,0:T(8,128)(2,1)}) fusion(bf16[32,37,512]{2,0,1:T(8,128)(2,1)S(1)} %copy-done.12, f32[32,37]{1,0:T(8,128)S(1)} %fusion.45, bf16[1536,512,1]{1,0,2:T(8,128)(2,1)S(1)} %bitcast.63, bf16[32,37,512]{2,1,0:T(8,128)(2,1)S(1)} %slice.141, bf16[32,37,1024]{2,1,0:T(8,128)(2,1)S(1)} %bitcast.67), kind=kOutput, calls=%fused_computation.30 | convolution fusion | flops 1878638592 | bytes 8852096 | tf_op jit(solution)/shard_map/rui,io->ruo/dot_general | solution.py:251
  38.9 1.1 copy-done.13
  40.0 4.0 %fusion.16 = f32[512,1536,1]{1,0,2:T(8,128)} fusion(bf16[32,37,512]{2,1,0:T(8,128)(2,1)S(1)} %get-tuple-element.39, bf16[32,37,512]{2,1,0:T(8,128)(2,1)S(1)} %slice.141, bf16[32,37,1024]{2,1,0:T(8,128)(2,1)S(1)} %bitcast.68), kind=kOutput, calls=%fused_computation.34 | convolution fusion | flops 1869545472 | bytes 7995392 | tf_op jit(solution)/shard_map/ruo,rui->oi/dot_general | solution.py:261
  43.9 1.5 %dynamic-slice_bitcast_fusion = f32[32,8,1536]{2,1,0:T(8,128)S(1)} fusion(f32[32,2,8,1536]{3,2,1,0:T(8,128)} %bitcast.69, s32[]{:T(128)S(6)} %select_n.95), kind=kLoop, calls=%fused_computation.39 | loop fusion | bytes 3145732 | tf_op jit(solution)/shard_map/jit(dynamic_index_in_dim)/squeeze | solution.py:319
  45.5 3.7 %collective-permute-start = (f32[32,8,1536]{2,1,0:T(8,128)S(1)}, f32[32,8,1536]{2,1,0:T(8,128)}, u32[]{:S(2)}, u32[]{:S(2)}) collective-permute-start(f32[32,8,1536]{2,1,0:T(8,128)S(1)} %dynamic-slice_bitcast_fusion), channel_id=1, source_target_pairs={{0,32},{32,0},{64,96},{96,64},{128,160},{160,128},{192,224},{224,1... | collective-permute-start | bytes 4718600 | tf_op jit(solution)/shard_map/ppermute | solution.py:320
  49.1 3.6 %fusion.59 = f32[32,37,1536]{2,1,0:T(8,128)S(1)} fusion(bf16[32,37,512]{2,1,0:T(8,128)(2,1)} %copy-done.13, bf16[1536,512,1]{1,0,2:T(8,128)(2,1)S(1)} %bitcast.64), kind=kOutput, calls=%fused_computation.123 | convolution fusion | flops 1862270976 | bytes 10059776 | tf_op jit(solution)/shard_map/ruo,io->rui/dot_general | solution.py:263
  52.7 0.0 slice-start
  52.7 0.2 slice.143
  53.0 0.0 copy-start.4
  53.0 0.6 slice.142
  53.7 1.3 slice-done
  54.9 0.4 slice-done.1
  55.3 5.7 %multiply_reduce_fusion.1 = (f32[32,1024]{1,0:T(8,128)S(1)}, f32[1024]{0:T(1024)S(1)}, f32[32,1024]{1,0:T(8,128)S(1)}, f32[1024]{0:T(1024)S(1)}, f32[32,38,1024]{2,1,0:T(8,128)S(1)}) fusion(f32[1024]{0:T(1024)S(1)} %get-tuple-element.51, f32[32,1024]{1,0:T(8,128)S(1)} %copy-done.4, f32[32,38,1024]{2,1,0:T(8,128)S(1)} %bitcast.66, ...), kind=kLoop, calls=%fused_computation.16 | loop fusion | flops 29816832 | bytes 17932416 | tf_op jit(solution)/shard_map/reduce_sum | solution.py:233
  61.0 0.6 slice_add_fusion.7
  61.6 0.1 fusion.28
  61.8 2.6 %fusion.22 = f32[1024,15]{0,1:T(8,128)} fusion(bf16[32,38,5]{1,2,0:T(8,128)(2,1)S(1)} %copy.82, bf16[32,38,10]{1,2,0:T(8,128)(2,1)S(1)} %copy-done.6, f32[32,38,1024]{2,1,0:T(8,128)S(1)} %get-tuple-element.36, f32[32,1024]{1,0:T(8,128)S(1)} %pad_maximum_fusion.7, f32[32,1024]{1,0:T(8,128)S(1)} %pad_maximum_fusion.6, f32[1024]{0:T(1024)S(1)} %get-tuple-element.51, ...), kind=kOutput, calls=%fused_computation.43 | convolution fusion | flops 51125504 | bytes 10743552 | tf_op jit(solution)/shard_map/ruj,rum->jm/dot_general | solution.py:278
  64.4 0.1 add.242
  64.5 0.1 copy.73
  64.6 0.8 add.240
  65.4 0.7 copy.72
  66.1 6.4 %fusion.26 = f32[1024,15]{0,1:T(8,128)S(1)} fusion(f32[1024,15]{0,1:T(8,128)} %fusion.22, bf16[32,38,5]{1,2,0:T(8,128)(2,1)S(1)} %copy.82, bf16[32,38,10]{1,2,0:T(8,128)(2,1)} %copy-done.5, f32[32,38,1024]{2,1,0:T(8,128)} %copy-done.2, f32[32,1024]{1,0:T(8,128)} %copy-done.8, f32[32,1024]{1,0:T(8,128)} %copy-done.7, f32[1024]{0:T(1024)S(1)} %get-tuple-element.51, ...), kind=kOutput, calls=%fused_computation.45 | convolution fusion | flops 54876416 | bytes 10804992 | tf_op jit(solution)/shard_map/ruj,rum->jm/dot_general | solution.py:280
  72.5 1.2 concatenate.56
  73.8 1.1 copy.71
  75.0 0.8 copy.75
  75.7 1.9 %collective-permute-start.1 = (f32[32,8,12]{2,1,0:T(8,128)}, f32[32,8,12]{2,1,0:T(8,128)}, u32[]{:S(2)}, u32[]{:S(2)}) collective-permute-start(f32[32,8,12]{2,1,0:T(8,128)} %bitcast.16), channel_id=1, source_target_pairs={{0,32},{32,0},{64,96},{96,64},{128,160},{160,128},{192,224},{224,1... | collective-permute-start | bytes 36872 | tf_op jit(solution)/shard_map/ppermute | solution.py:320
  77.6 2.7 %copy.77 = bf16[32,37,512]{2,0,1:T(8,128)(2,1)} copy(bf16[32,37,512]{2,1,0:T(8,128)(2,1)} %get-tuple-element.40) | data formatting | bytes 2424832
  80.4 0.1 copy.74
  80.5 1.6 %subtract_convert_fusion.6 = (bf16[32,8,12]{2,1,0:T(8,128)(2,1)S(1)}, bf16[32,8,12]{2,1,0:T(8,128)(2,1)}) fusion(f32[32,8,12]{2,1,0:T(8,128)} %collective-permute-done.1, f32[32,1,8,12]{3,2,0,1:T(8,128)S(1)} %copy.74), kind=kLoop, calls=%fused_computation.52 | loop fusion | flops 15360 | bytes 36864 | tf_op jit(solution)/shard_map/convert_element_type | solution.py:325
  82.1 2.1 %fusion.18 = bf16[32,8,1536]{2,1,0:T(8,128)(2,1)S(1)} fusion(f32[32,8,1536]{2,1,0:T(8,128)} %collective-permute-done, f32[32,2,8,1536]{3,2,1,0:T(8,128)} %bitcast.70, s32[]{:T(128)S(6)} %select_n.94), kind=kLoop, calls=%fused_computation.38 | loop fusion | flops 786432 | bytes 3932164 | tf_op jit(solution)/shard_map/convert_element_type | solution.py:322
  84.1 1.8 %concatenate.58.refs_0_ = bf16[32,8,1560]{2,1,0:T(8,128)(2,1)} concatenate(bf16[32,8,1536]{2,1,0:T(8,128)(2,1)S(1)} %fusion.18, bf16[32,8,12]{2,1,0:T(8,128)(2,1)} %get-tuple-element.42, bf16[32,8,12]{2,1,0:T(8,128)(2,1)S(1)} %get-tuple-element.41), dimensions={2} | concatenate | bytes 1597440 | tf_op jit(solution)/shard_map/concatenate | solution.py:327
  85.9 25.7 %shard_map.120 = bf16[32,8,1560]{2,1,0:T(8,128)(2,1)} custom-call(bf16[32,8,1560]{2,1,0:T(8,128)(2,1)} %concatenate.58.refs_0_), custom_call_target="tpu_custom_call" | custom-call | tf_op jit(solution)/shard_map/pallas_call | solution.py:81
  111.7 1.3 convert_reduce_fusion
  112.9 0.1 slice_add_fusion.5
  113.0 0.7 reshape.332.src_ref
  113.7 19.7 %shard_map.121 = f32[16,1,1548]{2,1,0:T(1,128)} custom-call(f32[8,1,1548]{2,1,0:T(1,128)} %reshape.332.src_ref), custom_call_target="tpu_custom_call" | custom-call | tf_op jit(solution)/shard_map/pallas_call | solution.py:172
  133.4 0.9 copy.90
  134.3 0.7 slice_reduce_fusion
  135.0 0.7 copy.79
  135.6 0.1 reshape.335
  135.7 0.7 copy.78
  (47 shorter events, 0.3 us)
Async XLA Ops:
  0.6 33.0 %copy-start = (bf16[3,512,512]{2,1,0:T(8,128)(2,1)S(1)}, bf16[3,512,512]{2,1,0:T(8,128)(2,1)}, u32[]{:S(2)}) copy-start(bf16[3,512,512]{2,1,0:T(8,128)(2,1)} %param.14) | copy-start | bytes 4718596
  26.8 3.5 %copy-start.5 = (bf16[32,38,10]{1,2,0:T(8,128)(2,1)}, bf16[32,38,10]{1,2,0:T(8,128)(2,1)S(1)}, u32[]{:S(2)}) copy-start(bf16[32,38,10]{1,2,0:T(8,128)(2,1)S(1)} %copy.81) | copy-start | bytes 72964
  26.9 3.5 %copy-start.10 = (f32[512]{0:T(512)S(1)}, f32[512]{0:T(512)}, u32[]{:S(2)}) copy-start(f32[512]{0:T(512)} %param.12) | copy-start | bytes 6148
  26.9 3.5 %copy-start.11 = (f32[512]{0:T(512)S(1)}, f32[512]{0:T(512)}, u32[]{:S(2)}) copy-start(f32[512]{0:T(512)} %param.13) | copy-start | bytes 6148
  28.7 4.2 %copy-start.1 = (f32[32,38,1024]{2,1,0:T(8,128)}, f32[32,38,1024]{2,1,0:T(8,128)S(1)}, u32[]{:S(2)}) copy-start(f32[32,38,1024]{2,1,0:T(8,128)S(1)} %get-tuple-element.50) | copy-start | bytes 14942212
  30.3 3.3 %copy-start.3 = (f32[32,1024]{1,0:T(8,128)}, f32[32,1024]{1,0:T(8,128)S(1)}, u32[]{:S(2)}) copy-start(f32[32,1024]{1,0:T(8,128)S(1)} %pad_maximum_fusion.5) | copy-start | bytes 393220
  30.4 3.3 %copy-start.12 = (bf16[32,37,512]{2,0,1:T(8,128)(2,1)S(1)}, bf16[32,37,512]{2,0,1:T(8,128)(2,1)}, u32[]{:S(2)}) copy-start(bf16[32,37,512]{2,0,1:T(8,128)(2,1)} %param.15) | copy-start | bytes 3637252
  38.9 1.1 copy-start.13
  45.5 36.6 %collective-permute-start = (f32[32,8,1536]{2,1,0:T(8,128)S(1)}, f32[32,8,1536]{2,1,0:T(8,128)}, u32[]{:S(2)}, u32[]{:S(2)}) collective-permute-start(f32[32,8,1536]{2,1,0:T(8,128)S(1)} %dynamic-slice_bitcast_fusion), channel_id=1, source_target_pairs={{0,32},{32,0},{64,96},{96,64},{128,160},{160,128},{192,224},{224,1... | collective-permute-start | bytes 4718600 | tf_op jit(solution)/shard_map/ppermute | solution.py:320
  52.7 2.2 %slice-start = ((s8[5242880]{0:T(1024)(128)(4,1)}), s8[4194304]{0:T(1024)(128)(4,1)S(1)}, s32[]{:S(2)}) async-start(s8[5242880]{0:T(1024)(128)(4,1)} %bitcast.65), calls=%async_computation | async-start | bytes 8388608
  53.0 2.3 %slice-start.1 = ((s8[5242880]{0:T(1024)(128)(4,1)}), s8[1048576]{0:T(1024)(128)(4,1)S(1)}, s32[]{:S(2)}) async-start(s8[5242880]{0:T(1024)(128)(4,1)} %bitcast.65), calls=%async_computation.1 | async-start | bytes 2097152
  53.0 2.3 %copy-start.4 = (f32[32,1024]{1,0:T(8,128)S(1)}, f32[32,1024]{1,0:T(8,128)}, u32[]{:S(2)}) copy-start(f32[32,1024]{1,0:T(8,128)} %copy-done.3) | copy-start | bytes 393220
  55.3 6.5 %copy-start.6 = (bf16[32,38,10]{1,2,0:T(8,128)(2,1)S(1)}, bf16[32,38,10]{1,2,0:T(8,128)(2,1)}, u32[]{:S(2)}) copy-start(bf16[32,38,10]{1,2,0:T(8,128)(2,1)} %copy-done.5) | copy-start | bytes 72964
  61.0 3.4 %copy-start.2 = (f32[32,38,1024]{2,1,0:T(8,128)}, f32[32,38,1024]{2,1,0:T(8,128)S(1)}, u32[]{:S(2)}) copy-start(f32[32,38,1024]{2,1,0:T(8,128)S(1)} %get-tuple-element.36) | copy-start | bytes 14942212
  61.7 2.7 %copy-start.7 = (f32[32,1024]{1,0:T(8,128)}, f32[32,1024]{1,0:T(8,128)S(1)}, u32[]{:S(2)}) copy-start(f32[32,1024]{1,0:T(8,128)S(1)} %pad_maximum_fusion.6) | copy-start | bytes 393220
  61.8 2.6 %copy-start.8 = (f32[32,1024]{1,0:T(8,128)}, f32[32,1024]{1,0:T(8,128)S(1)}, u32[]{:S(2)}) copy-start(f32[32,1024]{1,0:T(8,128)S(1)} %pad_maximum_fusion.7) | copy-start | bytes 393220
  66.1 8.8 %copy-start.9 = (f32[32,2,8,1]{0,2,3,1:T(8,128)S(1)}, f32[32,2,8,1]{0,2,3,1:T(8,128)}, u32[]{:S(2)}) copy-start(f32[32,2,8,1]{0,2,3,1:T(8,128)} %copy.72) | copy-start | bytes 6148
  75.7 4.8 %collective-permute-start.1 = (f32[32,8,12]{2,1,0:T(8,128)}, f32[32,8,12]{2,1,0:T(8,128)}, u32[]{:S(2)}, u32[]{:S(2)}) collective-permute-start(f32[32,8,12]{2,1,0:T(8,128)} %bitcast.16), channel_id=1, source_target_pairs={{0,32},{32,0},{64,96},{96,64},{128,160},{160,128},{192,224},{224,1... | collective-permute-start | bytes 36872 | tf_op jit(solution)/shard_map/ppermute | solution.py:320

commit v12 on v11

--- a/solution.py
+++ b/solution.py
@@ -321,8 +321,9 @@
 
     mine_kernel = pair_sum(grad_kernel).astype(jnp.bfloat16)
     mine_small = pair_sum(small)
-    small_high = mine_small.astype(jnp.bfloat16)
-    small_low = (mine_small - small_high.astype(jnp.float32)).astype(jnp.bfloat16)
+    rounded = lax.reduce_precision(mine_small, exponent_bits=8, mantissa_bits=7)
+    small_high = rounded.astype(jnp.bfloat16)
+    small_low = (mine_small - rounded).astype(jnp.bfloat16)
     (pieces,) = exchange(
         [jnp.concatenate([mine_kernel, small_high, small_low], axis=2)], members, "dev", 1, False, 0
     )

time: 137 us -> 137 us (level)
  no operation moved by 1% of the time
where the time goes in v12:
time: 137 us; the launch traced here: 136 us
  Pallas kernels  64.4 us (47%)
  matrix products  23.6 us (17%)
  local copies, waits for them, and re-layouts  23.5 us (17%)
  other arithmetic  18.2 us (13%)
  starting transfers between devices  5.58 us (4%)
    pallas_call x2, Pallas kernels, exchange(): pl.pallas_call(functools.partial(exchange_kernel, members, axis, stride,...  44.7 us
    pallas_call x1, Pallas kernels, reduce_gather(): pl.pallas_call(functools.partial(reduce_gather_kernel, rows_y), out_shape...  19.7 us
    unnamed x38, local copies, waits for them, and re-layouts  8.19 us
    reduce_sum x2, other arithmetic, fold(): s = jnp.sum(x, axis=1)  7.13 us
    dot_general x1, matrix products, local_pass(): jnp.einsum('ruj,rum->jm', low, patches, preferred_element_type=jnp.float32)  6.44 us
    ppermute x2, starting transfers between devices, pair_sum(): return keep + lax.ppermute(give, 'grp', pairs)  5.58 us
    dot_general x1, matrix products, local_pass(): jnp.einsum('rui,io->ruo', taps, kernel, preferred_element_type=jnp.float32)  5.22 us
    dot_general x1, matrix products, local_pass(): jnp.einsum('ruo,rui->oi', grad1, taps, preferred_element_type=jnp.float32)  3.99 us
  transfers between devices with their start and end apart: 2, of which 0 were waited for; matrix products, arithmetic and copies ran while one was open for 21% of the time, Pallas kernels for 0%

profile of v12, /device:TPU:1, one launch (start us, length us, event | category | flops | bytes accessed | tf_op | source)
XLA Modules:
  0.0 136.4 jit_solution(14751510377647808722)
XLA Ops:
  0.6 0.0 copy-start
  0.7 0.8 fusion.49
  1.5 0.7 compare_and_fusion
  2.2 0.9 dynamic-slice_reduce_fusion
  3.1 1.4 %gather_fusion = bf16[32,384]{1,0:T(8,128)(2,1)S(1)} fusion(bf16[32,384]{1,0:T(8,128)(2,1)} %param.8, s32[1024]{0:T(1024)S(1)} %pad_clamp_fusion), kind=kCustom, calls=%fused_computation | custom fusion | bytes 49280 | tf_op jit(solution)/shard_map/jit(_take)/gather | solution.py:295
  4.5 0.7 broadcast_select_fusion.refs_0_
  5.2 19.0 %shard_map.119 = bf16[32,1,384]{2,1,0:T(2,128)(2,1)} custom-call(bf16[32,1,384]{2,1,0:T(2,128)(2,1)} %broadcast_select_fusion.refs_0_), custom_call_target="tpu_custom_call" | custom-call | tf_op jit(solution)/shard_map/pallas_call | solution.py:81
  24.2 0.9 copy.86
  25.3 0.8 reshape.327
  26.0 0.2 select_reduce_fusion
  26.3 0.1 fusion.45
  26.3 0.2 copy.82
  26.5 0.2 copy.81
  26.8 0.1 broadcast_add_fusion
  26.9 0.0 copy-start.10
  26.9 0.0 copy-start.11
  26.9 1.8 %fusion.5 = (f32[32,1024]{1,0:T(8,128)S(1)}, f32[32,38,1024]{2,1,0:T(8,128)S(1)}) fusion(s32[38,1024]{1,0:T(8,128)S(1)} %broadcast_add_fusion, s32[32]{0:T(128)S(1)} %get-tuple-element.48, bf16[10,512]{1,0:T(8,128)(2,1)} %param.11, bf16[32,38,5]{1,2,0:T(8,128)(2,1)S(1)} %copy.82, bf16[32,38,10]{1,2,0:T(8,128)(2,1)S(1)} %copy.81), kind=kOutput, calls=%fused_computation.12 | convolution fusion | flops 41254144 | bytes 5314304 | tf_op jit(solution)/shard_map/rum,mc->ruc/dot_general | solution.py:223
  28.7 0.1 fusion.33
  28.8 1.4 %multiply_reduce_fusion.2 = f32[32,1024]{1,0:T(8,128)S(1)} fusion(f32[32,38,1024]{2,1,0:T(8,128)S(1)} %get-tuple-element.50, f32[32,1024]{1,0:T(8,128)S(1)} %pad_maximum_fusion.4, s32[38,1024]{1,0:T(8,128)S(1)} %broadcast_add_fusion, s32[32]{0:T(128)S(1)} %get-tuple-element.48), kind=kLoop, calls=%fused_computation.19 | loop fusion | flops 6193152 | bytes 5398656 | tf_op jit(solution)/shard_map/reduce_sum | solution.py:233
  30.2 0.1 fusion.32
  30.3 0.0 copy-start.3
  30.4 0.0 copy-start.12
  30.4 2.5 %fusion.6 = bf16[32,38,1024]{2,1,0:T(8,128)(2,1)S(1)} fusion(f32[1024]{0:T(1024)S(1)} %get-tuple-element.52, f32[1024]{0:T(1024)S(1)} %get-tuple-element.51, s32[38,1024]{1,0:T(8,128)S(1)} %broadcast_add_fusion, s32[32]{0:T(128)S(1)} %get-tuple-element.48, f32[32,1024]{1,0:T(8,128)S(1)} %pad_maximum_fusion.5, f32[32,38,1024]{2,1,0:T(8,128)S(1)} %get-tuple-element.50, ...), kind=kLoop, calls=%fused_computation.13 | loop fusion | flops 14942208 | bytes 7897216 | tf_op jit(solution)/shard_map/convert_element_type | solution.py:248
  32.9 0.7 slice.141
  33.6 5.2 %fusion.14 = (bf16[32,37,512]{2,1,0:T(8,128)(2,1)S(1)}, bf16[32,37,512]{2,1,0:T(8,128)(2,1)}) fusion(bf16[32,37,512]{2,0,1:T(8,128)(2,1)S(1)} %copy-done.12, f32[32,37]{1,0:T(8,128)S(1)} %fusion.45, bf16[1536,512,1]{1,0,2:T(8,128)(2,1)S(1)} %bitcast.61, bf16[32,37,512]{2,1,0:T(8,128)(2,1)S(1)} %slice.141, bf16[32,37,1024]{2,1,0:T(8,128)(2,1)S(1)} %bitcast.65), kind=kOutput, calls=%fused_computation.30 | convolution fusion | flops 1878638592 | bytes 8852096 | tf_op jit(solution)/shard_map/rui,io->ruo/dot_general | solution.py:251
  38.9 1.1 copy-done.13
  40.0 4.0 %fusion.16 = f32[512,1536,1]{1,0,2:T(8,128)} fusion(bf16[32,37,512]{2,1,0:T(8,128)(2,1)S(1)} %get-tuple-element.39, bf16[32,37,512]{2,1,0:T(8,128)(2,1)S(1)} %slice.141, bf16[32,37,1024]{2,1,0:T(8,128)(2,1)S(1)} %bitcast.66), kind=kOutput, calls=%fused_computation.34 | convolution fusion | flops 1869545472 | bytes 7995392 | tf_op jit(solution)/shard_map/ruo,rui->oi/dot_general | solution.py:261
  43.9 1.5 %dynamic-slice_bitcast_fusion = f32[32,8,1536]{2,1,0:T(8,128)S(1)} fusion(f32[32,2,8,1536]{3,2,1,0:T(8,128)} %bitcast.67, s32[]{:T(128)S(6)} %select_n.95), kind=kLoop, calls=%fused_computation.39 | loop fusion | bytes 3145732 | tf_op jit(solution)/shard_map/jit(dynamic_index_in_dim)/squeeze | solution.py:319
  45.5 3.7 %collective-permute-start = (f32[32,8,1536]{2,1,0:T(8,128)S(1)}, f32[32,8,1536]{2,1,0:T(8,128)}, u32[]{:S(2)}, u32[]{:S(2)}) collective-permute-start(f32[32,8,1536]{2,1,0:T(8,128)S(1)} %dynamic-slice_bitcast_fusion), channel_id=1, source_target_pairs={{0,32},{32,0},{64,96},{96,64},{128,160},{160,128},{192,224},{224,1... | collective-permute-start | bytes 4718600 | tf_op jit(solution)/shard_map/ppermute | solution.py:320
  49.1 3.6 %fusion.59 = f32[32,37,1536]{2,1,0:T(8,128)S(1)} fusion(bf16[32,37,512]{2,1,0:T(8,128)(2,1)} %copy-done.13, bf16[1536,512,1]{1,0,2:T(8,128)(2,1)S(1)} %bitcast.62), kind=kOutput, calls=%fused_computation.124 | convolution fusion | flops 1862270976 | bytes 10059776 | tf_op jit(solution)/shard_map/ruo,io->rui/dot_general | solution.py:263
  52.7 0.0 slice-start
  52.7 0.2 slice.143
  53.0 0.0 copy-start.4
  53.0 0.6 slice.142
  53.7 1.3 slice-done
  54.9 0.4 slice-done.1
  55.3 5.7 %multiply_reduce_fusion.1 = (f32[32,1024]{1,0:T(8,128)S(1)}, f32[1024]{0:T(1024)S(1)}, f32[32,1024]{1,0:T(8,128)S(1)}, f32[1024]{0:T(1024)S(1)}, f32[32,38,1024]{2,1,0:T(8,128)S(1)}) fusion(f32[1024]{0:T(1024)S(1)} %get-tuple-element.51, f32[32,1024]{1,0:T(8,128)S(1)} %copy-done.4, f32[32,38,1024]{2,1,0:T(8,128)S(1)} %bitcast.64, ...), kind=kLoop, calls=%fused_computation.16 | loop fusion | flops 29816832 | bytes 17932416 | tf_op jit(solution)/shard_map/reduce_sum | solution.py:233
  61.0 0.6 slice_add_fusion.7
  61.6 0.1 fusion.29
  61.8 2.6 %fusion.22 = f32[1024,15]{0,1:T(8,128)} fusion(bf16[32,38,5]{1,2,0:T(8,128)(2,1)S(1)} %copy.82, bf16[32,38,10]{1,2,0:T(8,128)(2,1)S(1)} %copy-done.6, f32[32,38,1024]{2,1,0:T(8,128)S(1)} %get-tuple-element.36, f32[32,1024]{1,0:T(8,128)S(1)} %pad_maximum_fusion.7, f32[32,1024]{1,0:T(8,128)S(1)} %pad_maximum_fusion.6, f32[1024]{0:T(1024)S(1)} %get-tuple-element.51, ...), kind=kOutput, calls=%fused_computation.43 | convolution fusion | flops 51125504 | bytes 10743552 | tf_op jit(solution)/shard_map/ruj,rum->jm/dot_general | solution.py:278
  64.4 0.1 add.242
  64.5 0.1 copy.73
  64.6 0.8 add.240
  65.4 0.7 copy.72
  66.1 6.4 %fusion.26 = f32[1024,15]{0,1:T(8,128)S(1)} fusion(f32[1024,15]{0,1:T(8,128)} %fusion.22, bf16[32,38,5]{1,2,0:T(8,128)(2,1)S(1)} %copy.82, bf16[32,38,10]{1,2,0:T(8,128)(2,1)} %copy-done.5, f32[32,38,1024]{2,1,0:T(8,128)} %copy-done.2, f32[32,1024]{1,0:T(8,128)} %copy-done.8, f32[32,1024]{1,0:T(8,128)} %copy-done.7, f32[1024]{0:T(1024)S(1)} %get-tuple-element.51, ...), kind=kOutput, calls=%fused_computation.45 | convolution fusion | flops 54876416 | bytes 10804992 | tf_op jit(solution)/shard_map/ruj,rum->jm/dot_general | solution.py:280
  72.5 1.2 concatenate.56
  73.8 1.1 copy.71
  75.0 0.8 copy.75
  75.7 1.9 %collective-permute-start.1 = (f32[32,8,12]{2,1,0:T(8,128)}, f32[32,8,12]{2,1,0:T(8,128)}, u32[]{:S(2)}, u32[]{:S(2)}) collective-permute-start(f32[32,8,12]{2,1,0:T(8,128)} %bitcast.16), channel_id=1, source_target_pairs={{0,32},{32,0},{64,96},{96,64},{128,160},{160,128},{192,224},{224,1... | collective-permute-start | bytes 36872 | tf_op jit(solution)/shard_map/ppermute | solution.py:320
  77.6 2.7 %copy.77 = bf16[32,37,512]{2,0,1:T(8,128)(2,1)} copy(bf16[32,37,512]{2,1,0:T(8,128)(2,1)} %get-tuple-element.40) | data formatting | bytes 2424832
  80.4 0.1 copy.74
  80.5 1.6 %fusion.27 = (bf16[32,8,12]{2,1,0:T(8,128)(2,1)S(1)}, bf16[32,8,12]{2,1,0:T(8,128)(2,1)}) fusion(f32[32,8,12]{2,1,0:T(8,128)} %collective-permute-done.1, f32[32,1,8,12]{3,2,0,1:T(8,128)S(1)} %copy.74), kind=kLoop, calls=%fused_computation.48 | loop fusion | flops 15360 | bytes 36864 | tf_op jit(solution)/shard_map/convert_element_type | solution.py:326
  82.1 2.1 %fusion.18 = bf16[32,8,1536]{2,1,0:T(8,128)(2,1)S(1)} fusion(f32[32,8,1536]{2,1,0:T(8,128)} %collective-permute-done, f32[32,2,8,1536]{3,2,1,0:T(8,128)} %bitcast.68, s32[]{:T(128)S(6)} %select_n.94), kind=kLoop, calls=%fused_computation.38 | loop fusion | flops 786432 | bytes 3932164 | tf_op jit(solution)/shard_map/convert_element_type | solution.py:322
  84.1 1.8 %concatenate.58.refs_0_ = bf16[32,8,1560]{2,1,0:T(8,128)(2,1)} concatenate(bf16[32,8,1536]{2,1,0:T(8,128)(2,1)S(1)} %fusion.18, bf16[32,8,12]{2,1,0:T(8,128)(2,1)} %get-tuple-element.42, bf16[32,8,12]{2,1,0:T(8,128)(2,1)S(1)} %get-tuple-element.41), dimensions={2} | concatenate | bytes 1597440 | tf_op jit(solution)/shard_map/concatenate | solution.py:328
  85.9 25.7 %shard_map.120 = bf16[32,8,1560]{2,1,0:T(8,128)(2,1)} custom-call(bf16[32,8,1560]{2,1,0:T(8,128)(2,1)} %concatenate.58.refs_0_), custom_call_target="tpu_custom_call" | custom-call | tf_op jit(solution)/shard_map/pallas_call | solution.py:81
  111.7 1.3 convert_reduce_fusion
  112.9 0.1 slice_add_fusion.5
  113.0 0.7 reshape.332.src_ref
  113.7 19.7 %shard_map.121 = f32[16,1,1548]{2,1,0:T(1,128)} custom-call(f32[8,1,1548]{2,1,0:T(1,128)} %reshape.332.src_ref), custom_call_target="tpu_custom_call" | custom-call | tf_op jit(solution)/shard_map/pallas_call | solution.py:172
  133.4 0.9 copy.90
  134.3 0.7 slice_reduce_fusion
  135.0 0.7 copy.79
  135.7 0.1 reshape.335
  135.7 0.7 copy.78
  (47 shorter events, 0.3 us)
Async XLA Ops:
  0.6 33.0 %copy-start = (bf16[3,512,512]{2,1,0:T(8,128)(2,1)S(1)}, bf16[3,512,512]{2,1,0:T(8,128)(2,1)}, u32[]{:S(2)}) copy-start(bf16[3,512,512]{2,1,0:T(8,128)(2,1)} %param.14) | copy-start | bytes 4718596
  26.8 3.5 %copy-start.5 = (bf16[32,38,10]{1,2,0:T(8,128)(2,1)}, bf16[32,38,10]{1,2,0:T(8,128)(2,1)S(1)}, u32[]{:S(2)}) copy-start(bf16[32,38,10]{1,2,0:T(8,128)(2,1)S(1)} %copy.81) | copy-start | bytes 72964
  26.9 3.5 %copy-start.10 = (f32[512]{0:T(512)S(1)}, f32[512]{0:T(512)}, u32[]{:S(2)}) copy-start(f32[512]{0:T(512)} %param.12) | copy-start | bytes 6148
  26.9 3.5 %copy-start.11 = (f32[512]{0:T(512)S(1)}, f32[512]{0:T(512)}, u32[]{:S(2)}) copy-start(f32[512]{0:T(512)} %param.13) | copy-start | bytes 6148
  28.7 4.2 %copy-start.1 = (f32[32,38,1024]{2,1,0:T(8,128)}, f32[32,38,1024]{2,1,0:T(8,128)S(1)}, u32[]{:S(2)}) copy-start(f32[32,38,1024]{2,1,0:T(8,128)S(1)} %get-tuple-element.50) | copy-start | bytes 14942212
  30.3 3.3 %copy-start.3 = (f32[32,1024]{1,0:T(8,128)}, f32[32,1024]{1,0:T(8,128)S(1)}, u32[]{:S(2)}) copy-start(f32[32,1024]{1,0:T(8,128)S(1)} %pad_maximum_fusion.5) | copy-start | bytes 393220
  30.4 3.3 %copy-start.12 = (bf16[32,37,512]{2,0,1:T(8,128)(2,1)S(1)}, bf16[32,37,512]{2,0,1:T(8,128)(2,1)}, u32[]{:S(2)}) copy-start(bf16[32,37,512]{2,0,1:T(8,128)(2,1)} %param.15) | copy-start | bytes 3637252
  38.9 1.1 copy-start.13
  45.5 36.6 %collective-permute-start = (f32[32,8,1536]{2,1,0:T(8,128)S(1)}, f32[32,8,1536]{2,1,0:T(8,128)}, u32[]{:S(2)}, u32[]{:S(2)}) collective-permute-start(f32[32,8,1536]{2,1,0:T(8,128)S(1)} %dynamic-slice_bitcast_fusion), channel_id=1, source_target_pairs={{0,32},{32,0},{64,96},{96,64},{128,160},{160,128},{192,224},{224,1... | collective-permute-start | bytes 4718600 | tf_op jit(solution)/shard_map/ppermute | solution.py:320
  52.7 2.2 %slice-start = ((s8[5242880]{0:T(1024)(128)(4,1)}), s8[4194304]{0:T(1024)(128)(4,1)S(1)}, s32[]{:S(2)}) async-start(s8[5242880]{0:T(1024)(128)(4,1)} %bitcast.63), calls=%async_computation | async-start | bytes 8388608
  53.0 2.3 %slice-start.1 = ((s8[5242880]{0:T(1024)(128)(4,1)}), s8[1048576]{0:T(1024)(128)(4,1)S(1)}, s32[]{:S(2)}) async-start(s8[5242880]{0:T(1024)(128)(4,1)} %bitcast.63), calls=%async_computation.1 | async-start | bytes 2097152
  53.0 2.3 %copy-start.4 = (f32[32,1024]{1,0:T(8,128)S(1)}, f32[32,1024]{1,0:T(8,128)}, u32[]{:S(2)}) copy-start(f32[32,1024]{1,0:T(8,128)} %copy-done.3) | copy-start | bytes 393220
  55.3 6.5 %copy-start.6 = (bf16[32,38,10]{1,2,0:T(8,128)(2,1)S(1)}, bf16[32,38,10]{1,2,0:T(8,128)(2,1)}, u32[]{:S(2)}) copy-start(bf16[32,38,10]{1,2,0:T(8,128)(2,1)} %copy-done.5) | copy-start | bytes 72964
  61.0 3.4 %copy-start.2 = (f32[32,38,1024]{2,1,0:T(8,128)}, f32[32,38,1024]{2,1,0:T(8,128)S(1)}, u32[]{:S(2)}) copy-start(f32[32,38,1024]{2,1,0:T(8,128)S(1)} %get-tuple-element.36) | copy-start | bytes 14942212
  61.7 2.7 %copy-start.7 = (f32[32,1024]{1,0:T(8,128)}, f32[32,1024]{1,0:T(8,128)S(1)}, u32[]{:S(2)}) copy-start(f32[32,1024]{1,0:T(8,128)S(1)} %pad_maximum_fusion.6) | copy-start | bytes 393220
  61.8 2.6 %copy-start.8 = (f32[32,1024]{1,0:T(8,128)}, f32[32,1024]{1,0:T(8,128)S(1)}, u32[]{:S(2)}) copy-start(f32[32,1024]{1,0:T(8,128)S(1)} %pad_maximum_fusion.7) | copy-start | bytes 393220
  66.1 8.8 %copy-start.9 = (f32[32,2,8,1]{0,2,3,1:T(8,128)S(1)}, f32[32,2,8,1]{0,2,3,1:T(8,128)}, u32[]{:S(2)}) copy-start(f32[32,2,8,1]{0,2,3,1:T(8,128)} %copy.72) | copy-start | bytes 6148
  75.7 4.8 %collective-permute-start.1 = (f32[32,8,12]{2,1,0:T(8,128)}, f32[32,8,12]{2,1,0:T(8,128)}, u32[]{:S(2)}, u32[]{:S(2)}) collective-permute-start(f32[32,8,12]{2,1,0:T(8,128)} %bitcast.16), channel_id=1, source_target_pairs={{0,32},{32,0},{64,96},{96,64},{128,160},{160,128},{192,224},{224,1... | collective-permute-start | bytes 36872 | tf_op jit(solution)/shard_map/ppermute | solution.py:320

commit v13 on v12

--- a/solution.py
+++ b/solution.py
@@ -292,7 +292,8 @@
     share = rows // members
     own_order = lax.dynamic_index_in_dim(order, member, 0, keepdims=False)
     dealt = own_order.reshape(share, members).T.reshape(rows)
-    outgoing = jnp.take(wave, dealt, axis=0)
+    chooser = (dealt[:, None] == jnp.arange(rows, dtype=jnp.int32)[None, :]).astype(wave.dtype)
+    outgoing = jnp.dot(chooser, wave, preferred_element_type=jnp.float32).astype(wave.dtype)
     (arrived,) = exchange([outgoing.reshape(members, share, -1)], members, "dev", 1, False, 3)
     arrived = arrived.reshape(rows, -1)
     picks = lax.dynamic_index_in_dim(

time: 137 us -> 135 us (0.985)
  other arithmetic: 18.2 us -> 15.3 us
    select_n x2 -> x0, other arithmetic: 1.56 us -> none  [shards(): outgoing = jnp.take(wave, dealt, axis=0)]
    gather x1 -> x0, local copies, waits for them, and re-layouts: 1.37 us -> none  [shards(): outgoing = jnp.take(wave, dealt, axis=0)]
where the time goes in v13:
time: 135 us; the launch traced here: 134 us
  Pallas kernels  64.4 us (48%)
  matrix products  24.6 us (18%)
  local copies, waits for them, and re-layouts  22.9 us (17%)
  other arithmetic  15.3 us (11%)
  starting transfers between devices  5.57 us (4%)
    pallas_call x2, Pallas kernels, exchange(): pl.pallas_call(functools.partial(exchange_kernel, members, axis, stride,...  44.8 us
    pallas_call x1, Pallas kernels, reduce_gather(): pl.pallas_call(functools.partial(reduce_gather_kernel, rows_y), out_shape...  19.6 us
    unnamed x38, local copies, waits for them, and re-layouts  8.19 us
    reduce_sum x2, other arithmetic, fold(): s = jnp.sum(x, axis=1)  7.13 us
    dot_general x1, matrix products, local_pass(): jnp.einsum('ruj,rum->jm', low, patches, preferred_element_type=jnp.float32)  6.44 us
    ppermute x2, starting transfers between devices, pair_sum(): return keep + lax.ppermute(give, 'grp', pairs)  5.57 us
    dot_general x1, matrix products, local_pass(): jnp.einsum('rui,io->ruo', taps, kernel, preferred_element_type=jnp.float32)  5.23 us
    dot_general x1, matrix products, local_pass(): jnp.einsum('ruo,rui->oi', grad1, taps, preferred_element_type=jnp.float32)  3.99 us
  transfers between devices with their start and end apart: 2, of which 0 were waited for; matrix products, arithmetic and copies ran while one was open for 21% of the time, Pallas kernels for 0%

profile of v13, /device:TPU:1, one launch (start us, length us, event | category | flops | bytes accessed | tf_op | source)
XLA Modules:
  0.0 133.8 jit_solution(11249035244991980969)
XLA Ops:
  0.6 0.0 copy-start
  0.7 0.8 fusion.51
  1.5 0.9 dynamic-slice_reduce_fusion
  2.4 0.9 fusion.27
  3.3 0.7 copy.64.refs_0_
  4.0 19.0 %shard_map.119 = bf16[32,1,384]{2,1,0:T(2,128)(2,1)} custom-call(bf16[32,1,384]{2,1,0:T(2,128)(2,1)} %copy.64.refs_0_), custom_call_target="tpu_custom_call" | custom-call | tf_op jit(solution)/shard_map/pallas_call | solution.py:81
  23.0 0.9 copy.86
  24.0 0.8 reshape.274
  24.8 0.2 select_reduce_fusion
  25.0 0.1 fusion.46
  25.1 0.2 copy.82
  25.3 0.2 copy.81
  25.5 0.1 broadcast_add_fusion
  25.6 0.0 copy-start.10
  25.6 0.0 copy-start.11
  25.6 1.8 %fusion.5 = (f32[32,1024]{1,0:T(8,128)S(1)}, f32[32,38,1024]{2,1,0:T(8,128)S(1)}) fusion(s32[38,1024]{1,0:T(8,128)S(1)} %broadcast_add_fusion, s32[32]{0:T(128)S(1)} %get-tuple-element.48, bf16[10,512]{1,0:T(8,128)(2,1)} %param.11, bf16[32,38,5]{1,2,0:T(8,128)(2,1)S(1)} %copy.82, bf16[32,38,10]{1,2,0:T(8,128)(2,1)S(1)} %copy.81), kind=kOutput, calls=%fused_computation.11 | convolution fusion | flops 41254144 | bytes 5314304 | tf_op jit(solution)/shard_map/rum,mc->ruc/dot_general | solution.py:223
  27.5 0.1 fusion.34
  27.6 1.4 %multiply_reduce_fusion.2 = f32[32,1024]{1,0:T(8,128)S(1)} fusion(f32[32,38,1024]{2,1,0:T(8,128)S(1)} %get-tuple-element.50, f32[32,1024]{1,0:T(8,128)S(1)} %pad_maximum_fusion.4, s32[38,1024]{1,0:T(8,128)S(1)} %broadcast_add_fusion, s32[32]{0:T(128)S(1)} %get-tuple-element.48), kind=kLoop, calls=%fused_computation.18 | loop fusion | flops 6193152 | bytes 5398656 | tf_op jit(solution)/shard_map/reduce_sum | solution.py:233
  29.0 0.1 fusion.33
  29.1 0.0 copy-start.3
  29.1 0.0 copy-start.12
  29.2 2.5 %fusion.6 = bf16[32,38,1024]{2,1,0:T(8,128)(2,1)S(1)} fusion(f32[1024]{0:T(1024)S(1)} %get-tuple-element.52, f32[1024]{0:T(1024)S(1)} %get-tuple-element.51, s32[38,1024]{1,0:T(8,128)S(1)} %broadcast_add_fusion, s32[32]{0:T(128)S(1)} %get-tuple-element.48, f32[32,1024]{1,0:T(8,128)S(1)} %pad_maximum_fusion.5, f32[32,38,1024]{2,1,0:T(8,128)S(1)} %get-tuple-element.50, ...), kind=kLoop, calls=%fused_computation.12 | loop fusion | flops 14942208 | bytes 7897216 | tf_op jit(solution)/shard_map/convert_element_type | solution.py:248
  31.7 0.7 slice.139
  32.4 5.2 %fusion.14 = (bf16[32,37,512]{2,1,0:T(8,128)(2,1)S(1)}, bf16[32,37,512]{2,1,0:T(8,128)(2,1)}) fusion(bf16[32,37,512]{2,0,1:T(8,128)(2,1)S(1)} %copy-done.12, f32[32,37]{1,0:T(8,128)S(1)} %fusion.46, bf16[1536,512,1]{1,0,2:T(8,128)(2,1)S(1)} %bitcast.59, bf16[32,37,512]{2,1,0:T(8,128)(2,1)S(1)} %slice.139, bf16[32,37,1024]{2,1,0:T(8,128)(2,1)S(1)} %bitcast.63), kind=kOutput, calls=%fused_computation.29 | convolution fusion | flops 1878638592 | bytes 8852096 | tf_op jit(solution)/shard_map/rui,io->ruo/dot_general | solution.py:251
  37.6 1.1 copy-done.13
  38.7 4.0 %fusion.16 = f32[512,1536,1]{1,0,2:T(8,128)} fusion(bf16[32,37,512]{2,1,0:T(8,128)(2,1)S(1)} %get-tuple-element.39, bf16[32,37,512]{2,1,0:T(8,128)(2,1)S(1)} %slice.139, bf16[32,37,1024]{2,1,0:T(8,128)(2,1)S(1)} %bitcast.64), kind=kOutput, calls=%fused_computation.33 | convolution fusion | flops 1869545472 | bytes 7995392 | tf_op jit(solution)/shard_map/ruo,rui->oi/dot_general | solution.py:261
  42.7 1.5 %dynamic-slice_bitcast_fusion = f32[32,8,1536]{2,1,0:T(8,128)S(1)} fusion(f32[32,2,8,1536]{3,2,1,0:T(8,128)} %bitcast.65, s32[]{:T(128)S(6)} %select_n.66), kind=kLoop, calls=%fused_computation.38 | loop fusion | bytes 3145732 | tf_op jit(solution)/shard_map/jit(dynamic_index_in_dim)/squeeze | solution.py:320
  44.2 3.7 %collective-permute-start = (f32[32,8,1536]{2,1,0:T(8,128)S(1)}, f32[32,8,1536]{2,1,0:T(8,128)}, u32[]{:S(2)}, u32[]{:S(2)}) collective-permute-start(f32[32,8,1536]{2,1,0:T(8,128)S(1)} %dynamic-slice_bitcast_fusion), channel_id=1, source_target_pairs={{0,32},{32,0},{64,96},{96,64},{128,160},{160,128},{192,224},{224,1... | collective-permute-start | bytes 4718600 | tf_op jit(solution)/shard_map/ppermute | solution.py:321
  47.9 3.6 %fusion.61 = f32[32,37,1536]{2,1,0:T(8,128)S(1)} fusion(bf16[32,37,512]{2,1,0:T(8,128)(2,1)} %copy-done.13, bf16[1536,512,1]{1,0,2:T(8,128)(2,1)S(1)} %bitcast.60), kind=kOutput, calls=%fused_computation.122 | convolution fusion | flops 1862270976 | bytes 10059776 | tf_op jit(solution)/shard_map/ruo,io->rui/dot_general | solution.py:263
  51.5 0.0 slice-start
  51.5 0.2 slice.141
  51.8 0.0 slice-start.1
  51.8 0.0 copy-start.4
  51.8 0.6 slice.140
  52.4 1.3 slice-done
  53.7 0.4 slice-done.1
  54.0 5.7 %multiply_reduce_fusion.1 = (f32[32,1024]{1,0:T(8,128)S(1)}, f32[1024]{0:T(1024)S(1)}, f32[32,1024]{1,0:T(8,128)S(1)}, f32[1024]{0:T(1024)S(1)}, f32[32,38,1024]{2,1,0:T(8,128)S(1)}) fusion(f32[1024]{0:T(1024)S(1)} %get-tuple-element.51, f32[32,1024]{1,0:T(8,128)S(1)} %copy-done.4, f32[32,38,1024]{2,1,0:T(8,128)S(1)} %bitcast.62, ...), kind=kLoop, calls=%fused_computation.15 | loop fusion | flops 29816832 | bytes 17932416 | tf_op jit(solution)/shard_map/reduce_sum | solution.py:233
  59.8 0.6 slice_add_fusion.7
  60.4 0.1 fusion.30
  60.6 2.6 %fusion.22 = f32[1024,15]{0,1:T(8,128)} fusion(bf16[32,38,5]{1,2,0:T(8,128)(2,1)S(1)} %copy.82, bf16[32,38,10]{1,2,0:T(8,128)(2,1)S(1)} %copy-done.6, f32[32,38,1024]{2,1,0:T(8,128)S(1)} %get-tuple-element.36, f32[32,1024]{1,0:T(8,128)S(1)} %pad_maximum_fusion.7, f32[32,1024]{1,0:T(8,128)S(1)} %pad_maximum_fusion.6, f32[1024]{0:T(1024)S(1)} %get-tuple-element.51, ...), kind=kOutput, calls=%fused_computation.42 | convolution fusion | flops 51125504 | bytes 10743552 | tf_op jit(solution)/shard_map/ruj,rum->jm/dot_general | solution.py:278
  63.2 0.1 add.217
  63.3 0.1 copy.73
  63.4 0.8 add.215
  64.2 0.7 copy.72
  64.9 6.4 %fusion.26 = f32[1024,15]{0,1:T(8,128)S(1)} fusion(f32[1024,15]{0,1:T(8,128)} %fusion.22, bf16[32,38,5]{1,2,0:T(8,128)(2,1)S(1)} %copy.82, bf16[32,38,10]{1,2,0:T(8,128)(2,1)} %copy-done.5, f32[32,38,1024]{2,1,0:T(8,128)} %copy-done.2, f32[32,1024]{1,0:T(8,128)} %copy-done.8, f32[32,1024]{1,0:T(8,128)} %copy-done.7, f32[1024]{0:T(1024)S(1)} %get-tuple-element.51, ...), kind=kOutput, calls=%fused_computation.44 | convolution fusion | flops 54876416 | bytes 10804992 | tf_op jit(solution)/shard_map/ruj,rum->jm/dot_general | solution.py:280
  71.3 1.2 concatenate.56
  72.6 1.1 copy.71
  73.7 0.8 copy.75
  74.5 1.9 %collective-permute-start.1 = (f32[32,8,12]{2,1,0:T(8,128)}, f32[32,8,12]{2,1,0:T(8,128)}, u32[]{:S(2)}, u32[]{:S(2)}) collective-permute-start(f32[32,8,12]{2,1,0:T(8,128)} %bitcast.73), channel_id=1, source_target_pairs={{0,32},{32,0},{64,96},{96,64},{128,160},{160,128},{192,224},{224,1... | collective-permute-start | bytes 36872 | tf_op jit(solution)/shard_map/ppermute | solution.py:321
  76.4 2.7 %copy.77 = bf16[32,37,512]{2,0,1:T(8,128)(2,1)} copy(bf16[32,37,512]{2,1,0:T(8,128)(2,1)} %get-tuple-element.40) | data formatting | bytes 2424832
  79.1 0.1 copy.74
  79.3 0.9 fusion.28
  80.2 2.1 %fusion.18 = bf16[32,8,1536]{2,1,0:T(8,128)(2,1)S(1)} fusion(f32[32,8,1536]{2,1,0:T(8,128)} %collective-permute-done, f32[32,2,8,1536]{3,2,1,0:T(8,128)} %bitcast.66, s32[]{:T(128)S(6)} %select_n.65), kind=kLoop, calls=%fused_computation.37 | loop fusion | flops 786432 | bytes 3932164 | tf_op jit(solution)/shard_map/convert_element_type | solution.py:323
  82.3 1.1 concatenate.58.refs_0_
  83.4 25.7 %shard_map.120 = bf16[32,8,1560]{2,1,0:T(8,128)(2,1)} custom-call(bf16[32,8,1560]{2,1,0:T(8,128)(2,1)} %concatenate.58.refs_0_), custom_call_target="tpu_custom_call" | custom-call | tf_op jit(solution)/shard_map/pallas_call | solution.py:81
  109.1 1.3 convert_reduce_fusion
  110.4 0.1 slice_add_fusion.5
  110.5 0.7 reshape.280.src_ref
  111.2 19.6 %shard_map.121 = f32[16,1,1548]{2,1,0:T(1,128)} custom-call(f32[8,1,1548]{2,1,0:T(1,128)} %reshape.280.src_ref), custom_call_target="tpu_custom_call" | custom-call | tf_op jit(solution)/shard_map/pallas_call | solution.py:172
  130.8 0.9 copy.89
  131.7 0.7 slice_reduce_fusion
  132.4 0.7 copy.79
  133.1 0.1 reshape.283
  133.2 0.7 copy.78
  (45 shorter events, 0.3 us)
Async XLA Ops:
  0.6 31.8 %copy-start = (bf16[3,512,512]{2,1,0:T(8,128)(2,1)S(1)}, bf16[3,512,512]{2,1,0:T(8,128)(2,1)}, u32[]{:S(2)}) copy-start(bf16[3,512,512]{2,1,0:T(8,128)(2,1)} %param.14) | copy-start | bytes 4718596
  25.5 3.5 %copy-start.5 = (bf16[32,38,10]{1,2,0:T(8,128)(2,1)}, bf16[32,38,10]{1,2,0:T(8,128)(2,1)S(1)}, u32[]{:S(2)}) copy-start(bf16[32,38,10]{1,2,0:T(8,128)(2,1)S(1)} %copy.81) | copy-start | bytes 72964
  25.6 3.5 %copy-start.10 = (f32[512]{0:T(512)S(1)}, f32[512]{0:T(512)}, u32[]{:S(2)}) copy-start(f32[512]{0:T(512)} %param.12) | copy-start | bytes 6148
  25.6 3.5 %copy-start.11 = (f32[512]{0:T(512)S(1)}, f32[512]{0:T(512)}, u32[]{:S(2)}) copy-start(f32[512]{0:T(512)} %param.13) | copy-start | bytes 6148
  27.4 4.2 %copy-start.1 = (f32[32,38,1024]{2,1,0:T(8,128)}, f32[32,38,1024]{2,1,0:T(8,128)S(1)}, u32[]{:S(2)}) copy-start(f32[32,38,1024]{2,1,0:T(8,128)S(1)} %get-tuple-element.50) | copy-start | bytes 14942212
  29.1 3.3 %copy-start.3 = (f32[32,1024]{1,0:T(8,128)}, f32[32,1024]{1,0:T(8,128)S(1)}, u32[]{:S(2)}) copy-start(f32[32,1024]{1,0:T(8,128)S(1)} %pad_maximum_fusion.5) | copy-start | bytes 393220
  29.1 3.3 %copy-start.12 = (bf16[32,37,512]{2,0,1:T(8,128)(2,1)S(1)}, bf16[32,37,512]{2,0,1:T(8,128)(2,1)}, u32[]{:S(2)}) copy-start(bf16[32,37,512]{2,0,1:T(8,128)(2,1)} %param.15) | copy-start | bytes 3637252
  37.6 1.1 copy-start.13
  44.2 36.0 %collective-permute-start = (f32[32,8,1536]{2,1,0:T(8,128)S(1)}, f32[32,8,1536]{2,1,0:T(8,128)}, u32[]{:S(2)}, u32[]{:S(2)}) collective-permute-start(f32[32,8,1536]{2,1,0:T(8,128)S(1)} %dynamic-slice_bitcast_fusion), channel_id=1, source_target_pairs={{0,32},{32,0},{64,96},{96,64},{128,160},{160,128},{192,224},{224,1... | collective-permute-start | bytes 4718600 | tf_op jit(solution)/shard_map/ppermute | solution.py:321
  51.5 2.2 %slice-start = ((s8[5242880]{0:T(1024)(128)(4,1)}), s8[4194304]{0:T(1024)(128)(4,1)S(1)}, s32[]{:S(2)}) async-start(s8[5242880]{0:T(1024)(128)(4,1)} %bitcast.61), calls=%async_computation | async-start | bytes 8388608
  51.8 2.3 %slice-start.1 = ((s8[5242880]{0:T(1024)(128)(4,1)}), s8[1048576]{0:T(1024)(128)(4,1)S(1)}, s32[]{:S(2)}) async-start(s8[5242880]{0:T(1024)(128)(4,1)} %bitcast.61), calls=%async_computation.1 | async-start | bytes 2097152
  51.8 2.3 %copy-start.4 = (f32[32,1024]{1,0:T(8,128)S(1)}, f32[32,1024]{1,0:T(8,128)}, u32[]{:S(2)}) copy-start(f32[32,1024]{1,0:T(8,128)} %copy-done.3) | copy-start | bytes 393220
  54.0 6.5 %copy-start.6 = (bf16[32,38,10]{1,2,0:T(8,128)(2,1)S(1)}, bf16[32,38,10]{1,2,0:T(8,128)(2,1)}, u32[]{:S(2)}) copy-start(bf16[32,38,10]{1,2,0:T(8,128)(2,1)} %copy-done.5) | copy-start | bytes 72964
  59.8 3.4 %copy-start.2 = (f32[32,38,1024]{2,1,0:T(8,128)}, f32[32,38,1024]{2,1,0:T(8,128)S(1)}, u32[]{:S(2)}) copy-start(f32[32,38,1024]{2,1,0:T(8,128)S(1)} %get-tuple-element.36) | copy-start | bytes 14942212
  60.5 2.7 %copy-start.7 = (f32[32,1024]{1,0:T(8,128)}, f32[32,1024]{1,0:T(8,128)S(1)}, u32[]{:S(2)}) copy-start(f32[32,1024]{1,0:T(8,128)S(1)} %pad_maximum_fusion.6) | copy-start | bytes 393220
  60.5 2.6 %copy-start.8 = (f32[32,1024]{1,0:T(8,128)}, f32[32,1024]{1,0:T(8,128)S(1)}, u32[]{:S(2)}) copy-start(f32[32,1024]{1,0:T(8,128)S(1)} %pad_maximum_fusion.7) | copy-start | bytes 393220
  64.9 8.8 %copy-start.9 = (f32[32,2,8,1]{0,2,3,1:T(8,128)S(1)}, f32[32,2,8,1]{0,2,3,1:T(8,128)}, u32[]{:S(2)}) copy-start(f32[32,2,8,1]{0,2,3,1:T(8,128)} %copy.72) | copy-start | bytes 6148
  74.5 4.8 %collective-permute-start.1 = (f32[32,8,12]{2,1,0:T(8,128)}, f32[32,8,12]{2,1,0:T(8,128)}, u32[]{:S(2)}, u32[]{:S(2)}) collective-permute-start(f32[32,8,12]{2,1,0:T(8,128)} %bitcast.73), channel_id=1, source_target_pairs={{0,32},{32,0},{64,96},{96,64},{128,160},{160,128},{192,224},{224,1... | collective-permute-start | bytes 36872 | tf_op jit(solution)/shard_map/ppermute | solution.py:321
